TPU v7x, 32 devices: a whole 2x2x4 slice. The times are simulated.
32 devices in a mesh: dp: 4 (over z), ctx: 4 (over x, core), tp: 2 (over y).
Axes of the slice: x: 2, y: 2, z: 4, core: 2. Of those that a mesh axis runs over, the one named last changes fastest.
Arguments:
- hidden_in: bfloat16 [8, 1536, 1024], P('dp', 'ctx'), may hold values from -6 to 6
- positions: int32 [8, 1536], P('dp', 'ctx'), may hold values from 0 to 2046, as said below
- valid_mask: int32 [8, 1536], P('dp', 'ctx'), may hold values from 0 to 1, as said below
- teacher: bfloat16 [8, 1536, 1024], P('dp', 'ctx'), may hold values from -6 to 6
- cotangent: bfloat16 [8, 1536, 1024], P('dp', 'ctx'), may hold values from -6 to 6
- mixer_gain: float32 [1024], replicated, may hold values from 0.5 to 1.5
- query_weight: bfloat16 [1024, 512], P(('dp', 'ctx'), 'tp'), may hold values from -0.1875 to 0.1875
- keyvalue_projection_weight: bfloat16 [1024, 2, 128], P(('dp', 'ctx'), None, 'tp'), may hold values from -0.1875 to 0.1875
- attnout_weight: bfloat16 [512, 1024], P('tp', ('dp', 'ctx')), may hold values from -3 to 3
- stream_weight: bfloat16 [1024, 2, 1536], P(('dp', 'ctx'), None, 'tp'), may hold values from -0.1875 to 0.1875
- state_weight: bfloat16 [1024, 256], P(('dp', 'ctx')), may hold values from -0.1875 to 0.1875
- step_weight: bfloat16 [1024, 24], P(('dp', 'ctx'), 'tp'), may hold values from -0.1875 to 0.1875
- conv_stream: float32 [4, 1536], P(None, 'tp'), may hold values from -3 to 3
- bias_stream: float32 [1536], P('tp'), may hold values from -3 to 3
- conv_state: float32 [4, 256], replicated, may hold values from -3 to 3
- bias_state: float32 [256], replicated, may hold values from -3 to 3
- step_bias: float32 [24], P('tp'), may hold values from -7 to -4
- decay_log: float32 [24], P('tp'), may hold values from -2 to 1
- skip_scale: float32 [24], P('tp'), may hold values from 0.5 to 1.5
- mambaout_weight: bfloat16 [1536, 1024], P('tp', ('dp', 'ctx')), may hold values from -0.03125 to 0.03125
- ffn_gain: float32 [1024], replicated, may hold values from 0.5 to 1.5
- gateup_weight: bfloat16 [1024, 2, 2048], P(('dp', 'ctx'), None, 'tp'), may hold values from -0.1875 to 0.1875
- down_weight: bfloat16 [2048, 1024], P('tp', ('dp', 'ctx')), may hold values from -0.125 to 0.125
Outputs:
- block_out: bfloat16 [8, 1536, 1024], P('dp', 'ctx')
- loss: float32 [], replicated
- input_grad: bfloat16 [8, 1536, 1024], P('dp', 'ctx')
- mixgain_grad: float32 [1024], replicated
- query_grad: float32 [1024, 512], P(('dp', 'ctx'), 'tp')
- keyval_grad: float32 [1024, 2, 128], P(('dp', 'ctx'), None, 'tp')
- attnout_grad: float32 [512, 1024], P('tp', ('dp', 'ctx'))
- stream_grad: float32 [1024, 2, 1536], P(('dp', 'ctx'), None, 'tp')
- state_grad: float32 [1024, 256], P(('dp', 'ctx'))
- step_grad: float32 [1024, 24], P(('dp', 'ctx'), 'tp')
- convstream_grad: float32 [4, 1536], P(None, 'tp')
- biasstream_grad: float32 [1536], P('tp')
- convstate_grad: float32 [4, 256], replicated
- biasstate_grad: float32 [256], replicated
- stepbias_grad: float32 [24], P('tp')
- decay_grad: float32 [24], P('tp')
- skip_grad: float32 [24], P('tp')
- mambaout_grad: float32 [1536, 1024], P('tp', ('dp', 'ctx'))
- ffngain_grad: float32 [1024], replicated
- gateup_grad: float32 [1024, 2, 2048], P(('dp', 'ctx'), None, 'tp')
- down_grad: float32 [2048, 1024], P('tp', ('dp', 'ctx'))
Inputs may be any that keep to these rules, and one draw needn't show every extreme that they name: Within each sequence the positions rise by one from token to token, starting at an offset of 0 to 511; some sequence starts at 0 and some at 511. `valid_mask`: 1 marks a valid token; the first token of every sequence is valid.
All inputs are finite; a program needn't handle non-finite values.
Results may differ from a plain program's by a relative error of at most 0.015.
Values may be sent and summed in bfloat16 or wider, within the bound.
No kernel may reach another device: no remote copies, remote signals or barrier semaphores. Data moves between devices by JAX's collectives and lax.ppermute only.
A program may use at most 192 MiB of HBM per device.

v0:
```python
import jax
import jax.numpy as jnp
from jax import lax
from jax.sharding import PartitionSpec as P

HEAD_SIZE = 64
MP = 64
NS = 128
KC = 4
CBLK = 128


eps_norm = 1e-05
rope_base = 100000000000.0
highest = lax.Precision.HIGHEST


def passed_along(block, axis, distance):
    devices = range(lax.axis_size(axis))
    route = [(i - distance, i) for i in devices if i - distance in devices]
    return lax.ppermute(block, axis, route)


def prefix_2(part, axis, combine, identity, reverse):
    count = lax.axis_size(axis)
    place = lax.axis_index(axis)
    ahead = count - 1 - place if reverse else place
    gathered = jax.tree.map(lambda a: lax.all_gather(a, axis), part)
    state = jax.tree.map(lambda a, e: jnp.zeros_like(a) + jnp.asarray(e, a.dtype), part, identity)

    def one(turn, state):
        source = count - 1 - turn if reverse else turn
        return combine(
            state, jax.tree.map(lambda a: lax.dynamic_index_in_dim(a, source, 0, False), gathered)
        )

    return lax.fori_loop(0, ahead, one, state)


def rms_norm(values, gain):
    return values * lax.rsqrt(jnp.mean(values * values, -1, keepdims=True) + eps_norm) * gain


def rotary(values, places):
    half = values.shape[-1] // 2
    freqs = rope_base ** (-2.0 * jnp.arange(half, dtype=jnp.float32) / values.shape[-1])
    angles = places.astype(jnp.float32)[..., None] * freqs
    cosine = jnp.cos(angles)[..., None, :]
    sine = jnp.sin(angles)[..., None, :]
    first = values[..., :half]
    second = values[..., half:]
    return jnp.concatenate([first * cosine - second * sine, second * cosine + first * sine], -1)


def causal_conv(pre, prev, taps, bias):
    sequence_length = pre.shape[-2]
    extended = jnp.concatenate([prev, pre], -2)
    total = bias + taps[0] * extended[..., 0:sequence_length, :]
    for offset in range(1, taps.shape[0]):
        total = total + taps[offset] * extended[..., offset : offset + sequence_length, :]
    return jax.nn.silu(total)


def block_terms(stream, steps, rate, entry_map, read_map):
    sequence_length = stream.shape[0]
    logs = jnp.cumsum(-steps * rate, axis=0)
    gaps = logs.T[:, :, None] - logs.T[:, None, :]
    places = jnp.arange(sequence_length, dtype=jnp.int32)
    causal = places[:, None] >= places[None, :]
    decay = jnp.where(causal, jnp.exp(jnp.where(causal, gaps, 0.0)), 0.0)
    inner = jnp.dot(read_map, entry_map.T, precision=highest, preferred_element_type=jnp.float32)
    weighted = steps[:, :, None] * stream
    local_out = jnp.einsum("hts,ts,shp->thp", decay, inner, weighted, precision=highest)
    tail = jnp.exp(logs[-1][None, :] - logs)
    local_state = jnp.einsum("sh,shp,sn->hpn", tail, weighted, entry_map, precision=highest)
    return (local_out, local_state, jnp.exp(logs[-1]), logs)


def state_terms(logs, read_map, carried):
    return (
        jnp.einsum("tn,hpn->thp", read_map, carried, precision=highest) * jnp.exp(logs)[:, :, None]
    )


def local_part(stream_act, state_act, step_raw, step_bias, decay_log):
    seq_count, tokens, channels = stream_act.shape
    heads_here = step_raw.shape[-1]
    stream_heads = stream_act.reshape(seq_count, tokens, heads_here, MP)
    steps = jax.nn.softplus(step_raw + step_bias)
    rate = jnp.exp(decay_log)
    local_out, local_state, totals, logs = jax.vmap(block_terms, in_axes=(0, 0, None, 0, 0))(
        stream_heads, steps, rate, state_act[..., :NS], state_act[..., NS:]
    )
    return (local_out, local_state, totals)


def finish(
    gate_z, stream_act, state_act, step_raw, step_bias, decay_log, skip_scale, local_out, carried
):
    seq_count, tokens, channels = stream_act.shape
    heads_here = step_raw.shape[-1]
    stream_heads = stream_act.reshape(seq_count, tokens, heads_here, MP)
    steps = jax.nn.softplus(step_raw + step_bias)
    logs = jnp.cumsum(-steps * jnp.exp(decay_log), axis=1)
    incoming = jax.vmap(state_terms)(logs, state_act[..., NS:], carried)
    mixer_out = local_out + incoming
    gated = (mixer_out + skip_scale[:, None] * stream_heads) * jax.nn.silu(
        gate_z.reshape(seq_count, tokens, heads_here, MP)
    )
    return gated.reshape(seq_count, tokens, channels)


def chain(earlier, later):
    return (earlier[0] * later[0], later[0][..., None, None] * earlier[1] + later[1])


def swiglu(pair):
    return jax.nn.silu(pair[:, :, 0]) * pair[:, :, 1]


def per_device(
    hidden_in,
    positions,
    valid_mask,
    teacher,
    cotangent,
    mixer_gain,
    query_weight,
    keyvalue_projection_weight,
    attnout_weight,
    stream_weight,
    state_weight,
    step_weight,
    conv_stream,
    bias_stream,
    conv_state,
    bias_state,
    step_bias,
    decay_log,
    skip_scale,
    mambaout_weight,
    ffn_gain,
    gateup_weight,
    down_weight,
):
    seq_count, tokens, width = hidden_in.shape
    tallies = jnp.sum(valid_mask.reshape(seq_count * tokens // CBLK, CBLK), -1).astype(jnp.bfloat16)
    gathered = (
        lax.all_gather(query_weight, ("dp", "ctx"), axis=0, tiled=True),
        lax.all_gather(keyvalue_projection_weight, ("dp", "ctx"), axis=0, tiled=True),
        lax.all_gather(attnout_weight, ("dp", "ctx"), axis=1, tiled=True),
        lax.all_gather(stream_weight, ("dp", "ctx"), axis=0, tiled=True),
        lax.all_gather(state_weight, ("dp", "ctx"), axis=0, tiled=True),
        lax.all_gather(step_weight, ("dp", "ctx"), axis=0, tiled=True),
        lax.all_gather(mambaout_weight, ("dp", "ctx"), axis=1, tiled=True),
        lax.all_gather(gateup_weight, ("dp", "ctx"), axis=0, tiled=True),
        lax.all_gather(down_weight, ("dp", "ctx"), axis=1, tiled=True),
        lax.all_gather(tallies, ("dp", "ctx"), axis=0, tiled=True),
    )
    (
        query_full,
        keyval_full,
        attnout_full,
        stream_full,
        state_full,
        step_full,
        mambaout_full,
        gateup_full,
        down_full,
    ) = gathered[:9]
    valid_total = jnp.sum(gathered[9].astype(jnp.float32))
    ctx_index = lax.axis_index("ctx")
    rim = KC - 1
    hidden = hidden_in.astype(jnp.float32)
    normed = rms_norm(hidden, mixer_gain).astype(jnp.bfloat16)
    query_heads = query_full.shape[1] // HEAD_SIZE
    kv_heads = keyval_full.shape[2] // HEAD_SIZE
    group = query_heads // kv_heads
    query_pre = jnp.dot(normed, query_full, preferred_element_type=jnp.float32).reshape(
        seq_count, tokens, query_heads, HEAD_SIZE
    )
    keyvalue_projected = jnp.einsum(
        "std,dcj->stcj", normed, keyval_full, preferred_element_type=jnp.float32
    )
    key_before_rotation = keyvalue_projected[:, :, 0].reshape(
        seq_count, tokens, kv_heads, HEAD_SIZE
    )
    value_projected = keyvalue_projected[:, :, 1]
    queries = rotary(query_pre, positions).astype(jnp.bfloat16)
    keys_mine = (
        rotary(key_before_rotation, positions)
        .astype(jnp.bfloat16)
        .reshape(seq_count, tokens, kv_heads * HEAD_SIZE)
    )
    keyval_send = jnp.concatenate([keys_mine, value_projected.astype(jnp.bfloat16)], -1)
    streams = jnp.einsum("std,dcj->stcj", normed, stream_full, preferred_element_type=jnp.float32)
    gate_z = streams[:, :, 0]
    stream_pre = streams[:, :, 1]
    state_pre = jnp.dot(normed, state_full, preferred_element_type=jnp.float32)
    step_raw = jnp.dot(normed, step_full, preferred_element_type=jnp.float32)
    tails = passed_along((stream_pre[:, tokens - rim :], state_pre[:, tokens - rim :]), "ctx", 1)
    keyval_all = lax.all_gather(keyval_send, "ctx", axis=1, tiled=True)
    all_tokens = keyval_all.shape[1]
    key_all = keyval_all[..., : kv_heads * HEAD_SIZE].reshape(
        seq_count, all_tokens, kv_heads, HEAD_SIZE
    )
    value_all = keyval_all[..., kv_heads * HEAD_SIZE :].reshape(
        seq_count, all_tokens, kv_heads, HEAD_SIZE
    )
    stream_act = causal_conv(stream_pre, tails[0], conv_stream, bias_stream)
    state_act = causal_conv(state_pre, tails[1], conv_state, bias_state)
    local_out, local_state, totals = local_part(
        stream_act, state_act, step_raw, step_bias, decay_log
    )
    identity = (jnp.ones_like(totals), jnp.zeros_like(local_state))
    prefix = prefix_2((totals, local_state), "ctx", chain, identity, False)
    carried = prefix[1]
    gated = finish(
        gate_z,
        stream_act,
        state_act,
        step_raw,
        step_bias,
        decay_log,
        skip_scale,
        local_out,
        carried,
    )
    gated_low = gated.astype(jnp.bfloat16)
    scale = HEAD_SIZE ** (-0.5)
    query_index = ctx_index * tokens + jnp.arange(tokens, dtype=jnp.int32)
    allowed = jnp.arange(all_tokens, dtype=jnp.int32)[None, :] <= query_index[:, None]
    query_groups = queries.reshape(seq_count, tokens, kv_heads, group, HEAD_SIZE)

    def seq_scores(query_seq, key_seq):
        scores = (
            jnp.einsum("qkgd,jkd->kgqj", query_seq, key_seq, preferred_element_type=jnp.float32)
            * scale
        )
        return jnp.where(allowed, scores, -1e30)

    def attend(pieces):
        query_seq, key_seq, value_seq = pieces
        scores = seq_scores(query_seq, key_seq)
        top_score = jnp.max(scores, -1, keepdims=True)
        expo = jnp.exp(scores - top_score)
        denom = jnp.sum(expo, -1, keepdims=True)
        probs = (expo / denom).astype(jnp.bfloat16)
        outputs = jnp.einsum("kgqj,jkd->qkgd", probs, value_seq, preferred_element_type=jnp.float32)
        return (outputs, top_score + jnp.log(denom))

    attended, log_total = lax.map(attend, (query_groups, key_all, value_all))
    attended_low = attended.reshape(seq_count, tokens, query_heads * HEAD_SIZE).astype(jnp.bfloat16)
    mix_part = jnp.dot(attended_low, attnout_full, preferred_element_type=jnp.float32) + jnp.dot(
        gated_low, mambaout_full, preferred_element_type=jnp.float32
    )
    mixed = lax.psum(mix_part, "tp")
    resid = hidden + mixed
    normed_two = rms_norm(resid, ffn_gain).astype(jnp.bfloat16)
    gateup = jnp.einsum(
        "std,dcf->stcf", normed_two, gateup_full, preferred_element_type=jnp.float32
    )
    inner = swiglu(gateup).astype(jnp.bfloat16)
    down_part = jnp.dot(inner, down_full, preferred_element_type=jnp.float32)
    down = lax.psum(down_part.astype(jnp.bfloat16), "tp").astype(jnp.float32)
    out_full = resid + down
    block_out = out_full.astype(jnp.bfloat16)
    mask_float = valid_mask.astype(jnp.float32)[..., None]
    diff = out_full - teacher.astype(jnp.float32)
    squares_local = jnp.sum(mask_float * diff * diff)
    loss_scale = 1.0 / (valid_total * width)
    out_grad = cotangent.astype(jnp.float32) + mask_float * 2.0 * diff * loss_scale
    (
        query_full,
        keyval_full,
        attnout_full,
        stream_full,
        state_full,
        step_full,
        mambaout_full,
        gateup_full,
        down_full,
    ) = (
        lax.all_gather(query_weight, ("dp", "ctx"), axis=0, tiled=True),
        lax.all_gather(keyvalue_projection_weight, ("dp", "ctx"), axis=0, tiled=True),
        lax.all_gather(attnout_weight, ("dp", "ctx"), axis=1, tiled=True),
        lax.all_gather(stream_weight, ("dp", "ctx"), axis=0, tiled=True),
        lax.all_gather(state_weight, ("dp", "ctx"), axis=0, tiled=True),
        lax.all_gather(step_weight, ("dp", "ctx"), axis=0, tiled=True),
        lax.all_gather(mambaout_weight, ("dp", "ctx"), axis=1, tiled=True),
        lax.all_gather(gateup_weight, ("dp", "ctx"), axis=0, tiled=True),
        lax.all_gather(down_weight, ("dp", "ctx"), axis=1, tiled=True),
    )
    down_in = out_grad.astype(jnp.bfloat16)
    down_wgrad = jnp.einsum("stf,std->fd", inner, down_in, preferred_element_type=jnp.float32)
    inner_grad = jnp.einsum("std,fd->stf", down_in, down_full, preferred_element_type=jnp.float32)
    _, swiglu_back = jax.vjp(swiglu, gateup)
    gateup_low = swiglu_back(inner_grad)[0].astype(jnp.bfloat16)
    gateup_wgrad = jnp.einsum(
        "std,stcf->dcf", normed_two, gateup_low, preferred_element_type=jnp.float32
    )
    normed_two_part = jnp.einsum(
        "stcf,dcf->std", gateup_low, gateup_full, preferred_element_type=jnp.float32
    )
    normed_two_grad = lax.psum(normed_two_part, "tp")
    _, norm_two_back = jax.vjp(rms_norm, resid, ffn_gain)
    resid_norm_grad, ffn_gain_grad = norm_two_back(normed_two_grad)
    resid_grad = out_grad + resid_norm_grad
    mixed_low = resid_grad.astype(jnp.bfloat16)
    attnout_wgrad = jnp.einsum(
        "sti,std->id", attended_low, mixed_low, preferred_element_type=jnp.float32
    )
    mambaout_wgrad = jnp.einsum(
        "stj,std->jd", gated_low, mixed_low, preferred_element_type=jnp.float32
    )
    attended_grad = jnp.einsum(
        "std,id->sti", mixed_low, attnout_full, preferred_element_type=jnp.float32
    )
    attended_grad = attended_grad.astype(jnp.bfloat16).reshape(
        seq_count, tokens, kv_heads, group, HEAD_SIZE
    )
    gated_grad = jnp.einsum(
        "std,jd->stj", mixed_low, mambaout_full, preferred_element_type=jnp.float32
    )

    def attend_back(pieces):
        query_seq, key_seq, value_seq, out_grad_seq, log_seq = pieces
        probs_full = jnp.exp(seq_scores(query_seq, key_seq) - log_seq)
        prob_grad = jnp.einsum(
            "qkgd,jkd->kgqj", out_grad_seq, value_seq, preferred_element_type=jnp.float32
        )
        centre = jnp.sum(probs_full * prob_grad, -1, keepdims=True)
        score_grad = (probs_full * (prob_grad - centre)).astype(jnp.bfloat16)
        query_part = (
            jnp.einsum("kgqj,jkd->qkgd", score_grad, key_seq, preferred_element_type=jnp.float32)
            * scale
        )
        key_part = (
            jnp.einsum("kgqj,qkgd->jkd", score_grad, query_seq, preferred_element_type=jnp.float32)
            * scale
        )
        value_part = jnp.einsum(
            "kgqj,qkgd->jkd",
            probs_full.astype(jnp.bfloat16),
            out_grad_seq,
            preferred_element_type=jnp.float32,
        )
        joined = jnp.concatenate(
            [
                key_part.reshape(all_tokens, kv_heads * HEAD_SIZE),
                value_part.reshape(all_tokens, kv_heads * HEAD_SIZE),
            ],
            -1,
        )
        return (query_part, joined)

    query_grad_rot, keyval_grad_all = lax.map(
        attend_back, (query_groups, key_all, value_all, attended_grad, log_total)
    )
    keyval_grad_mine = lax.psum_scatter(
        keyval_grad_all.astype(jnp.bfloat16), "ctx", scatter_dimension=1, tiled=True
    ).astype(jnp.float32)
    _, query_rope_back = jax.vjp(lambda values: rotary(values, positions), query_pre)
    query_in_grad = query_rope_back(
        query_grad_rot.reshape(seq_count, tokens, query_heads, HEAD_SIZE)
    )[0]
    query_in_low = query_in_grad.reshape(seq_count, tokens, query_heads * HEAD_SIZE).astype(
        jnp.bfloat16
    )
    _, key_rope_back = jax.vjp(lambda values: rotary(values, positions), key_before_rotation)
    key_in_grad = key_rope_back(
        keyval_grad_mine[..., : kv_heads * HEAD_SIZE].reshape(
            seq_count, tokens, kv_heads, HEAD_SIZE
        )
    )[0]
    keyval_in_low = jnp.stack(
        [
            key_in_grad.reshape(seq_count, tokens, kv_heads * HEAD_SIZE),
            keyval_grad_mine[..., kv_heads * HEAD_SIZE :],
        ],
        2,
    ).astype(jnp.bfloat16)
    _, finish_back = jax.vjp(
        finish,
        gate_z,
        stream_act,
        state_act,
        step_raw,
        step_bias,
        decay_log,
        skip_scale,
        local_out,
        carried,
    )
    (
        gate_grad,
        stream_grad_one,
        state_grad_one,
        step_grad_one,
        stepbias_one,
        decay_one,
        skip_grad_all,
        local_out_grad,
        carried_grad,
    ) = finish_back(gated_grad)
    after_prefix = prefix_2((totals, carried_grad), "ctx", chain, identity, True)
    later_grad = after_prefix[1]
    totals_grad = jnp.sum(later_grad * carried, (-2, -1))
    _, local_back = jax.vjp(local_part, stream_act, state_act, step_raw, step_bias, decay_log)
    stream_grad_two, state_grad_two, step_grad_two, stepbias_two, decay_two = local_back(
        (local_out_grad, later_grad, totals_grad)
    )
    _, stream_conv_back = jax.vjp(causal_conv, stream_pre, tails[0], conv_stream, bias_stream)
    stream_pre_grad, stream_tail_grad, conv_stream_grad, bias_stream_grad = stream_conv_back(
        stream_grad_one + stream_grad_two
    )
    _, state_conv_back = jax.vjp(causal_conv, state_pre, tails[1], conv_state, bias_state)
    state_pre_grad, state_tail_grad, conv_state_grad, bias_state_grad = state_conv_back(
        state_grad_one + state_grad_two
    )
    back_tails = passed_along((stream_tail_grad, state_tail_grad), "ctx", -1)
    stream_pre_grad = jnp.concatenate(
        [stream_pre_grad[:, : tokens - rim], stream_pre_grad[:, tokens - rim :] + back_tails[0]], 1
    )
    state_pre_grad = jnp.concatenate(
        [state_pre_grad[:, : tokens - rim], state_pre_grad[:, tokens - rim :] + back_tails[1]], 1
    )
    streams_low = jnp.stack([gate_grad, stream_pre_grad], 2).astype(jnp.bfloat16)
    step_low = (step_grad_one + step_grad_two).astype(jnp.bfloat16)
    normed_part = (
        jnp.einsum("sti,di->std", query_in_low, query_full, preferred_element_type=jnp.float32)
        + jnp.einsum(
            "stcj,dcj->std", keyval_in_low, keyval_full, preferred_element_type=jnp.float32
        )
        + jnp.einsum("stcj,dcj->std", streams_low, stream_full, preferred_element_type=jnp.float32)
        + jnp.einsum("sth,dh->std", step_low, step_full, preferred_element_type=jnp.float32)
        + jnp.einsum(
            "stn,dn->std", state_pre_grad, state_full.astype(jnp.float32), precision=highest
        )
    )
    normed_grad, state_pre_total = (
        lax.psum(normed_part.astype(jnp.bfloat16), "tp").astype(jnp.float32),
        lax.psum(state_pre_grad.astype(jnp.bfloat16), "tp").astype(jnp.float32),
    )
    _, norm_one_back = jax.vjp(rms_norm, hidden, mixer_gain)
    hidden_norm_grad, mixer_gain_grad = norm_one_back(normed_grad)
    input_grad = (resid_grad + hidden_norm_grad).astype(jnp.bfloat16)
    query_wgrad = jnp.einsum(
        "std,sti->di", normed, query_in_low, preferred_element_type=jnp.float32
    )
    keyval_wgrad = jnp.einsum(
        "std,stcj->dcj", normed, keyval_in_low, preferred_element_type=jnp.float32
    )
    stream_wgrad = jnp.einsum(
        "std,stcj->dcj", normed, streams_low, preferred_element_type=jnp.float32
    )
    state_wgrad = jnp.einsum(
        "std,stn->dn", normed.astype(jnp.float32), state_pre_total, precision=highest
    )
    step_wgrad = jnp.einsum("std,sth->dh", normed, step_low, preferred_element_type=jnp.float32)
    grad_terms = (
        query_wgrad,
        keyval_wgrad,
        attnout_wgrad,
        stream_wgrad,
        state_wgrad,
        step_wgrad,
        mambaout_wgrad,
        gateup_wgrad,
        down_wgrad,
    )
    reduced = (
        lax.psum_scatter(grad_terms[0], ("dp", "ctx"), scatter_dimension=0, tiled=True),
        lax.psum_scatter(grad_terms[1], ("dp", "ctx"), scatter_dimension=0, tiled=True),
        lax.psum_scatter(grad_terms[2], ("dp", "ctx"), scatter_dimension=1, tiled=True),
        lax.psum_scatter(grad_terms[3], ("dp", "ctx"), scatter_dimension=0, tiled=True),
        lax.psum_scatter(grad_terms[4], ("dp", "ctx"), scatter_dimension=0, tiled=True),
        lax.psum_scatter(grad_terms[5], ("dp", "ctx"), scatter_dimension=0, tiled=True),
        lax.psum_scatter(grad_terms[6], ("dp", "ctx"), scatter_dimension=1, tiled=True),
        lax.psum_scatter(grad_terms[7], ("dp", "ctx"), scatter_dimension=0, tiled=True),
        lax.psum_scatter(grad_terms[8], ("dp", "ctx"), scatter_dimension=1, tiled=True),
    )
    tp_index = lax.axis_index("tp")
    tp_count = lax.axis_size("tp")

    def widen(piece, axis_dim):
        shape_full = list(piece.shape)
        shape_full[axis_dim] = piece.shape[axis_dim] * tp_count
        blank = jnp.zeros(tuple(shape_full), jnp.float32)
        return lax.dynamic_update_slice_in_dim(
            blank, piece, tp_index * piece.shape[axis_dim], axis_dim
        )

    def narrow(whole, axis_dim, piece_size):
        return lax.dynamic_slice_in_dim(whole, tp_index * piece_size, piece_size, axis_dim)

    summed = lax.psum(
        (
            mixer_gain_grad / tp_count,
            ffn_gain_grad / tp_count,
            widen(conv_stream_grad, 1),
            widen(bias_stream_grad, 0),
            conv_state_grad,
            bias_state_grad,
            widen(stepbias_one + stepbias_two, 0),
            widen(decay_one + decay_two, 0),
            widen(skip_grad_all, 0),
            squares_local / tp_count,
        ),
        ("dp", "ctx", "tp"),
    )
    channels_here = conv_stream.shape[1]
    heads_here = step_bias.shape[0]
    loss = summed[9] * loss_scale
    return (
        block_out,
        loss,
        input_grad,
        summed[0],
        reduced[0],
        reduced[1],
        reduced[2],
        reduced[3],
        reduced[4],
        reduced[5],
        narrow(summed[2], 1, channels_here),
        narrow(summed[3], 0, channels_here),
        summed[4],
        summed[5],
        narrow(summed[6], 0, heads_here),
        narrow(summed[7], 0, heads_here),
        narrow(summed[8], 0, heads_here),
        reduced[6],
        summed[1],
        reduced[7],
        reduced[8],
    )


def solution(mesh):
    return jax.shard_map(
        per_device,
        mesh=mesh,
        in_specs=(
            P("dp", "ctx", None),
            P("dp", "ctx"),
            P("dp", "ctx"),
            P("dp", "ctx", None),
            P("dp", "ctx", None),
            P(),
            P(("dp", "ctx"), "tp"),
            P(("dp", "ctx"), None, "tp"),
            P("tp", ("dp", "ctx")),
            P(("dp", "ctx"), None, "tp"),
            P(("dp", "ctx"), None),
            P(("dp", "ctx"), "tp"),
            P(None, "tp"),
            P("tp"),
            P(),
            P(),
            P("tp"),
            P("tp"),
            P("tp"),
            P("tp", ("dp", "ctx")),
            P(),
            P(("dp", "ctx"), None, "tp"),
            P("tp", ("dp", "ctx")),
        ),
        out_specs=(
            P("dp", "ctx", None),
            P(),
            P("dp", "ctx", None),
            P(),
            P(("dp", "ctx"), "tp"),
            P(("dp", "ctx"), None, "tp"),
            P("tp", ("dp", "ctx")),
            P(("dp", "ctx"), None, "tp"),
            P(("dp", "ctx"), None),
            P(("dp", "ctx"), "tp"),
            P(None, "tp"),
            P("tp"),
            P(),
            P(),
            P("tp"),
            P("tp"),
            P("tp"),
            P("tp", ("dp", "ctx")),
            P(),
            P(("dp", "ctx"), None, "tp"),
            P("tp", ("dp", "ctx")),
        ),
        check_vma=False,
    )
```

profile of v0, /device:TPU:0, one launch (start us, length us, event | category | flops | bytes accessed | tf_op | source)
XLA Modules:
  0.0 1480.7 jit_solution(15852878700789439621)
XLA Ops:
  11.5 25.7 %all_gather.65 = bf16[1024,256]{1,0:T(8,128)(2,1)S(1)} all-gather(bf16[64,256]{1,0:T(8,128)(2,1)} %param.42), channel_id=1, replica_groups=mesh['dp'=4,'ctx'=4,'tp'=2] {'dp','ctx'}, dimensions={0}, use_global_device_ids=true | all-gather | bytes 557056 | tf_op jit(solution)/shard_map/all_gather | solution.py:153
  41.5 17.5 %all-gather.3 = bf16[16,64,12]{1,2,0:T(8,128)(2,1)S(1)} all-gather(bf16[1,64,12]{1,2,0:T(8,128)(2,1)S(1)} %bitcast.727), channel_id=1, replica_groups=mesh['dp'=4,'ctx'=4,'tp'=2] {'dp','ctx'}, dimensions={0}, use_global_device_ids=true | all-gather | bytes 26112 | tf_op jit(solution)/shard_map/all_gather | solution.py:154
  68.6 4.6 fusion.111
  85.2 4.2 fusion.136
  92.3 24.4 %all_gather.60 = bf16[1024,2,64]{2,1,0:T(2,128)(2,1)} all-gather(bf16[64,2,64]{2,1,0:T(2,128)(2,1)} %param.39), channel_id=1, replica_groups=mesh['dp'=4,'ctx'=4,'tp'=2] {'dp','ctx'}, dimensions={0}, use_global_device_ids=true | all-gather | bytes 278528 | tf_op jit(solution)/shard_map/all_gather | solution.py:150
  124.5 5.7 all-gather
  132.0 9.0 all_gather.61
  141.9 19.4 %all_gather.62 = bf16[1024,256]{1,0:T(8,128)(2,1)S(1)} all-gather(bf16[64,256]{1,0:T(8,128)(2,1)S(1)} %copy-done.94), channel_id=1, replica_groups=mesh['dp'=4,'ctx'=4,'tp'=2] {'dp','ctx'}, dimensions={0}, use_global_device_ids=true | all-gather | bytes 557056 | tf_op jit(solution)/shard_map/all_gather | solution.py:149
  165.9 17.2 %while.58 = (s32[]{:T(128)}, bf16[2,384,1,4,64]{1,4,3,2,0:T(8,128)(2,1)}, f32[2,1,4,384,1]{3,2,4,1,0:T(4,128)S(1)}, bf16[2,1536,1,64]{1,3,2,0:T(8,128)(2,1)}, bf...) while((s32[]{:T(128)}, ...), condition=%wide.region_4.5_spmd.clone.clone, body=%wide.region_1.4_spmd.clone.sunk.clone | while | flops 632879616 | bytes 33279596 | solution.py:252
  170.9 3.5 fusion.382
  179.5 3.5 fusion.382
  183.0 22.8 %all_gather.63 = bf16[256,1024]{0,1:T(8,128)(2,1)} all-gather(bf16[256,64]{0,1:T(8,128)(2,1)} %param.40), channel_id=1, replica_groups=mesh['dp'=4,'ctx'=4,'tp'=2] {'dp','ctx'}, dimensions={1}, use_global_device_ids=true | all-gather | bytes 557056 | tf_op jit(solution)/shard_map/all_gather | solution.py:151
  216.1 21.6 %fusion.130 = (bf16[2,384,12,64]{1,3,2,0:T(8,128)(2,1)}, f32[2,12,384,64]{2,3,1,0:T(8,128)}) fusion(f32[2,384,12,64]{1,3,2,0:T(8,128)S(1)} %fusion.214, f32[2,384,12,64]{1,3,2,0:T(8,128)S(1)} %bitcast.686, f32[12]{0:T(128)S(1)} %copy-done.139, f32[2,384,12]{1,2,0:T(8,128)} %copy.541, f32[2,384,12,64]{1,3,2,0:T(8,128)S(1)} %bitcast.694, ...), kind=kOutput, calls=%fused_computation.184 | convolution fusion | flops 2738552832 | bytes 12054576 | tf_op jit(solution)/shard_map/vmap(hts,ts,shp->thp)/dot_general | solution.py:73
  246.6 86.0 %all-reduce.35.cloned.1.call-done = f32[2,384,1024]{2,1,0:T(8,128)} async-done(((f32[2,384,1024]{2,1,0:T(8,128)}), f32[2,384,1024]{2,1,0:T(8,128)}) %all-reduce.35.cloned.1.call-update) | async-done | bytes 3145744 | tf_op jit(solution)/shard_map/psum | solution.py:257
  337.2 48.9 %all-gather.15.cloned.1.call-done = bf16[1024,2,1024]{2,0,1:T(8,128)(2,1)} async-done(((bf16[64,2,1024]{2,0,1:T(8,128)(2,1)}), bf16[1024,2,1024]{2,0,1:T(8,128)(2,1)}) %all-gather.15.cloned.1.call-update) | async-done | bytes 4194320 | tf_op jit(solution)/shard_map/all_gather | solution.py:156
  386.1 5.7 fusion.91
  396.5 31.7 %all-gather.17.cloned.1.call-done = bf16[1024,1024]{0,1:T(8,128)(2,1)} async-done(((bf16[1024,64]{0,1:T(8,128)(2,1)}), bf16[1024,1024]{0,1:T(8,128)(2,1)}) %all-gather.17.cloned.1.call-update) | async-done | bytes 2097168 | tf_op jit(solution)/shard_map/all_gather | solution.py:157
  428.2 5.0 fusion.156
  440.8 32.1 %all-reduce.27 = bf16[96]{0:T(256)(128)(2,1)} all-reduce(bf16[96]{0:T(256)(128)(2,1)} %dynamic-update-slice), channel_id=1, replica_groups=mesh['dp'=4,'ctx'=4,'tp'=2] {'dp','ctx'}, use_global_device_ids=true, to_apply=%add.27 | all-reduce | flops 96 | bytes 384
  476.1 7.6 all-reduce.37.cloned.1.call-done
  483.7 3.4 fusion.151
  494.0 5.2 fusion.148
  503.3 4.3 reduce-window.30
  522.4 62.7 %all-reduce.39.cloned.1.call-done = f32[2,384,1024]{2,1,0:T(8,128)} async-done(((f32[2,384,1024]{2,1,0:T(8,128)}), f32[2,384,1024]{2,1,0:T(8,128)}) %all-reduce.39.cloned.1.call-update) | async-done | bytes 3145744 | tf_op jit(solution)/shard_map/psum | solution.py:305
  585.2 4.5 multiply_reduce_fusion
  595.4 57.1 %while.59 = (s32[]{:T(128)}, f32[2,384,1,4,64]{1,4,3,2,0:T(8,128)}, bf16[2,1536,128]{1,2,0:T(8,128)(2,1)S(1)}, bf16[2,1536,1,64]{1,3,2,0:T(8,128)(2,1)S(1)}, bf1...) while((s32[]{:T(128)}, f32[2,384,1,4,64]{1,4,3,2,0:T(8,128)}, ...), condition=%wide.region_20.21_spmd.clone.clone, body=%wide.region_18.20_spmd.clone.sunk.clone | while | flops 1532852736 | bytes 126847664 | solution.py:357
  597.3 6.0 fusion.392
  603.3 9.6 fusion.393
  612.9 4.0 fusion.396
  616.9 5.3 fusion.395
  625.8 6.0 fusion.392
  631.8 9.6 fusion.393
  641.4 4.0 fusion.396
  645.5 5.3 fusion.395
  654.2 4.2 fusion.168
  658.4 3.3 copy.559
  661.7 4.9 multiply_reduce_fusion.10
  671.3 23.1 %fusion.78 = (f32[2,12,384]{2,1,0:T(8,128)}, f32[2,12,384]{2,1,0:T(8,128)}, f32[2,12,384,384]{3,2,1,0:T(8,128)}) fusion(f32[2,384,384]{2,1,0:T(8,128)} %fusion.223, f32[2,12,384]{2,1,0:T(8,128)} %get-tuple-element.694, pred[384,384]{1,0:T(8,128)(4,1)} %iota_compare_fusion.2, f32[2,384,12,64]{1,3,2,0:T(8,128)S(1)} %bitcast.689, ...), kind=kOutput, calls=%fused_computation.90 | convolution fusion | flops 2746791936 | bytes 20348928 | tf_op jit(solution)/shard_map/transpose(jvp(vmap(hts,ts,shp->thp)))/dot_general | solution.py:73
  700.3 7.5 reduce-window.34
  710.1 4.6 fusion.178
  714.7 7.5 fusion.64
  735.0 3.5 fusion.201
  738.6 6.0 while.57
  744.8 3.4 fusion.216
  749.2 16.1 %multiply_reduce_fusion.3 = (f32[2,384,12]{1,2,0:T(8,128)}, f32[2,384,12]{1,2,0:T(8,128)}, f32[2,384,12,64]{1,3,2,0:T(8,128)}) fusion(f32[2,384,12,64]{1,3,2,0:T(8,128)} %fusion.216, f32[2,384,12,64]{1,3,2,0:T(8,128)} %bitcast.687, f32[2,384,12]{1,2,0:T(8,128)S(1)} %copy-done.71, f32[2,12,384]{2,1,0:T(8,128)S(1)} %copy-done.73, ...), kind=kOutput, calls=%fused_computation.187 | convolution fusion | flops 2736764928 | bytes 10948608 | tf_op jit(solution)/shard_map/transpose(jvp(vmap(hts,ts,shp->thp)))/dot_general | solution.py:73
  768.5 8.6 multiply_reduce_fusion.4
  784.2 3.9 fusion.184
  798.9 7.5 reduce-window.36
  821.1 3.4 fusion.110
  827.8 8.7 convolution_bitcast_fusion.1
  838.3 6.0 convolution_bitcast_fusion.2
  850.0 5.7 convolution_bitcast_fusion.3
  855.8 4.4 convolution_bitcast_fusion.4
  862.8 24.0 %all-reduce.41.cloned.1.call-done = (bf16[2,384,1024]{2,1,0:T(8,128)(2,1)}, bf16[2,384,256]{2,1,0:T(8,128)(2,1)}) async-done(((bf16[2,384,1024]{2,1,0:T(8,128)(2,1)}, bf16[2,384,256]{2,1,0:T(8,128)(2,1)}), (bf16[2,384,1024]{2,1,0:T(8,128)(2,1)}, bf16[2,384,256]{2,1,0:T(8,128)(2,1)})) %all-reduce.41.cloned.1.call-update) | async-done | bytes 1966096 | tf_op jit(solution)/shard_map/psum | solution.py:442
  890.7 56.0 %reduce-scatter.33.cloned.1.call-done = f32[64,12]{1,0:T(8,128)} async-done(((f32[1024,12]{1,0:T(8,128)}), f32[64,12]{1,0:T(8,128)}) %reduce-scatter.33.cloned.1.call-update) | async-done | bytes 3088
  949.6 41.4 %all-reduce.28 = (f32[]{:T(128)}, f32[1024]{0:T(1024)}, f32[4,1536]{1,0:T(4,128)S(1)}, f32[1536]{0:T(1024)S(1)}, f32[4,256]{1,0:T(4,128)}, /*index=5*/f32[256]{0...) all-reduce(f32[]{:T(128)S(6)} %div.92, ...), channel_id=1, replica_groups=mesh['dp'=4,'ctx'=4,'tp'=2] {'dp','ctx','tp'}, use_global_device_ids=true, to_apply=%region_13.14 | all-reduce | flops 11081 | bytes 88648 | tf_op jit(solution)/shard_map/psum | solution.py:497
  994.7 4.0 fusion.103
  998.7 56.2 %reduce-scatter.27.cloned.1.call-done = f32[64,2,1024]{2,0,1:T(8,128)} async-done(((f32[1024,2,1024]{2,0,1:T(8,128)}), f32[64,2,1024]{2,0,1:T(8,128)}) %reduce-scatter.27.cloned.1.call-update) | async-done | bytes 524304 | tf_op jit(solution)/shard_map/reduce_scatter | solution.py:480
  1057.1 87.1 %reduce-scatter.21.cloned.1.call-done = f32[64,2,768]{2,0,1:T(8,128)} async-done(((f32[1024,2,768]{2,0,1:T(8,128)}), f32[64,2,768]{2,0,1:T(8,128)}) %reduce-scatter.21.cloned.1.call-update) | async-done | bytes 393232 | tf_op jit(solution)/shard_map/reduce_scatter | solution.py:476
  1146.2 58.5 %reduce-scatter.15.cloned.1.call-done = f32[64,256]{1,0:T(8,128)} async-done(((f32[1024,256]{1,0:T(8,128)}), f32[64,256]{1,0:T(8,128)}) %reduce-scatter.15.cloned.1.call-update) | async-done | bytes 65552 | tf_op jit(solution)/shard_map/reduce_scatter | solution.py:473
  1204.8 60.9 %reduce-scatter.19.cloned.1.call-done = f32[256,64]{0,1:T(8,128)} async-done(((f32[256,1024]{0,1:T(8,128)}), f32[256,64]{0,1:T(8,128)}) %reduce-scatter.19.cloned.1.call-update) | async-done | bytes 65552 | tf_op jit(solution)/shard_map/reduce_scatter | solution.py:475
  1265.7 75.8 %reduce-scatter.29.cloned.1.call-done = f32[1024,64]{0,1:T(8,128)} async-done(((f32[1024,1024]{0,1:T(8,128)}), f32[1024,64]{0,1:T(8,128)}) %reduce-scatter.29.cloned.1.call-update) | async-done | bytes 262160 | tf_op jit(solution)/shard_map/reduce_scatter | solution.py:481
  1341.5 70.1 %reduce-scatter.25.cloned.1.call-done = f32[768,64]{0,1:T(8,128)} async-done(((f32[768,1024]{0,1:T(8,128)}), f32[768,64]{0,1:T(8,128)}) %reduce-scatter.25.cloned.1.call-update) | async-done | bytes 196624 | tf_op jit(solution)/shard_map/reduce_scatter | solution.py:479
  1411.6 60.9 %reduce-scatter.23.cloned.1.call-done = f32[64,256]{1,0:T(8,128)} async-done(((f32[1024,256]{1,0:T(8,128)}), f32[64,256]{1,0:T(8,128)}) %reduce-scatter.23.cloned.1.call-update) | async-done | bytes 65552 | tf_op jit(solution)/shard_map/reduce_scatter | solution.py:477
  (589 shorter events, 230.3 us)
Async XLA Ops:
  7.2 30.7 %copy-start.16 = (bf16[2,384,1024]{2,1,0:T(8,128)(2,1)S(1)}, bf16[2,384,1024]{2,1,0:T(8,128)(2,1)}, u32[]{:S(2)}) copy-start(bf16[2,384,1024]{2,1,0:T(8,128)(2,1)} %param.32) | copy-start | bytes 4718596
  7.2 30.7 %copy-start.105 = (f32[1024]{0:T(1024)S(1)}, f32[1024]{0:T(1024)}, u32[]{:S(2)}) copy-start(f32[1024]{0:T(1024)} %param.37) | copy-start | bytes 12292
  7.2 61.4 %all-gather.11.cloned.1.call-start = ((), (), s32[]{:S(2)}) async-start(), calls=%async_computation.10 | async-start | bytes 3342336 | tf_op jit(solution)/shard_map/all_gather | solution.py:152
  9.0 202.0 %all-gather.19.cloned.1.call-start = ((), (), s32[]{:S(2)}) async-start(), calls=%async_computation.25 | async-start | bytes 3932160 | tf_op jit(solution)/shard_map/all_gather | solution.py:28
  11.4 47.8 %copy-start.97 = (f32[2,384]{1,0:T(2,128)}, f32[2,384]{1,0:T(2,128)S(1)}, u32[]{:S(2)}) copy-start(f32[2,384]{1,0:T(2,128)S(1)} %fusion.277) | copy-start | bytes 9220
  11.4 30.1 %copy-start.137 = (bf16[64,12]{0,1:T(8,128)(2,1)S(1)}, bf16[64,12]{0,1:T(8,128)(2,1)}, u32[]{:S(2)}) copy-start(bf16[64,12]{0,1:T(8,128)(2,1)} %param.43) | copy-start | bytes 4612
  37.9 21.2 %copy-start.146 = (f32[12]{0:T(128)S(1)}, f32[12]{0:T(128)}, u32[]{:S(2)}) copy-start(f32[12]{0:T(128)} %param.49) | copy-start | bytes 148
  37.9 21.3 %copy-start.151 = (f32[12]{0:T(128)S(1)}, f32[12]{0:T(128)}, u32[]{:S(2)}) copy-start(f32[12]{0:T(128)} %param.48) | copy-start | bytes 148
  38.6 39.9 %copy-start.46 = (f32[2,384,256]{2,1,0:T(8,128)}, f32[2,384,256]{2,1,0:T(8,128)S(1)}, u32[]{:S(2)}) copy-start(f32[2,384,256]{2,1,0:T(8,128)S(1)} %fusion.204) | copy-start | bytes 2359300
  39.2 39.2 %collective-permute-start = (f32[2,3,256]{2,1,0:T(4,128)}, f32[2,3,256]{2,1,0:T(4,128)S(1)}, u32[]{:S(2)}, u32[]{:S(2)}) collective-permute-start(f32[2,3,256]{2,1,0:T(4,128)} %slice.222), channel_id=1, source_target_pairs={{0,2},{2,4},{4,6},{1,3},{3,5},{5,7},{8,10},{10,12},{12,14},{9,11},... | collective-permute-start | bytes 18440 | tf_op jit(solution)/shard_map/ppermute | solution.py:21
  60.4 12.8 copy-start.80
  66.2 13.8 copy-start.84
  66.2 13.8 copy-start.86
  66.2 13.8 copy-start.88
  66.2 13.8 copy-start.90
  67.0 11.4 copy-start.120
  67.1 11.5 copy-start.122
  67.1 11.5 copy-start.124
  67.1 11.5 copy-start.126
  76.2 3.7 collective-permute-start.1
  79.9 125.9 %copy-start.23 = (f32[2,384,256]{2,1,0:T(8,128)}, f32[2,384,256]{2,1,0:T(8,128)S(1)}, u32[]{:S(2)}) copy-start(f32[2,384,256]{2,1,0:T(8,128)S(1)} %get-tuple-element.650) | copy-start | bytes 2359300
  85.2 129.6 %copy-start.5 = (f32[2,384,768]{1,2,0:T(8,128)}, f32[2,384,768]{1,2,0:T(8,128)S(1)}, u32[]{:S(2)}) copy-start(f32[2,384,768]{1,2,0:T(8,128)S(1)} %copy.537) | copy-start | bytes 7077892
  85.2 33.5 %copy-start.98 = (f32[2,384]{1,0:T(2,128)S(1)}, f32[2,384]{1,0:T(2,128)}, u32[]{:S(2)}) copy-start(f32[2,384]{1,0:T(2,128)} %copy-done.97) | copy-start | bytes 9220
  85.2 33.5 %copy-start.106 = (f32[1024]{0:T(1024)S(1)}, f32[1024]{0:T(1024)}, u32[]{:S(2)}) copy-start(f32[1024]{0:T(1024)} %param.37) | copy-start | bytes 12292
  89.4 148.3 %all-gather.13.cloned.1.call-start = ((), (), s32[]{:S(2)}) async-start(), calls=%async_computation.11 | async-start | bytes 1671168 | tf_op jit(solution)/shard_map/all_gather | solution.py:155
  90.1 242.5 %all-reduce.35.cloned.1.call-start = ((), (), s32[]{:S(2)}) async-start(), calls=%async_computation.12 | async-start | bytes 6291456 | tf_op jit(solution)/shard_map/psum | solution.py:257
  92.3 30.3 %copy-start.129 = (f32[32]{0:T(128)}, f32[32]{0:T(128)S(1)}, u32[]{:S(2)}) copy-start(f32[32]{0:T(128)S(1)} %multiply_power_fusion) | copy-start | bytes 388
  92.3 28.5 %copy-start.138 = (s32[2,384]{1,0:T(2,128)S(1)}, s32[2,384]{1,0:T(2,128)}, u32[]{:S(2)}) copy-start(s32[2,384]{1,0:T(2,128)} %param.33) | copy-start | bytes 9220
  131.0 10.9 copy-start.94
  131.0 31.1 %copy-start.17 = (bf16[2,384,1024]{2,1,0:T(8,128)(2,1)S(1)}, bf16[2,384,1024]{2,1,0:T(8,128)(2,1)}, u32[]{:S(2)}) copy-start(bf16[2,384,1024]{2,1,0:T(8,128)(2,1)} %param.32) | copy-start | bytes 4718596
  131.0 31.1 %copy-start.107 = (f32[1024]{0:T(1024)S(1)}, f32[1024]{0:T(1024)}, u32[]{:S(2)}) copy-start(f32[1024]{0:T(1024)} %param.37) | copy-start | bytes 12292
  211.3 26.4 %copy-start.1 = (f32[2,12,64,128]{3,2,1,0:T(8,128)}, f32[2,12,64,128]{3,2,1,0:T(8,128)S(1)}, u32[]{:S(2)}) copy-start(f32[2,12,64,128]{3,2,1,0:T(8,128)S(1)} %get-tuple-element.238) | copy-start | bytes 2359300
  244.3 141.8 %all-gather.15.cloned.1.call-start = ((), (), s32[]{:S(2)}) async-start(), calls=%async_computation.13 | async-start | bytes 4456448 | tf_op jit(solution)/shard_map/all_gather | solution.py:156
  246.0 182.2 %all-gather.17.cloned.1.call-start = ((), (), s32[]{:S(2)}) async-start(), calls=%async_computation.14 | async-start | bytes 2228224 | tf_op jit(solution)/shard_map/all_gather | solution.py:157
  246.6 237.1 %all-reduce.37.cloned.1.call-start = ((), (), s32[]{:S(2)}) async-start(), calls=%async_computation.15 | async-start | bytes 3145728 | tf_op jit(solution)/shard_map/psum | solution.py:265
  335.4 254.2 %copy-start.3 = (f32[2,384,1024]{2,1,0:T(8,128)}, f32[2,384,1024]{2,1,0:T(8,128)S(1)}, u32[]{:S(2)}) copy-start(f32[2,384,1024]{2,1,0:T(8,128)S(1)} %get-tuple-element.647) | copy-start | bytes 9437188
  433.3 151.8 %all-reduce.39.cloned.1.call-start = ((), (), s32[]{:S(2)}) async-start(), calls=%async_computation.16 | async-start | bytes 6291456 | tf_op jit(solution)/shard_map/psum | solution.py:305
  499.2 230.1 %reduce-scatter.31.cloned.1.call-start = ((), (), s32[]{:S(2)}) async-start(), calls=%async_computation.27 | async-start | bytes 983040
  612.9 9.3 slice-start
  641.4 9.3 slice-start
  654.1 84.4 %all-gather.21.cloned.1.call-start = ((), (), s32[]{:S(2)}) async-start(), calls=%async_computation.26 | async-start | bytes 3932160 | tf_op jit(solution)/shard_map/all_gather | solution.py:28
  671.2 189.7 %reduce-scatter.17.cloned.1.call-start = ((), (), s32[]{:S(2)}) async-start(), calls=%async_computation.18 | async-start | bytes 1114112 | tf_op jit(solution)/shard_map/reduce_scatter | solution.py:474
  695.8 14.2 copy-start.2
  695.8 14.2 copy-start.22
  695.8 14.2 copy-start.66
  710.1 16.9 %copy-start.58 = (bf16[2,384,4,64]{1,3,2,0:T(8,128)(2,1)}, bf16[2,384,4,64]{1,3,2,0:T(8,128)(2,1)S(1)}, u32[]{:S(2)}) copy-start(bf16[2,384,4,64]{1,3,2,0:T(8,128)(2,1)S(1)} %add_convert_fusion.1) | copy-start | bytes 1179652
  738.5 148.3 %all-reduce.41.cloned.1.call-start = ((), (), s32[]{:S(2)}) async-start(), calls=%async_computation.29 | async-start | bytes 3932160 | tf_op jit(solution)/shard_map/psum | solution.py:442
  748.8 16.5 %copy-start.110 = (f32[2,12]{1,0:T(2,128)}, f32[2,12]{1,0:T(2,128)S(1)}, u32[]{:S(2)}) copy-start(f32[2,12]{1,0:T(2,128)S(1)} %get-tuple-element.680) | copy-start | bytes 292
  768.5 8.7 copy-start.85
  782.6 31.4 %collective-permute-start.2 = (f32[2,3,768]{2,1,0:T(4,128)}, f32[2,3,768]{2,1,0:T(4,128)}, u32[]{:S(2)}, u32[]{:S(2)}) collective-permute-start(f32[2,3,768]{2,1,0:T(4,128)} %pad_add_fusion.2), channel_id=1, source_target_pairs={{2,0},{4,2},{6,4},{3,1},{5,3},{7,5},{10,8},{12,10},{14,12},{11,9},... | collective-permute-start | bytes 55304 | tf_op jit(solution)/shard_map/ppermute | solution.py:21
  790.3 16.4 %copy-start.81 = (u8[384,12]{0,1:T(8,128)(4,1)S(1)}, u8[384,12]{0,1:T(8,128)(4,1)}, u32[]{:S(2)}) copy-start(u8[384,12]{0,1:T(8,128)(4,1)} %copy-done.80) | copy-start | bytes 13828
  790.3 22.0 %collective-permute-start.3 = (f32[2,3,256]{2,1,0:T(4,128)}, f32[2,3,256]{2,1,0:T(4,128)}, u32[]{:S(2)}, u32[]{:S(2)}) collective-permute-start(f32[2,3,256]{2,1,0:T(4,128)} %pad_add_fusion.3), channel_id=1, source_target_pairs={{2,0},{4,2},{6,4},{3,1},{5,3},{7,5},{10,8},{12,10},{14,12},{11,9},... | collective-permute-start | bytes 18440 | tf_op jit(solution)/shard_map/ppermute | solution.py:21
  824.5 122.1 %reduce-scatter.33.cloned.1.call-start = ((), (), s32[]{:S(2)}) async-start(), calls=%async_computation.28 | async-start | bytes 557056
  827.7 227.2 %reduce-scatter.27.cloned.1.call-start = ((), (), s32[]{:S(2)}) async-start(), calls=%async_computation.23 | async-start | bytes 8912896 | tf_op jit(solution)/shard_map/reduce_scatter | solution.py:480
  836.6 307.6 %reduce-scatter.21.cloned.1.call-start = ((), (), s32[]{:S(2)}) async-start(), calls=%async_computation.20 | async-start | bytes 6684672 | tf_op jit(solution)/shard_map/reduce_scatter | solution.py:476
  844.3 360.4 %reduce-scatter.15.cloned.1.call-start = ((), (), s32[]{:S(2)}) async-start(), calls=%async_computation.17 | async-start | bytes 1114112 | tf_op jit(solution)/shard_map/reduce_scatter | solution.py:473
  847.1 418.6 %reduce-scatter.19.cloned.1.call-start = ((), (), s32[]{:S(2)}) async-start(), calls=%async_computation.19 | async-start | bytes 1114112 | tf_op jit(solution)/shard_map/reduce_scatter | solution.py:475
  849.9 491.6 %reduce-scatter.29.cloned.1.call-start = ((), (), s32[]{:S(2)}) async-start(), calls=%async_computation.24 | async-start | bytes 4456448 | tf_op jit(solution)/shard_map/reduce_scatter | solution.py:481
  855.7 555.9 %reduce-scatter.25.cloned.1.call-start = ((), (), s32[]{:S(2)}) async-start(), calls=%async_computation.22 | async-start | bytes 3342336 | tf_op jit(solution)/shard_map/reduce_scatter | solution.py:479
  860.3 612.3 %reduce-scatter.23.cloned.1.call-start = ((), (), s32[]{:S(2)}) async-start(), calls=%async_computation.21 | async-start | bytes 1114112 | tf_op jit(solution)/shard_map/reduce_scatter | solution.py:477
  886.8 61.2 %copy-start.36 = (bf16[2,384,1024]{2,1,0:T(8,128)(2,1)S(1)}, bf16[2,384,1024]{2,1,0:T(8,128)(2,1)}, u32[]{:S(2)}) copy-start(bf16[2,384,1024]{2,1,0:T(8,128)(2,1)} %get-tuple-element.636) | copy-start | bytes 4718596
  889.8 59.8 %copy-start.109 = (f32[1024]{0:T(1024)S(1)}, f32[1024]{0:T(1024)}, u32[]{:S(2)}) copy-start(f32[1024]{0:T(1024)} %get-tuple-element.544) | copy-start | bytes 12292
  889.8 59.9 %copy-start.132 = (f32[256]{0:T(256)S(1)}, f32[256]{0:T(256)}, u32[]{:S(2)}) copy-start(f32[256]{0:T(256)} %get-tuple-element.564) | copy-start | bytes 3076
  889.8 105.0 %copy-start.101 = (f32[2,384]{1,0:T(2,128)S(1)}, f32[2,384]{1,0:T(2,128)}, u32[]{:S(2)}) copy-start(f32[2,384]{1,0:T(2,128)} %copy-done.100) | copy-start | bytes 9220
  (120 other events, 415.3 us)
Sparse Core Ops, SparseCore 0:
  10.9 48.7 all-gather.10
  89.5 32.7 all-gather.18
  124.7 42.0 all-gather.12
  244.4 88.1 all-reduce.34
  335.4 50.5 all-gather.14
  388.3 39.8 all-gather.16
  433.4 50.2 all-reduce.36
  499.3 85.7 all-reduce.38
  654.3 23.2 reduce-scatter.30
  678.9 28.5 all-gather.20
  738.6 57.3 reduce-scatter.16
  824.6 62.1 all-reduce.40
  890.9 55.7 reduce-scatter.32
  951.1 103.7 reduce-scatter.26
  1059.2 84.9 reduce-scatter.20
  1148.2 56.4 reduce-scatter.14
  1209.2 56.4 reduce-scatter.18
  1270.0 71.4 reduce-scatter.28
  1346.4 65.2 reduce-scatter.24
  1416.1 56.4 reduce-scatter.22
where the time goes:
time: 1490 us; the launch traced here: 1480 us
  waiting for transfers between devices  788 us (53%)
  matrix products  230 us (15%)
  blocking collectives  198 us (13%)
  other arithmetic  137 us (9%)
  local copies, waits for them, and re-layouts  98.3 us (7%)
  between operations  20.1 us (1%)
    reduce_scatter x1, waiting for transfers between devices, per_device(): lax.psum_scatter(grad_terms[3], ('dp', 'ctx'), scatter_dimension=0, tiled...  87.1 us
    psum x1, waiting for transfers between devices, per_device(): mixed = lax.psum(mix_part, 'tp')  86 us
    reduce_scatter x1, waiting for transfers between devices, per_device(): lax.psum_scatter(grad_terms[8], ('dp', 'ctx'), scatter_dimension=1, tiled...  75.8 us
    reduce_scatter x1, waiting for transfers between devices, per_device(): lax.psum_scatter(grad_terms[6], ('dp', 'ctx'), scatter_dimension=1, tiled...  70.1 us
    psum x1, waiting for transfers between devices, per_device(): normed_two_grad = lax.psum(normed_two_part, 'tp')  62.7 us
    reduce_scatter x1, waiting for transfers between devices, per_device(): lax.psum_scatter(grad_terms[4], ('dp', 'ctx'), scatter_dimension=0, tiled...  60.9 us
    reduce_scatter x1, waiting for transfers between devices, per_device(): lax.psum_scatter(grad_terms[2], ('dp', 'ctx'), scatter_dimension=1, tiled...  60.9 us
    dot_general x3, matrix products, block_terms(): jnp.einsum('hts,ts,shp->thp', decay, inner, weighted, precision=highest)  60.8 us
  transfers between devices with their start and end apart: 24, of which 14 were waited for; matrix products, arithmetic and copies ran while one was open for 23% of the time, Pallas kernels for 0%

commit v1 on v0

v1 whole, which is shorter than its diff:
```python
import jax
import jax.numpy as jnp
from jax import lax
from jax.sharding import PartitionSpec as P

HEAD_SIZE = 64
MP = 64
NS = 128
KC = 4
CBLK = 128


eps_norm = 1e-05
rope_base = 100000000000.0
highest = lax.Precision.HIGHEST


def passed_along(block, axis, distance):
    devices = range(lax.axis_size(axis))
    route = [(i - distance, i) for i in devices if i - distance in devices]
    return lax.ppermute(block, axis, route)


def prefix_2(part, axis, combine, identity, reverse):
    count = lax.axis_size(axis)
    place = lax.axis_index(axis)
    ahead = count - 1 - place if reverse else place
    gathered = jax.tree.map(lambda a: lax.all_gather(a, axis), part)
    state = jax.tree.map(lambda a, e: jnp.zeros_like(a) + jnp.asarray(e, a.dtype), part, identity)

    def one(turn, state):
        source = count - 1 - turn if reverse else turn
        return combine(
            state, jax.tree.map(lambda a: lax.dynamic_index_in_dim(a, source, 0, False), gathered)
        )

    return lax.fori_loop(0, ahead, one, state)


def rms_norm(values, gain):
    return values * lax.rsqrt(jnp.mean(values * values, -1, keepdims=True) + eps_norm) * gain


def rotary(values, places):
    half = values.shape[-1] // 2
    freqs = rope_base ** (-2.0 * jnp.arange(half, dtype=jnp.float32) / values.shape[-1])
    angles = places.astype(jnp.float32)[..., None] * freqs
    cosine = jnp.cos(angles)[..., None, :]
    sine = jnp.sin(angles)[..., None, :]
    first = values[..., :half]
    second = values[..., half:]
    return jnp.concatenate([first * cosine - second * sine, second * cosine + first * sine], -1)


def causal_conv(pre, prev, taps, bias):
    sequence_length = pre.shape[-2]
    extended = jnp.concatenate([prev, pre], -2)
    total = bias + taps[0] * extended[..., 0:sequence_length, :]
    for offset in range(1, taps.shape[0]):
        total = total + taps[offset] * extended[..., offset : offset + sequence_length, :]
    return jax.nn.silu(total)


def running_sum(terms):
    places = jnp.arange(terms.shape[0], dtype=jnp.int32)
    lower = (places[:, None] >= places[None, :]).astype(jnp.float32)
    return jnp.dot(lower, terms, precision=highest)


def pair_sum(parts):
    if lax.axis_size("tp") != 2:
        return jax.tree.map(lambda a: lax.psum(a, "tp"), parts)
    low = jax.tree.map(lambda a: a.astype(jnp.bfloat16), parts)
    other = jax.tree.map(lambda a: lax.ppermute(a, "tp", [(0, 1), (1, 0)]), low)
    return jax.tree.map(lambda a, b: a.astype(jnp.float32) + b.astype(jnp.float32), low, other)


def block_terms(stream, steps, rate, entry_map, read_map):
    sequence_length = stream.shape[0]
    logs = running_sum(-steps * rate)
    gaps = logs.T[:, :, None] - logs.T[:, None, :]
    places = jnp.arange(sequence_length, dtype=jnp.int32)
    causal = places[:, None] >= places[None, :]
    decay = jnp.where(causal, jnp.exp(jnp.where(causal, gaps, 0.0)), 0.0)
    inner = jnp.dot(read_map, entry_map.T, precision=highest, preferred_element_type=jnp.float32)
    weighted = steps[:, :, None] * stream
    local_out = jnp.einsum("hts,ts,shp->thp", decay, inner, weighted, precision=highest)
    tail = jnp.exp(logs[-1][None, :] - logs)
    local_state = jnp.einsum("sh,shp,sn->hpn", tail, weighted, entry_map, precision=highest)
    return (local_out, local_state, jnp.exp(logs[-1]), logs)


def state_terms(logs, read_map, carried):
    return (
        jnp.einsum("tn,hpn->thp", read_map, carried, precision=highest) * jnp.exp(logs)[:, :, None]
    )


def local_part(stream_act, state_act, step_raw, step_bias, decay_log):
    seq_count, tokens, channels = stream_act.shape
    heads_here = step_raw.shape[-1]
    stream_heads = stream_act.reshape(seq_count, tokens, heads_here, MP)
    steps = jax.nn.softplus(step_raw + step_bias)
    rate = jnp.exp(decay_log)
    local_out, local_state, totals, logs = jax.vmap(block_terms, in_axes=(0, 0, None, 0, 0))(
        stream_heads, steps, rate, state_act[..., :NS], state_act[..., NS:]
    )
    return (local_out, local_state, totals)


def finish(
    gate_z, stream_act, state_act, step_raw, step_bias, decay_log, skip_scale, local_out, carried
):
    seq_count, tokens, channels = stream_act.shape
    heads_here = step_raw.shape[-1]
    stream_heads = stream_act.reshape(seq_count, tokens, heads_here, MP)
    steps = jax.nn.softplus(step_raw + step_bias)
    logs = jax.vmap(running_sum)(-steps * jnp.exp(decay_log))
    incoming = jax.vmap(state_terms)(logs, state_act[..., NS:], carried)
    mixer_out = local_out + incoming
    gated = (mixer_out + skip_scale[:, None] * stream_heads) * jax.nn.silu(
        gate_z.reshape(seq_count, tokens, heads_here, MP)
    )
    return gated.reshape(seq_count, tokens, channels)


def chain(earlier, later):
    return (earlier[0] * later[0], later[0][..., None, None] * earlier[1] + later[1])


def swiglu(pair):
    return jax.nn.silu(pair[:, :, 0]) * pair[:, :, 1]


def per_device(
    hidden_in,
    positions,
    valid_mask,
    teacher,
    cotangent,
    mixer_gain,
    query_weight,
    keyvalue_projection_weight,
    attnout_weight,
    stream_weight,
    state_weight,
    step_weight,
    conv_stream,
    bias_stream,
    conv_state,
    bias_state,
    step_bias,
    decay_log,
    skip_scale,
    mambaout_weight,
    ffn_gain,
    gateup_weight,
    down_weight,
):
    low, f32 = jnp.bfloat16, jnp.float32
    seq_count, tokens, width = hidden_in.shape
    owners = ("dp", "ctx")
    rows = query_weight.shape[0]
    q_cols = query_weight.shape[1]
    kv_cols = keyvalue_projection_weight.shape[2]
    channels = stream_weight.shape[2]
    bc_cols = state_weight.shape[1]
    heads = step_weight.shape[1]
    hidden_units = gateup_weight.shape[2]
    step_cols = 128

    tallies = jnp.sum(valid_mask.reshape(seq_count * tokens // CBLK, CBLK), -1).astype(low)
    spare = jnp.zeros((rows, step_cols - heads), low)
    spare = spare.at[0, : tallies.shape[0]].set(tallies)
    mixer_shard = jnp.concatenate(
        [
            stream_weight.reshape(rows, 2 * channels),
            state_weight,
            query_weight,
            keyvalue_projection_weight.reshape(rows, 2 * kv_cols),
            step_weight,
            spare,
        ],
        1,
    )
    mixer_full = lax.all_gather(mixer_shard, owners, axis=0, tiled=True)
    out_shard = jnp.concatenate([attnout_weight.T, mambaout_weight.T], 1)
    ffn_shard = jnp.concatenate([gateup_weight.reshape(rows, 2 * hidden_units), out_shard], 1)
    ffn_full = lax.all_gather(ffn_shard, owners, axis=0, tiled=True)
    gateup_full = ffn_full[:, : 2 * hidden_units]
    out_full_w = ffn_full[:, 2 * hidden_units :]
    down_full = lax.all_gather(down_weight.T, owners, axis=0, tiled=True)

    edges = [0]
    for size in (channels, channels, bc_cols, q_cols, kv_cols, kv_cols, heads):
        edges.append(edges[-1] + size)
    all_cols = mixer_full.shape[1]

    counts = mixer_full.reshape(-1, rows, all_cols)[:, 0, edges[7] : edges[7] + tallies.shape[0]]
    valid_total = jnp.sum(counts.astype(f32))
    ctx_index = lax.axis_index("ctx")
    rim = KC - 1
    hidden = hidden_in.astype(f32)
    normed = rms_norm(hidden, mixer_gain).astype(low)
    query_heads = q_cols // HEAD_SIZE
    kv_heads = kv_cols // HEAD_SIZE
    group = query_heads // kv_heads
    pre = jnp.einsum("std,dc->stc", normed, mixer_full, preferred_element_type=f32)
    gate_z, stream_pre, state_pre, query_pre, key_pre, value_projected, step_raw = (
        pre[..., edges[i] : edges[i + 1]] for i in range(7)
    )
    query_pre = query_pre.reshape(seq_count, tokens, query_heads, HEAD_SIZE)
    key_before_rotation = key_pre.reshape(seq_count, tokens, kv_heads, HEAD_SIZE)
    queries = rotary(query_pre, positions).astype(low)
    keys_mine = (
        rotary(key_before_rotation, positions)
        .astype(low)
        .reshape(seq_count, tokens, kv_heads * HEAD_SIZE)
    )
    keyval_send = jnp.concatenate([keys_mine, value_projected.astype(low)], -1)
    tails = passed_along((stream_pre[:, tokens - rim :], state_pre[:, tokens - rim :]), "ctx", 1)
    keyval_all = lax.all_gather(keyval_send, "ctx", axis=1, tiled=True)
    all_tokens = keyval_all.shape[1]
    key_all = keyval_all[..., : kv_heads * HEAD_SIZE].reshape(
        seq_count, all_tokens, kv_heads, HEAD_SIZE
    )
    value_all = keyval_all[..., kv_heads * HEAD_SIZE :].reshape(
        seq_count, all_tokens, kv_heads, HEAD_SIZE
    )
    stream_act = causal_conv(stream_pre, tails[0], conv_stream, bias_stream)
    state_act = causal_conv(state_pre, tails[1], conv_state, bias_state)
    local_out, local_state, totals = local_part(
        stream_act, state_act, step_raw, step_bias, decay_log
    )
    identity = (jnp.ones_like(totals), jnp.zeros_like(local_state))
    prefix = prefix_2((totals, local_state), "ctx", chain, identity, False)
    carried = prefix[1]
    gated = finish(
        gate_z,
        stream_act,
        state_act,
        step_raw,
        step_bias,
        decay_log,
        skip_scale,
        local_out,
        carried,
    )
    gated_low = gated.astype(low)
    scale = HEAD_SIZE ** (-0.5)
    query_index = ctx_index * tokens + jnp.arange(tokens, dtype=jnp.int32)
    allowed = jnp.arange(all_tokens, dtype=jnp.int32)[None, :] <= query_index[:, None]
    query_groups = queries.reshape(seq_count, tokens, kv_heads, group, HEAD_SIZE)

    def seq_scores(query_seq, key_seq):
        scores = (
            jnp.einsum("qkgd,jkd->kgqj", query_seq, key_seq, preferred_element_type=jnp.float32)
            * scale
        )
        return jnp.where(allowed, scores, -1e30)

    def attend(pieces):
        query_seq, key_seq, value_seq = pieces
        scores = seq_scores(query_seq, key_seq)
        top_score = jnp.max(scores, -1, keepdims=True)
        expo = jnp.exp(scores - top_score)
        denom = jnp.sum(expo, -1, keepdims=True)
        probs = (expo / denom).astype(jnp.bfloat16)
        outputs = jnp.einsum("kgqj,jkd->qkgd", probs, value_seq, preferred_element_type=jnp.float32)
        return (outputs, top_score + jnp.log(denom))

    attended, log_total = lax.map(attend, (query_groups, key_all, value_all))
    attended_low = attended.reshape(seq_count, tokens, q_cols).astype(low)
    mixers = jnp.concatenate([attended_low, gated_low], -1)

    mask_float = valid_mask.astype(f32)[..., None]
    loss_scale = 1.0 / (valid_total * width)
    squares_local = jnp.zeros((), f32)
    seqs = range(seq_count)
    resid, normed_two, gateup, inner, out_full = [], [], [], [], []
    mixed = [
        pair_sum(jnp.einsum("ti,di->td", mixers[s], out_full_w, preferred_element_type=f32))
        for s in seqs
    ]
    for s in seqs:
        resid.append(hidden[s] + mixed[s])
        normed_two.append(rms_norm(resid[s], ffn_gain).astype(low))
        gateup.append(jnp.dot(normed_two[s], gateup_full, preferred_element_type=f32))
        inner.append(
            (jax.nn.silu(gateup[s][:, :hidden_units]) * gateup[s][:, hidden_units:]).astype(low)
        )
    down = [
        pair_sum(jnp.einsum("tf,df->td", inner[s], down_full, preferred_element_type=f32))
        for s in seqs
    ]
    out_grad, down_in, gateup_low = [], [], []

    def swiglu_flat(both):
        return jax.nn.silu(both[:, :hidden_units]) * both[:, hidden_units:]

    for s in seqs:
        out_full.append(resid[s] + down[s])
        diff = out_full[s] - teacher[s].astype(f32)
        squares_local = squares_local + jnp.sum(mask_float[s] * diff * diff)
        out_grad.append(cotangent[s].astype(f32) + mask_float[s] * 2.0 * diff * loss_scale)
        down_in.append(out_grad[s].astype(low))
        inner_grad = jnp.einsum("td,df->tf", down_in[s], down_full, preferred_element_type=f32)
        gateup_low.append(jax.vjp(swiglu_flat, gateup[s])[1](inner_grad)[0].astype(low))
    normed_two_part = [
        jnp.einsum("tc,dc->td", gateup_low[s], gateup_full, preferred_element_type=f32)
        for s in seqs
    ]
    normed_two_grad = [pair_sum(normed_two_part[s]) for s in seqs]
    block_out = jnp.stack(out_full).astype(low)

    def wgrad(left, right):
        return jnp.einsum("td,tc->dc", left, right, preferred_element_type=f32).astype(low)

    join = lambda parts: jnp.concatenate(parts, 0)
    ffn_terms = jnp.concatenate(
        [
            wgrad(join(normed_two), join(gateup_low)),
            wgrad(join(down_in), join(inner)),
        ],
        1,
    )
    ffn_reduced = lax.psum_scatter(ffn_terms, owners, scatter_dimension=0, tiled=True)

    resid_grad, ffn_gain_grad = [], 0.0
    for s in seqs:
        back = jax.vjp(rms_norm, resid[s], ffn_gain)[1](normed_two_grad[s])
        resid_grad.append(out_grad[s] + back[0])
        ffn_gain_grad = ffn_gain_grad + back[1]
    resid_grad = jnp.stack(resid_grad)
    mixed_low = resid_grad.astype(low)
    out_wgrad = wgrad(
        mixed_low.reshape(-1, width), mixers.reshape(-1, q_cols + channels)
    )
    mixers_grad = jnp.einsum("std,di->sti", mixed_low, out_full_w, preferred_element_type=f32)
    attended_grad = (
        mixers_grad[..., :q_cols]
        .astype(low)
        .reshape(seq_count, tokens, kv_heads, group, HEAD_SIZE)
    )
    gated_grad = mixers_grad[..., q_cols:]

    def attend_back(pieces):
        query_seq, key_seq, value_seq, out_grad_seq, log_seq = pieces
        probs_full = jnp.exp(seq_scores(query_seq, key_seq) - log_seq)
        prob_grad = jnp.einsum(
            "qkgd,jkd->kgqj", out_grad_seq, value_seq, preferred_element_type=jnp.float32
        )
        centre = jnp.sum(probs_full * prob_grad, -1, keepdims=True)
        score_grad = (probs_full * (prob_grad - centre)).astype(jnp.bfloat16)
        query_part = (
            jnp.einsum("kgqj,jkd->qkgd", score_grad, key_seq, preferred_element_type=jnp.float32)
            * scale
        )
        key_part = (
            jnp.einsum("kgqj,qkgd->jkd", score_grad, query_seq, preferred_element_type=jnp.float32)
            * scale
        )
        value_part = jnp.einsum(
            "kgqj,qkgd->jkd",
            probs_full.astype(jnp.bfloat16),
            out_grad_seq,
            preferred_element_type=jnp.float32,
        )
        joined = jnp.concatenate(
            [
                key_part.reshape(all_tokens, kv_heads * HEAD_SIZE),
                value_part.reshape(all_tokens, kv_heads * HEAD_SIZE),
            ],
            -1,
        )
        return (query_part, joined)

    query_grad_rot, keyval_grad_all = lax.map(
        attend_back, (query_groups, key_all, value_all, attended_grad, log_total)
    )
    keyval_grad_mine = lax.psum_scatter(
        keyval_grad_all.astype(low), "ctx", scatter_dimension=1, tiled=True
    ).astype(f32)
    _, query_rope_back = jax.vjp(lambda values: rotary(values, positions), query_pre)
    query_in_grad = query_rope_back(
        query_grad_rot.reshape(seq_count, tokens, query_heads, HEAD_SIZE)
    )[0].reshape(seq_count, tokens, q_cols)
    _, key_rope_back = jax.vjp(lambda values: rotary(values, positions), key_before_rotation)
    key_in_grad = key_rope_back(
        keyval_grad_mine[..., :kv_cols].reshape(seq_count, tokens, kv_heads, HEAD_SIZE)
    )[0].reshape(seq_count, tokens, kv_cols)
    value_in_grad = keyval_grad_mine[..., kv_cols:]
    _, finish_back = jax.vjp(
        finish,
        gate_z,
        stream_act,
        state_act,
        step_raw,
        step_bias,
        decay_log,
        skip_scale,
        local_out,
        carried,
    )
    (
        gate_grad,
        stream_grad_one,
        state_grad_one,
        step_grad_one,
        stepbias_one,
        decay_one,
        skip_grad_all,
        local_out_grad,
        carried_grad,
    ) = finish_back(gated_grad)
    after_prefix = prefix_2((totals, carried_grad), "ctx", chain, identity, True)
    later_grad = after_prefix[1]
    totals_grad = jnp.sum(later_grad * carried, (-2, -1))
    _, local_back = jax.vjp(local_part, stream_act, state_act, step_raw, step_bias, decay_log)
    stream_grad_two, state_grad_two, step_grad_two, stepbias_two, decay_two = local_back(
        (local_out_grad, later_grad, totals_grad)
    )
    _, stream_conv_back = jax.vjp(causal_conv, stream_pre, tails[0], conv_stream, bias_stream)
    stream_pre_grad, stream_tail_grad, conv_stream_grad, bias_stream_grad = stream_conv_back(
        stream_grad_one + stream_grad_two
    )
    _, state_conv_back = jax.vjp(causal_conv, state_pre, tails[1], conv_state, bias_state)
    state_pre_grad, state_tail_grad, conv_state_grad, bias_state_grad = state_conv_back(
        state_grad_one + state_grad_two
    )
    back_tails = passed_along((stream_tail_grad, state_tail_grad), "ctx", -1)
    stream_pre_grad = jnp.concatenate(
        [stream_pre_grad[:, : tokens - rim], stream_pre_grad[:, tokens - rim :] + back_tails[0]], 1
    )
    state_pre_grad = jnp.concatenate(
        [state_pre_grad[:, : tokens - rim], state_pre_grad[:, tokens - rim :] + back_tails[1]], 1
    )
    step_grad = step_grad_one + step_grad_two
    pre_grad = jnp.concatenate(
        [
            part.astype(low)
            for part in (
                gate_grad,
                stream_pre_grad,
                state_pre_grad,
                query_in_grad,
                key_in_grad,
                value_in_grad,
                step_grad,
                jnp.zeros((seq_count, tokens, step_cols - heads), f32),
            )
        ],
        -1,
    )
    mixer_terms = jnp.concatenate(
        [
            wgrad(normed.reshape(-1, width), pre_grad.reshape(-1, all_cols)),
            out_wgrad,
        ],
        1,
    )
    mixer_reduced = lax.psum_scatter(mixer_terms, owners, scatter_dimension=0, tiled=True)
    normed_part = jnp.einsum("stc,dc->std", pre_grad, mixer_full, preferred_element_type=f32)
    _, norm_one_back = jax.vjp(rms_norm, hidden, mixer_gain)
    mixer_gain_grad = norm_one_back(normed_part)[1]
    hidden_norm_grad = norm_one_back(
        jnp.stack([pair_sum(normed_part[s]) for s in seqs])
    )[0]
    input_grad = (resid_grad + hidden_norm_grad).astype(low)

    tp_index = lax.axis_index("tp")
    tp_count = lax.axis_size("tp")

    def widen(piece, axis_dim):
        shape_full = list(piece.shape)
        shape_full[axis_dim] = piece.shape[axis_dim] * tp_count
        blank = jnp.zeros(tuple(shape_full), f32)
        return lax.dynamic_update_slice_in_dim(
            blank, piece, tp_index * piece.shape[axis_dim], axis_dim
        )

    def narrow(whole, axis_dim, piece_size):
        return lax.dynamic_slice_in_dim(whole, tp_index * piece_size, piece_size, axis_dim)

    summed = lax.psum(
        (
            mixer_gain_grad,
            ffn_gain_grad / tp_count,
            widen(conv_stream_grad, 1),
            widen(bias_stream_grad, 0),
            conv_state_grad,
            bias_state_grad,
            widen(stepbias_one + stepbias_two, 0),
            widen(decay_one + decay_two, 0),
            widen(skip_grad_all, 0),
            squares_local / tp_count,
        ),
        ("dp", "ctx", "tp"),
    )
    loss = summed[9] * loss_scale
    reduced = mixer_reduced.astype(f32)
    ffn_reduced = ffn_reduced.astype(f32)
    piece = [reduced[:, edges[i] : edges[i + 1]] for i in range(7)]
    state_reduced = pair_sum(piece[2])
    out_reduced = reduced[:, all_cols:]
    return (
        block_out,
        loss,
        input_grad,
        summed[0],
        piece[3],
        jnp.stack([piece[4], piece[5]], 1),
        out_reduced[:, :q_cols].T,
        reduced[:, : 2 * channels].reshape(rows, 2, channels),
        state_reduced,
        piece[6],
        narrow(summed[2], 1, channels),
        narrow(summed[3], 0, channels),
        summed[4],
        summed[5],
        narrow(summed[6], 0, heads),
        narrow(summed[7], 0, heads),
        narrow(summed[8], 0, heads),
        out_reduced[:, q_cols:].T,
        summed[1],
        ffn_reduced[:, : 2 * hidden_units].reshape(rows, 2, hidden_units),
        ffn_reduced[:, 2 * hidden_units :].T,
    )


def solution(mesh):
    return jax.shard_map(
        per_device,
        mesh=mesh,
        in_specs=(
            P("dp", "ctx", None),
            P("dp", "ctx"),
            P("dp", "ctx"),
            P("dp", "ctx", None),
            P("dp", "ctx", None),
            P(),
            P(("dp", "ctx"), "tp"),
            P(("dp", "ctx"), None, "tp"),
            P("tp", ("dp", "ctx")),
            P(("dp", "ctx"), None, "tp"),
            P(("dp", "ctx"), None),
            P(("dp", "ctx"), "tp"),
            P(None, "tp"),
            P("tp"),
            P(),
            P(),
            P("tp"),
            P("tp"),
            P("tp"),
            P("tp", ("dp", "ctx")),
            P(),
            P(("dp", "ctx"), None, "tp"),
            P("tp", ("dp", "ctx")),
        ),
        out_specs=(
            P("dp", "ctx", None),
            P(),
            P("dp", "ctx", None),
            P(),
            P(("dp", "ctx"), "tp"),
            P(("dp", "ctx"), None, "tp"),
            P("tp", ("dp", "ctx")),
            P(("dp", "ctx"), None, "tp"),
            P(("dp", "ctx"), None),
            P(("dp", "ctx"), "tp"),
            P(None, "tp"),
            P("tp"),
            P(),
            P(),
            P("tp"),
            P("tp"),
            P("tp"),
            P("tp", ("dp", "ctx")),
            P(),
            P(("dp", "ctx"), None, "tp"),
            P("tp", ("dp", "ctx")),
        ),
        check_vma=False,
    )
```

time: 1490 us -> 710 us (0.48)
  waiting for transfers between devices: 788 us -> 181 us
  blocking collectives: 198 us -> 61.3 us
  matrix products: 230 us -> 198 us
  local copies, waits for them, and re-layouts: 98.3 us -> 82.9 us
    reduce_scatter x8 -> x3, waiting for transfers between devices: 470 us -> 0.01 us  [the longest x1 0.01 us: per_device(): lax.psum_scatter(keyval_grad_all.astype(low), 'ctx', scatter_dimension=1,...]
    psum x4 -> x0, waiting for transfers between devices: 180 us -> none  [the longest x1 86 us: per_device(): mixed = lax.psum(mix_part, 'tp')]
    ppermute x0 -> x9, waiting for transfers between devices: none -> 114 us  [pair_sum(): other = jax.tree.map(lambda a: lax.ppermute(a, 'tp', [(0, 1), (1, 0)]), low)]
    all_gather x5 -> x0, blocking collectives: 110 us -> none  [the longest x1 25.7 us: per_device(): lax.all_gather(state_weight, ('dp', 'ctx'), axis=0, tiled=True)]
    unnamed x22 -> x8, waiting for transfers between devices: 57.5 us -> 0.64 us
    unnamed x1 -> x0, blocking collectives: 32.1 us -> none
    dot_general x27 -> x20, matrix products: 90.8 us -> 64.8 us  [the longest x4 18.9 us: wgrad(): jnp.einsum('td,tc->dc', left, right, preferred_element_type=f32).astype(low)]
    unnamed x321 -> x379, local copies, waits for them, and re-layouts: 43.2 us -> 22.5 us
  transfers between devices with their start and end apart: 24 -> 21, of which waited for: 14 -> 11; matrix products, arithmetic and copies ran while one was open for 23% -> 40% of each run, Pallas kernels for 0% -> 0%
where the time goes in v1:
time: 710 us; the launch traced here: 700 us
  matrix products  198 us (28%)
  waiting for transfers between devices  181 us (25%)
  other arithmetic  137 us (19%)
  local copies, waits for them, and re-layouts  82.9 us (12%)
  blocking collectives  61.3 us (9%)
  between operations  20.4 us (3%)
  starting transfers between devices  18.9 us (3%)
    ppermute x9, waiting for transfers between devices, pair_sum(): other = jax.tree.map(lambda a: lax.ppermute(a, 'tp', [(0, 1), (1, 0)]), low)  114 us
    dot_general x3, matrix products, block_terms(): jnp.einsum('hts,ts,shp->thp', decay, inner, weighted, precision=highest)  57.2 us
    all_gather x1, waiting for transfers between devices, per_device(): mixer_full = lax.all_gather(mixer_shard, owners, axis=0, tiled=True)  52.5 us
    psum x1, blocking collectives, per_device(): lax.psum((mixer_gain_grad, ffn_gain_grad / tp_count, widen(conv_stream_gr...  41.6 us
    unnamed x379, local copies, waits for them, and re-layouts  22.5 us
    another operation x5, other arithmetic  21.1 us
    dot_general x4, matrix products, wgrad(): jnp.einsum('td,tc->dc', left, right, preferred_element_type=f32).astype(low)  18.9 us
    dot_general x4, matrix products, seq_scores(): jnp.einsum('qkgd,jkd->kgqj', query_seq, key_seq, preferred_element_type=j...  15.1 us
  transfers between devices with their start and end apart: 21, of which 11 were waited for; matrix products, arithmetic and copies ran while one was open for 40% of the time, Pallas kernels for 0%

profile of v1, /device:TPU:0, one launch (start us, length us, event | category | flops | bytes accessed | tf_op | source)
XLA Modules:
  0.0 700.0 jit_solution(15798356557485683711)
XLA Ops:
  15.9 52.5 %all-gather.8.cloned.1.call-done = bf16[1024,2304]{1,0:T(8,128)(2,1)} async-done(((bf16[64,2304]{1,0:T(8,128)(2,1)}), bf16[1024,2304]{1,0:T(8,128)(2,1)}) %all-gather.8.cloned.1.call-update) | async-done | bytes 4718608 | tf_op jit(solution)/shard_map/all_gather | solution.py:186
  68.5 6.2 fusion.86
  74.8 2.9 fusion.298
  83.0 2.6 collective-permute-start
  87.9 3.0 fusion.118
  91.0 3.1 copy.251
  94.0 4.9 fusion.116
  105.3 3.3 copy.253
  108.6 5.9 all_gather.32
  116.4 13.8 %all_gather.31 = bf16[2,1536,128]{2,1,0:T(8,128)(2,1)S(1)} all-gather(bf16[2,384,128]{2,1,0:T(8,128)(2,1)S(1)} %pad_maximum_fusion.11), channel_id=1, replica_groups=mesh['dp'=4,'ctx'=4,'tp'=2] {'ctx'}, dimensions={1}, use_global_device_ids=true | all-gather | bytes 983040 | tf_op jit(solution)/shard_map/all_gather | solution.py:222
  137.7 17.4 %while.59 = (s32[]{:T(128)}, bf16[2,384,1,4,64]{1,4,3,2,0:T(8,128)(2,1)}, f32[2,1,4,384,1]{3,2,4,1,0:T(4,128)S(1)}, bf16[2,1536,1,64]{1,3,2,0:T(8,128)(2,1)}, bf...) while((s32[]{:T(128)}, ...), condition=%wide.region_5.6_spmd.clone.clone, body=%wide.region_2.5_spmd.clone.sunk.clone | while | flops 632879616 | bytes 34852496 | solution.py:272
  141.9 3.8 fusion.366
  150.5 3.8 fusion.366
  161.1 22.7 %multiply_convert_fusion.1 = (bf16[2,384,12,64]{1,3,2,0:T(8,128)(2,1)}, f32[2,384,12,64]{1,3,2,0:T(8,128)}) fusion(f32[2,384,12,64]{1,3,2,0:T(8,128)} %bitcast.558, f32[2,384,12,64]{1,3,2,0:T(8,128)S(1)} %bitcast.555, f32[12]{0:T(128)S(1)} %copy-done.183, f32[2,384,12,64]{1,3,2,0:T(8,128)S(1)} %fusion.234, f32[2,384,12]{1,2,0:T(8,128)} %get-tuple-element.709, ...), kind=kOutput, calls=%fused_computation.169 | convolution fusion | flops 2738552832 | bytes 12054576 | tf_op jit(solution)/shard_map/vmap(hts,ts,shp->thp)/dot_general | solution.py:87
  183.7 13.3 %all-gather.10.cloned.1.call-done = bf16[1024,3072]{1,0:T(8,128)(2,1)} async-done(((bf16[64,3072]{1,0:T(8,128)(2,1)}), bf16[1024,3072]{1,0:T(8,128)(2,1)}) %all-gather.10.cloned.1.call-update) | async-done | bytes 6291472 | tf_op jit(solution)/shard_map/all_gather | solution.py:189
  197.0 2.9 fusion.173
  204.7 15.7 %collective-permute-done.2 = bf16[384,1024]{1,0:T(8,128)(2,1)S(1)} collective-permute-done((bf16[384,1024]{1,0:T(8,128)(2,1)S(1)}, bf16[384,1024]{1,0:T(8,128)(2,1)S(1)}, u32[]{:S(2)}, u32[]{:S(2)}) %collective-permute-start.2) | collective-permute-done | bytes 786464 | tf_op jit(solution)/shard_map/ppermute | solution.py:74
  220.4 16.2 %collective-permute-done.4 = bf16[384,1024]{1,0:T(8,128)(2,1)S(1)} collective-permute-done((bf16[384,1024]{1,0:T(8,128)(2,1)S(1)}, bf16[384,1024]{1,0:T(8,128)(2,1)S(1)}, u32[]{:S(2)}, u32[]{:S(2)}) %collective-permute-start.4) | collective-permute-done | bytes 786464 | tf_op jit(solution)/shard_map/ppermute | solution.py:74
  243.4 3.8 convolution_convert_fusion.3
  248.7 4.0 fusion.97
  261.3 6.7 collective-permute-done.3
  268.0 15.4 %collective-permute-done.5 = bf16[384,1024]{1,0:T(8,128)(2,1)} collective-permute-done((bf16[384,1024]{1,0:T(8,128)(2,1)}, bf16[384,1024]{1,0:T(8,128)(2,1)}, u32[]{:S(2)}, u32[]{:S(2)}) %collective-permute-start.5) | collective-permute-done | bytes 786464 | tf_op jit(solution)/shard_map/ppermute | solution.py:74
  283.4 4.4 fusion.221
  290.0 2.7 fusion.170
  295.9 2.7 fusion.167
  299.2 14.3 %collective-permute-done.7 = bf16[384,1024]{1,0:T(8,128)(2,1)} collective-permute-done((bf16[384,1024]{1,0:T(8,128)(2,1)}, bf16[384,1024]{1,0:T(8,128)(2,1)}, u32[]{:S(2)}, u32[]{:S(2)}) %collective-permute-start.7) | collective-permute-done | bytes 786464 | tf_op jit(solution)/shard_map/ppermute | solution.py:74
  313.6 14.5 %collective-permute-done.6 = bf16[384,1024]{1,0:T(8,128)(2,1)} collective-permute-done((bf16[384,1024]{1,0:T(8,128)(2,1)}, bf16[384,1024]{1,0:T(8,128)(2,1)}, u32[]{:S(2)}, u32[]{:S(2)}) %collective-permute-start.6) | collective-permute-done | bytes 786464 | tf_op jit(solution)/shard_map/ppermute | solution.py:74
  328.0 5.1 multiply_reduce_fusion.11
  333.2 3.8 fusion.151
  336.9 4.3 fusion.147
  341.3 4.0 fusion.123
  347.2 60.4 %while.60 = (s32[]{:T(128)}, f32[2,384,1,4,64]{1,4,3,2,0:T(8,128)}, bf16[2,1536,128]{2,1,0:T(8,128)(2,1)}, bf16[2,1536,1,64]{1,3,2,0:T(8,128)(2,1)S(1)}, bf16[2,...) while((s32[]{:T(128)}, f32[2,384,1,4,64]{1,4,3,2,0:T(8,128)}, ...), condition=%wide.region_20.22_spmd.clone.clone, body=%wide.region_18.21_spmd.clone.sunk.clone | while | flops 1532852736 | bytes 141003568 | solution.py:378
  350.2 5.9 fusion.376
  356.1 9.6 %fusion.377 = bf16[4,384,1536]{1,2,0:T(8,128)(2,1)} fusion(f32[1,4,384,1536]{2,3,1,0:T(8,128)} %get-tuple-element.956, f32[1536,384,4]{1,0,2:T(8,128)} %copy-done, f32[4,384]{1,0:T(4,128)S(1)} %get-tuple-element.957), kind=kLoop, calls=%fused_computation.36.clone.1.clone | loop fusion | flops 7077888 | bytes 23599104 | tf_op jit(solution)/shard_map/reshape.39
  365.7 3.4 fusion.378
  369.1 5.5 fusion.379
  380.3 5.9 fusion.376
  386.2 9.6 %fusion.377 = bf16[4,384,1536]{1,2,0:T(8,128)(2,1)} fusion(f32[1,4,384,1536]{2,3,1,0:T(8,128)} %get-tuple-element.956, f32[1536,384,4]{1,0,2:T(8,128)} %copy-done, f32[4,384]{1,0:T(4,128)S(1)} %get-tuple-element.957), kind=kLoop, calls=%fused_computation.36.clone.1.clone | loop fusion | flops 7077888 | bytes 23599104 | tf_op jit(solution)/shard_map/reshape.39
  395.8 3.4 fusion.378
  399.2 5.5 fusion.379
  411.2 7.3 %multiply_reduce_fusion.10 = (f32[2,384,12]{1,2,0:T(8,128)}, f32[2,384,12,64]{1,3,2,0:T(8,128)S(1)}, bf16[2,384,12,64]{1,3,2,0:T(8,128)(2,1)}) fusion(f32[2,384,12,64]{1,3,2,0:T(8,128)} %copy-done.31, f32[2,384,12,64]{1,3,2,0:T(8,128)} %bitcast.560, f32[2,384,12,64]{1,3,2,0:T(8,128)} %bitcast.559, f32[2,384,12,64]{1,3,2,0:T(8,128)} %get-tuple-element.720), kind=kLoop, calls=%fused_computation.165 | loop fusion | flops 8838144 | bytes 13012992 | tf_op jit(solution)/shard_map/transpose(jvp(vmap()))/reduce_sum | solution.py:95
  418.5 3.2 fusion.121
  423.3 3.8 convolution_convert_fusion.1
  427.2 3.8 convolution_convert_fusion
  431.0 3.2 pad_maximum_fusion.1
  435.1 19.2 %fusion.62 = (f32[2,384,384]{2,1,0:T(8,128)S(1)}, f32[2,12,384,384]{3,2,1,0:T(8,128)}) fusion(f32[2,12,384]{2,1,0:T(8,128)S(1)} %bitcast.570, pred[384,384]{1,0:T(8,128)(4,1)S(1)} %copy-done.72, f32[2,384,12,64]{1,3,2,0:T(8,128)} %bitcast.553, f32[2,384,12]{1,2,0:T(8,128)S(1)} %copy-done.92, f32[2,384,12,64]{1,3,2,0:T(8,128)S(1)} %get-tuple-element.642), kind=kOutput, calls=%fused_computation.75 | convolution fusion | flops 2735898624 | bytes 20275200 | tf_op jit(solution)/shard_map/transpose(jvp(vmap(hts,ts,shp->thp)))/dot_general | solution.py:87
  454.3 2.9 fusion.247
  459.1 4.6 fusion.179
  463.8 3.3 bitcast_convert_fusion.1
  471.0 12.0 %fusion.73 = (f32[2,12,384]{2,1,0:T(8,128)S(1)}, f32[2,12,384]{2,1,0:T(8,128)S(1)}) fusion(f32[2,12,384,384]{3,2,1,0:T(8,128)} %get-tuple-element.722, f32[2,384,384]{2,1,0:T(8,128)S(1)} %copy-done.47, f32[2,12,384]{2,1,0:T(8,128)} %bitcast.569, pred[384,384]{1,0:T(8,128)(4,1)} %iota_compare_fusion.2), kind=kLoop, calls=%fused_computation.86 | loop fusion | flops 28293120 | bytes 15593472 | tf_op jit(solution)/shard_map/transpose(jvp(vmap()))/reduce_sum | solution.py:81
  490.3 6.1 while.58
  498.5 15.4 %multiply_reduce_fusion.3 = (f32[2,384,12]{1,2,0:T(8,128)}, f32[2,384,12]{1,2,0:T(8,128)}, f32[2,384,12,64]{1,3,2,0:T(8,128)}) fusion(f32[2,384,12,64]{1,3,2,0:T(8,128)S(1)} %fusion.236, f32[2,384,12,64]{1,3,2,0:T(8,128)} %bitcast.554, f32[2,384,12]{1,2,0:T(8,128)S(1)} %copy-done.93, f32[2,384,384]{2,1,0:T(8,128)S(1)} %copy-done.48, ...), kind=kOutput, calls=%fused_computation.158 | convolution fusion | flops 2736764928 | bytes 10948608 | tf_op jit(solution)/shard_map/transpose(jvp(vmap(hts,ts,shp->thp)))/dot_general | solution.py:87
  513.9 3.1 copy.260
  517.0 9.1 %multiply_reduce_fusion.4 = (f32[768]{0:T(1024)S(1)}, f32[768]{0:T(1024)S(1)}, f32[768]{0:T(1024)}, f32[768]{0:T(1024)}, f32[768]{0:T(1024)}, /*index=5*/f32[768]{0:T(1024)}, f32[2,384,768]{2,1,0:T(8,128)S(1)}) fusion(f32[2,384,2304]{2,1,0:T(8,128)} %copy-done.14, f32[2,384,1024]{2,1,0:T(8,128)} %copy-done.32, f32[2,384,768]{2,1,0:T(8,128)} %get-tuple-element.652, ...), kind=kLoop, calls=%fused_computation.159 | loop fusion | flops 18279936 | bytes 16555008 | tf_op jit(solution)/shard_map/transpose(jvp())/reduce_sum | solution.py:121
  532.7 3.9 fusion.185
  548.4 2.7 pad_add_fusion
  559.2 6.3 concatenate.92
  565.5 8.0 %bitcast_convert_fusion = bf16[1024,2304]{1,0:T(8,128)(2,1)} fusion(bf16[2,384,2304]{2,1,0:T(8,128)(2,1)} %concatenate.92, bf16[2,384,1024]{2,1,0:T(8,128)(2,1)S(1)} %copy-done.13, f32[1024]{0:T(1024)S(1)} %copy-done.150, f32[2,384]{1,0:T(2,128)S(1)} %copy-done.134), kind=kOutput, calls=%fused_computation.84 | convolution fusion | flops 3629383680 | bytes 9837568 | tf_op jit(solution)/shard_map/td,tc->dc/dot_general | solution.py:317
  573.5 5.7 pad_maximum_fusion
  580.6 8.9 %fusion.301 = (bf16[2,384,1024]{2,1,0:T(8,128)(2,1)S(1)}, f32[2,384,1024]{2,1,0:T(8,128)}) fusion(bf16[2,384,2304]{2,1,0:T(8,128)(2,1)} %concatenate.92, bf16[1024,2304]{1,0:T(8,128)(2,1)} %all-gather.8.cloned.1.call-done), kind=kOutput, calls=%fused_computation.459 | convolution fusion | flops 3624665088 | bytes 12976128 | tf_op jit(solution)/shard_map/stc,dc->std/dot_general | solution.py:463
  595.2 15.5 %collective-permute-done.10 = bf16[384,1024]{1,0:T(8,128)(2,1)S(1)} collective-permute-done((bf16[384,1024]{1,0:T(8,128)(2,1)}, bf16[384,1024]{1,0:T(8,128)(2,1)S(1)}, u32[]{:S(2)}, u32[]{:S(2)}) %collective-permute-start.10) | collective-permute-done | bytes 786464 | tf_op jit(solution)/shard_map/ppermute | solution.py:74
  611.5 16.1 %collective-permute-done.11 = bf16[384,1024]{1,0:T(8,128)(2,1)} collective-permute-done((bf16[384,1024]{1,0:T(8,128)(2,1)S(1)}, bf16[384,1024]{1,0:T(8,128)(2,1)}, u32[]{:S(2)}, u32[]{:S(2)}) %collective-permute-start.11) | collective-permute-done | bytes 786464 | tf_op jit(solution)/shard_map/ppermute | solution.py:74
  631.2 41.6 %all-reduce.30 = (f32[]{:T(128)}, f32[1024]{0:T(1024)}, f32[4,1536]{1,0:T(4,128)S(1)}, f32[1536]{0:T(1024)S(1)}, f32[4,256]{1,0:T(4,128)}, /*index=5*/f32[256]{0...) all-reduce(f32[]{:T(128)S(6)} %div.111, ...), channel_id=1, replica_groups=mesh['dp'=4,'ctx'=4,'tp'=2] {'dp','ctx','tp'}, use_global_device_ids=true, to_apply=%region_12.13 | all-reduce | flops 11081 | bytes 88648 | tf_op jit(solution)/shard_map/psum | solution.py:485
  676.5 3.7 fusion.89
  (635 shorter events, 165.0 us)
Async XLA Ops:
  7.2 61.3 %copy-start.12 = (bf16[2,384,1024]{2,1,0:T(8,128)(2,1)S(1)}, bf16[2,384,1024]{2,1,0:T(8,128)(2,1)}, u32[]{:S(2)}) copy-start(bf16[2,384,1024]{2,1,0:T(8,128)(2,1)} %param.34) | copy-start | bytes 4718596
  7.2 61.3 %copy-start.149 = (f32[1024]{0:T(1024)S(1)}, f32[1024]{0:T(1024)}, u32[]{:S(2)}) copy-start(f32[1024]{0:T(1024)} %param.39) | copy-start | bytes 12292
  7.2 61.3 %all-gather.8.cloned.1.call-start = ((), (), s32[]{:S(2)}) async-start(), calls=%async_computation.3 | async-start | bytes 5013504 | tf_op jit(solution)/shard_map/all_gather | solution.py:186
  12.4 144.8 %all-gather.14.cloned.1.call-start = ((), (), s32[]{:S(2)}) async-start(), calls=%async_computation.9 | async-start | bytes 3932160 | tf_op jit(solution)/shard_map/all_gather | solution.py:28
  13.1 68.6 %copy-start.176 = (f32[12]{0:T(128)}, f32[12]{0:T(128)S(1)}, u32[]{:S(2)}) copy-start(f32[12]{0:T(128)S(1)} %exp.96) | copy-start | bytes 148
  14.0 73.8 %copy-start.118 = (f32[768]{0:T(1024)}, f32[768]{0:T(1024)S(1)}, u32[]{:S(2)}) copy-start(f32[768]{0:T(1024)S(1)} %get-tuple-element.567) | copy-start | bytes 9220
  14.0 73.8 %copy-start.120 = (f32[768]{0:T(1024)}, f32[768]{0:T(1024)S(1)}, u32[]{:S(2)}) copy-start(f32[768]{0:T(1024)S(1)} %get-tuple-element.568) | copy-start | bytes 9220
  14.0 73.8 %copy-start.122 = (f32[768]{0:T(1024)}, f32[768]{0:T(1024)S(1)}, u32[]{:S(2)}) copy-start(f32[768]{0:T(1024)S(1)} %get-tuple-element.569) | copy-start | bytes 9220
  14.0 73.8 %copy-start.124 = (f32[768]{0:T(1024)}, f32[768]{0:T(1024)S(1)}, u32[]{:S(2)}) copy-start(f32[768]{0:T(1024)S(1)} %get-tuple-element.570) | copy-start | bytes 9220
  15.8 58.9 %copy-start.135 = (f32[2,384]{1,0:T(2,128)}, f32[2,384]{1,0:T(2,128)S(1)}, u32[]{:S(2)}) copy-start(f32[2,384]{1,0:T(2,128)S(1)} %multiply_reduce_fusion.2) | copy-start | bytes 9220
  15.9 58.9 %copy-start.133 = (f32[2,384]{1,0:T(2,128)}, f32[2,384]{1,0:T(2,128)S(1)}, u32[]{:S(2)}) copy-start(f32[2,384]{1,0:T(2,128)S(1)} %fusion.276) | copy-start | bytes 9220
  15.9 70.5 %copy-start.156 = (f32[1,256]{1,0:T(1,128)}, f32[1,256]{1,0:T(1,128)S(1)}, u32[]{:S(2)}) copy-start(f32[1,256]{1,0:T(1,128)S(1)} %get-tuple-element.713) | copy-start | bytes 3076
  15.9 70.5 %copy-start.158 = (f32[1,256]{1,0:T(1,128)}, f32[1,256]{1,0:T(1,128)S(1)}, u32[]{:S(2)}) copy-start(f32[1,256]{1,0:T(1,128)S(1)} %get-tuple-element.714) | copy-start | bytes 3076
  15.9 70.5 %copy-start.160 = (f32[1,256]{1,0:T(1,128)}, f32[1,256]{1,0:T(1,128)S(1)}, u32[]{:S(2)}) copy-start(f32[1,256]{1,0:T(1,128)S(1)} %get-tuple-element.715) | copy-start | bytes 3076
  15.9 70.5 %copy-start.162 = (f32[1,256]{1,0:T(1,128)}, f32[1,256]{1,0:T(1,128)S(1)}, u32[]{:S(2)}) copy-start(f32[1,256]{1,0:T(1,128)S(1)} %get-tuple-element.716) | copy-start | bytes 3076
  79.4 11.6 %copy-start.33 = (f32[2,384,256]{2,1,0:T(8,128)}, f32[2,384,256]{2,1,0:T(8,128)S(1)}, u32[]{:S(2)}) copy-start(f32[2,384,256]{2,1,0:T(8,128)S(1)} %get-tuple-element.658) | copy-start | bytes 2359300
  79.4 8.4 %collective-permute-start.1 = (f32[2,3,768]{2,1,0:T(4,128)S(1)}, f32[2,3,768]{2,1,0:T(4,128)S(1)}, u32[]{:S(2)}, u32[]{:S(2)}) collective-permute-start(f32[2,3,768]{2,1,0:T(4,128)S(1)} %slice.361), channel_id=1, source_target_pairs={{0,2},{2,4},{4,6},{1,3},{3,5},{5,7},{8,10},{10,12},{12,14},{9,11},... | collective-permute-start | bytes 55304 | tf_op jit(solution)/shard_map/ppermute | solution.py:21
  83.0 3.4 collective-permute-start
  87.8 69.8 %copy-start.20 = (f32[2,384,256]{2,1,0:T(8,128)}, f32[2,384,256]{2,1,0:T(8,128)S(1)}, u32[]{:S(2)}) copy-start(f32[2,384,256]{2,1,0:T(8,128)S(1)} %get-tuple-element.647) | copy-start | bytes 2359300
  98.9 98.0 %all-gather.10.cloned.1.call-start = ((), (), s32[]{:S(2)}) async-start(), calls=%async_computation.4 | async-start | bytes 6684672 | tf_op jit(solution)/shard_map/all_gather | solution.py:189
  99.9 143.5 %all-gather.12.cloned.1.call-start = ((), (), s32[]{:S(2)}) async-start(), calls=%async_computation.5 | async-start | bytes 2228224 | tf_op jit(solution)/shard_map/all_gather | solution.py:192
  100.5 385.4 %reduce-scatter.4.cloned.1.call-start = ((), (), s32[]{:S(2)}) async-start(), calls=%async_computation.6 | async-start | bytes 983040 | tf_op jit(solution)/shard_map/reduce_scatter | solution.py:381
  102.0 12.4 %copy-start.164 = (f32[32]{0:T(128)}, f32[32]{0:T(128)S(1)}, u32[]{:S(2)}) copy-start(f32[32]{0:T(128)S(1)} %multiply_power_fusion) | copy-start | bytes 388
  102.0 12.4 %copy-start.114 = (f32[2,384]{1,0:T(2,128)}, f32[2,384]{1,0:T(2,128)S(1)}, u32[]{:S(2)}) copy-start(f32[2,384]{1,0:T(2,128)S(1)} %convert_element_type.257) | copy-start | bytes 9220
  157.6 26.2 %copy-start.1 = (f32[2,12,64,128]{3,2,1,0:T(8,128)}, f32[2,12,64,128]{3,2,1,0:T(8,128)S(1)}, u32[]{:S(2)}) copy-start(f32[2,12,64,128]{3,2,1,0:T(8,128)S(1)} %get-tuple-element.250) | copy-start | bytes 2359300
  161.1 35.9 %copy-start.99 = (bf16[2,384,1,4,64]{1,4,3,2,0:T(8,128)(2,1)S(1)}, bf16[2,384,1,4,64]{1,4,3,2,0:T(8,128)(2,1)}, u32[]{:S(2)}) copy-start(bf16[2,384,1,4,64]{1,4,3,2,0:T(8,128)(2,1)} %get-tuple-element.249) | copy-start | bytes 1179652
  199.9 20.4 %collective-permute-start.2 = (bf16[384,1024]{1,0:T(8,128)(2,1)S(1)}, bf16[384,1024]{1,0:T(8,128)(2,1)S(1)}, u32[]{:S(2)}, u32[]{:S(2)}) collective-permute-start(bf16[384,1024]{1,0:T(8,128)(2,1)S(1)} %fusion.173), channel_id=1, source_target_pairs={{0,1},{1,0},{2,3},{3,2},{4,5},{5,4},{6,7},{7,6},{8,9},{9,8},{10,11... | collective-permute-start | bytes 2359304 | tf_op jit(solution)/shard_map/ppermute | solution.py:74
  203.6 33.0 %collective-permute-start.4 = (bf16[384,1024]{1,0:T(8,128)(2,1)S(1)}, bf16[384,1024]{1,0:T(8,128)(2,1)S(1)}, u32[]{:S(2)}, u32[]{:S(2)}) collective-permute-start(bf16[384,1024]{1,0:T(8,128)(2,1)S(1)} %fusion.176), channel_id=1, source_target_pairs={{0,1},{1,0},{2,3},{3,2},{4,5},{5,4},{6,7},{7,6},{8,9},{9,8},{10,11... | collective-permute-start | bytes 2359304 | tf_op jit(solution)/shard_map/ppermute | solution.py:74
  204.6 32.7 %copy-start.111 = (f32[1024]{0:T(1024)S(1)}, f32[1024]{0:T(1024)}, u32[]{:S(2)}) copy-start(f32[1024]{0:T(1024)} %param.54) | copy-start | bytes 12292
  247.2 20.8 %collective-permute-start.3 = (bf16[384,1024]{1,0:T(8,128)(2,1)}, bf16[384,1024]{1,0:T(8,128)(2,1)}, u32[]{:S(2)}, u32[]{:S(2)}) collective-permute-start(bf16[384,1024]{1,0:T(8,128)(2,1)} %convolution_convert_fusion.3), channel_id=1, source_target_pairs={{0,1},{1,0},{2,3},{3,2},{4,5},{5,4},{6,7},{7,6},{8,9},{9,8},{10,11... | collective-permute-start | bytes 2359304 | tf_op jit(solution)/shard_map/ppermute | solution.py:74
  257.4 26.0 %collective-permute-start.5 = (bf16[384,1024]{1,0:T(8,128)(2,1)}, bf16[384,1024]{1,0:T(8,128)(2,1)}, u32[]{:S(2)}, u32[]{:S(2)}) collective-permute-start(bf16[384,1024]{1,0:T(8,128)(2,1)} %convolution_convert_fusion.2), channel_id=1, source_target_pairs={{0,1},{1,0},{2,3},{3,2},{4,5},{5,4},{6,7},{7,6},{8,9},{9,8},{10,11... | collective-permute-start | bytes 2359304 | tf_op jit(solution)/shard_map/ppermute | solution.py:74
  261.3 26.6 %copy-start.57 = (f32[384,2048]{1,0:T(8,128)S(1)}, f32[384,2048]{1,0:T(8,128)}, u32[]{:S(2)}) copy-start(f32[384,2048]{1,0:T(8,128)} %copy-done.56) | copy-start | bytes 9437188
  261.3 26.6 %copy-start.188 = (bf16[1024,1024]{1,0:T(8,128)(2,1)S(1)}, bf16[1024,1024]{1,0:T(8,128)(2,1)}, u32[]{:S(2)}) copy-start(bf16[1024,1024]{1,0:T(8,128)(2,1)} %all-gather.12.cloned.1.call-done) | copy-start | bytes 6291460
  292.8 20.8 %collective-permute-start.7 = (bf16[384,1024]{1,0:T(8,128)(2,1)}, bf16[384,1024]{1,0:T(8,128)(2,1)}, u32[]{:S(2)}, u32[]{:S(2)}) collective-permute-start(bf16[384,1024]{1,0:T(8,128)(2,1)} %fusion.170), channel_id=1, source_target_pairs={{0,1},{1,0},{2,3},{3,2},{4,5},{5,4},{6,7},{7,6},{8,9},{9,8},{10,11... | collective-permute-start | bytes 2359304 | tf_op jit(solution)/shard_map/ppermute | solution.py:74
  298.6 29.4 %collective-permute-start.6 = (bf16[384,1024]{1,0:T(8,128)(2,1)}, bf16[384,1024]{1,0:T(8,128)(2,1)}, u32[]{:S(2)}, u32[]{:S(2)}) collective-permute-start(bf16[384,1024]{1,0:T(8,128)(2,1)} %fusion.167), channel_id=1, source_target_pairs={{0,1},{1,0},{2,3},{3,2},{4,5},{5,4},{6,7},{7,6},{8,9},{9,8},{10,11... | collective-permute-start | bytes 2359304 | tf_op jit(solution)/shard_map/ppermute | solution.py:74
  299.2 33.9 %copy-start.144 = (f32[384]{0:T(512)S(1)}, f32[384]{0:T(512)}, u32[]{:S(2)}) copy-start(f32[384]{0:T(512)} %copy-done.143) | copy-start | bytes 4612
  299.2 33.9 %copy-start.146 = (f32[384]{0:T(512)S(1)}, f32[384]{0:T(512)}, u32[]{:S(2)}) copy-start(f32[384]{0:T(512)} %copy-done.145) | copy-start | bytes 4612
  299.2 33.9 %copy-start.24 = (bf16[2,384,1024]{2,1,0:T(8,128)(2,1)S(1)}, bf16[2,384,1024]{2,1,0:T(8,128)(2,1)}, u32[]{:S(2)}) copy-start(bf16[2,384,1024]{2,1,0:T(8,128)(2,1)} %param.37) | copy-start | bytes 4718596
  299.2 33.9 %copy-start.37 = (bf16[2,384,1024]{2,1,0:T(8,128)(2,1)S(1)}, bf16[2,384,1024]{2,1,0:T(8,128)(2,1)}, u32[]{:S(2)}) copy-start(bf16[2,384,1024]{2,1,0:T(8,128)(2,1)} %param.38) | copy-start | bytes 4718596
  299.2 33.9 %copy-start.112 = (f32[1024]{0:T(1024)S(1)}, f32[1024]{0:T(1024)}, u32[]{:S(2)}) copy-start(f32[1024]{0:T(1024)} %param.54) | copy-start | bytes 12292
  299.2 33.9 %copy-start.132 = (f32[384]{0:T(512)S(1)}, f32[384]{0:T(512)}, u32[]{:S(2)}) copy-start(f32[384]{0:T(512)} %copy-done.131) | copy-start | bytes 4612
  299.2 33.9 %copy-start.142 = (f32[384]{0:T(512)S(1)}, f32[384]{0:T(512)}, u32[]{:S(2)}) copy-start(f32[384]{0:T(512)} %broadcast_multiply_fusion.9) | copy-start | bytes 4612
  356.1 9.6 %copy-start.86 = (f32[2,384,1,4,64]{1,4,3,2,0:T(8,128)S(1)}, f32[2,384,1,4,64]{1,4,3,2,0:T(8,128)}, u32[]{:S(2)}) copy-start(f32[2,384,1,4,64]{1,4,3,2,0:T(8,128)} %get-tuple-element.1029) | copy-start | bytes 2359300 | tf_op jit(solution)/shard_map/while
  386.2 9.6 %copy-start.86 = (f32[2,384,1,4,64]{1,4,3,2,0:T(8,128)S(1)}, f32[2,384,1,4,64]{1,4,3,2,0:T(8,128)}, u32[]{:S(2)}) copy-start(f32[2,384,1,4,64]{1,4,3,2,0:T(8,128)} %get-tuple-element.1029) | copy-start | bytes 2359300 | tf_op jit(solution)/shard_map/while
  407.6 82.6 %all-gather.16.cloned.1.call-start = ((), (), s32[]{:S(2)}) async-start(), calls=%async_computation.10 | async-start | bytes 3932160 | tf_op jit(solution)/shard_map/all_gather | solution.py:28
  418.5 40.7 %copy-start.15 = (f32[2,384,12,64]{1,3,2,0:T(8,128)}, f32[2,384,12,64]{1,3,2,0:T(8,128)S(1)}, u32[]{:S(2)}) copy-start(f32[2,384,12,64]{1,3,2,0:T(8,128)S(1)} %get-tuple-element.642) | copy-start | bytes 7077892
  421.7 258.4 %reduce-scatter.8.cloned.1.call-start = ((), (), s32[]{:S(2)}) async-start(), calls=%async_computation.8 | async-start | bytes 6684672 | tf_op jit(solution)/shard_map/reduce_scatter | solution.py:327
  434.2 249.0 %reduce-scatter.6.cloned.1.call-start = ((), (), s32[]{:S(2)}) async-start(), calls=%async_computation.7 | async-start | bytes 7241728 | tf_op jit(solution)/shard_map/reduce_scatter | solution.py:462
  435.1 19.2 %copy-start.22 = (f32[2,384,256]{2,1,0:T(8,128)S(1)}, f32[2,384,256]{2,1,0:T(8,128)}, u32[]{:S(2)}) copy-start(f32[2,384,256]{2,1,0:T(8,128)} %copy-done.20) | copy-start | bytes 2359300
  471.0 13.9 %copy-start.78 = (f32[384,2,12]{0,2,1:T(8,128)S(1)}, f32[384,2,12]{0,2,1:T(8,128)}, u32[]{:S(2)}) copy-start(f32[384,2,12]{0,2,1:T(8,128)} %copy-done.76) | copy-start | bytes 110596
  471.0 13.9 %copy-start.113 = (f32[2,384,12]{1,2,0:T(8,128)S(1)}, f32[2,384,12]{1,2,0:T(8,128)}, u32[]{:S(2)}) copy-start(f32[2,384,12]{1,2,0:T(8,128)} %get-tuple-element.641) | copy-start | bytes 110596
  471.0 16.6 %copy-start.115 = (f32[2,384]{1,0:T(2,128)S(1)}, f32[2,384]{1,0:T(2,128)}, u32[]{:S(2)}) copy-start(f32[2,384]{1,0:T(2,128)} %copy-done.114) | copy-start | bytes 9220
  471.0 16.6 %copy-start.165 = (f32[32]{0:T(128)S(1)}, f32[32]{0:T(128)}, u32[]{:S(2)}) copy-start(f32[32]{0:T(128)} %copy-done.164) | copy-start | bytes 388
  517.0 9.1 %copy-start.119 = (f32[768]{0:T(1024)S(1)}, f32[768]{0:T(1024)}, u32[]{:S(2)}) copy-start(f32[768]{0:T(1024)} %copy-done.118) | copy-start | bytes 9220
  517.0 9.1 %copy-start.121 = (f32[768]{0:T(1024)S(1)}, f32[768]{0:T(1024)}, u32[]{:S(2)}) copy-start(f32[768]{0:T(1024)} %copy-done.120) | copy-start | bytes 9220
  517.0 9.1 %copy-start.123 = (f32[768]{0:T(1024)S(1)}, f32[768]{0:T(1024)}, u32[]{:S(2)}) copy-start(f32[768]{0:T(1024)} %copy-done.122) | copy-start | bytes 9220
  517.0 9.1 %copy-start.125 = (f32[768]{0:T(1024)S(1)}, f32[768]{0:T(1024)}, u32[]{:S(2)}) copy-start(f32[768]{0:T(1024)} %copy-done.124) | copy-start | bytes 9220
  531.0 25.0 %collective-permute-start.8 = (f32[2,3,768]{2,1,0:T(4,128)}, f32[2,3,768]{2,1,0:T(4,128)}, u32[]{:S(2)}, u32[]{:S(2)}) collective-permute-start(f32[2,3,768]{2,1,0:T(4,128)} %pad_add_fusion.2), channel_id=1, source_target_pairs={{2,0},{4,2},{6,4},{3,1},{5,3},{7,5},{10,8},{12,10},{14,12},{11,9},... | collective-permute-start | bytes 55304 | tf_op jit(solution)/shard_map/ppermute | solution.py:21
  540.8 13.3 %collective-permute-start.9 = (f32[2,3,256]{2,1,0:T(4,128)}, f32[2,3,256]{2,1,0:T(4,128)}, u32[]{:S(2)}, u32[]{:S(2)}) collective-permute-start(f32[2,3,256]{2,1,0:T(4,128)} %pad_add_fusion.3), channel_id=1, source_target_pairs={{2,0},{4,2},{6,4},{3,1},{5,3},{7,5},{10,8},{12,10},{14,12},{11,9},... | collective-permute-start | bytes 18440 | tf_op jit(solution)/shard_map/ppermute | solution.py:21
  590.6 20.0 %collective-permute-start.10 = (bf16[384,1024]{1,0:T(8,128)(2,1)}, bf16[384,1024]{1,0:T(8,128)(2,1)S(1)}, u32[]{:S(2)}, u32[]{:S(2)}) collective-permute-start(bf16[384,1024]{1,0:T(8,128)(2,1)} %get-tuple-element.681), channel_id=1, source_target_pairs={{0,1},{1,0},{2,3},{3,2},{4,5},{5,4},{6,7},{7,6},{8,9},{9,8},{10,11... | collective-permute-start | bytes 2359304 | tf_op jit(solution)/shard_map/ppermute | solution.py:74
  592.2 35.4 %collective-permute-start.11 = (bf16[384,1024]{1,0:T(8,128)(2,1)S(1)}, bf16[384,1024]{1,0:T(8,128)(2,1)}, u32[]{:S(2)}, u32[]{:S(2)}) collective-permute-start(bf16[384,1024]{1,0:T(8,128)(2,1)S(1)} %get-tuple-element.682), channel_id=1, source_target_pairs={{0,1},{1,0},{2,3},{3,2},{4,5},{5,4},{6,7},{7,6},{8,9},{9,8},{10,11... | collective-permute-start | bytes 2359304 | tf_op jit(solution)/shard_map/ppermute | solution.py:74
  595.2 34.8 %copy-start.50 = (f32[2,384,1024]{2,1,0:T(8,128)S(1)}, f32[2,384,1024]{2,1,0:T(8,128)}, u32[]{:S(2)}) copy-start(f32[2,384,1024]{2,1,0:T(8,128)} %get-tuple-element.724) | copy-start | bytes 9437188
  630.0 46.4 %copy-start.136 = (f32[2,384]{1,0:T(2,128)S(1)}, f32[2,384]{1,0:T(2,128)}, u32[]{:S(2)}) copy-start(f32[2,384]{1,0:T(2,128)} %copy-done.135) | copy-start | bytes 9220
  686.5 4.6 collective-permute-start.12
  (161 other events, 602.2 us)
Sparse Core Ops, SparseCore 0:
  12.5 55.9 all-gather.7
  99.1 33.1 all-gather.13
  135.1 61.8 all-gather.9
  199.0 40.0 all-gather.11
  407.7 21.8 reduce-scatter.3
  431.1 28.5 all-gather.15
  464.1 85.1 reduce-scatter.7
  579.3 90.0 reduce-scatter.5

commit v2 on v1

v2 whole, which is shorter than its diff:
```python
import functools

import jax
import jax.numpy as jnp
from jax import lax
from jax.experimental import pallas as pl
from jax.experimental.pallas import tpu as pltpu
from jax.sharding import PartitionSpec as P

HEAD_SIZE = 64
MP = 64
NS = 128
KC = 4
CBLK = 128
VMEM_BYTES = 56 * 1024 * 1024

low = jnp.bfloat16
f32 = jnp.float32
highest = lax.Precision.HIGHEST
NEG = -1e30
eps_norm = 1e-05
rope_base = 100000000000.0


def vmem_params():
    return pltpu.CompilerParams(
        dimension_semantics=("arbitrary",), vmem_limit_bytes=VMEM_BYTES
    )


def mm(left, right):
    return jnp.dot(left, right, preferred_element_type=f32)


def mm_nt(left, right):
    return lax.dot_general(left, right, (((1,), (1,)), ((), ())), preferred_element_type=f32)


def mm_tn(left, right):
    return lax.dot_general(left, right, (((0,), (0,)), ((), ())), preferred_element_type=f32)


def iota(shape, axis):
    return lax.broadcasted_iota(jnp.int32, shape, axis)


def sigmoid(v):
    return 1.0 / (1.0 + jnp.exp(-v))


def softplus(v):
    return jnp.maximum(v, 0.0) + jnp.log1p(jnp.exp(-jnp.abs(v)))


def silu_grad(v, sig):
    return sig * (1.0 + v * (1.0 - sig))


def halves(v):
    high = v.astype(low)
    return high, (v - high.astype(f32)).astype(low)


def head_map(channels):
    shape = (128, channels)
    return jnp.where(iota(shape, 1) // MP == iota(shape, 0), 1.0, 0.0).astype(low)


def expand(per_head, spread):
    high, rest = halves(per_head)
    return mm(high, spread) + mm(rest, spread)


def collect(per_channel, spread):
    high, rest = halves(per_channel)
    return mm_nt(high, spread) + mm_nt(rest, spread)


def rotate(u, cosine, sine):
    first = (iota(u.shape, 1) // 32) % 2 == 0
    return u * cosine + jnp.where(first, pltpu.roll(u, 96, 1), pltpu.roll(u, 32, 1)) * sine


def prep_body(q_ref, kv_ref, cos_ref, sin_ref, q_out, kv_out):
    cosine, sine = cos_ref[...], sin_ref[...]
    scale = HEAD_SIZE ** (-0.5)
    for j in range(q_ref.shape[1] // 128):
        cols = slice(128 * j, 128 * j + 128)
        q_out[:, cols] = rotate(q_ref[:, cols], cosine, sine).astype(low) * jnp.asarray(scale, low)
    kv = kv_ref[...]
    keep = iota(kv.shape, 1) < HEAD_SIZE
    kv_out[...] = jnp.where(keep, rotate(kv, cosine, sine), kv).astype(low)


def attend_body(at_ref, q_ref, *refs, hops):
    kv_refs, (o_ref, lse_ref) = refs[:hops], refs[hops:]
    at = at_ref[0]
    tokens = q_ref.shape[0]
    lane = iota((tokens, 128), 1)
    lo = lane < HEAD_SIZE
    causal = iota((tokens, tokens), 0) >= iota((tokens, tokens), 1)
    lse_all = jnp.zeros((tokens, 128), f32)
    for j in range(q_ref.shape[1] // 128):
        pair = q_ref[:, 128 * j : 128 * j + 128].astype(f32)
        sides = []
        for side in range(2):
            query = pair if side == 0 else pltpu.roll(pair, HEAD_SIZE, 1)
            query = jnp.where(lo, query, 0.0).astype(low)
            scores = []
            for d in range(hops):
                score = mm_nt(query, kv_refs[d][...])
                scores.append(
                    jnp.where(causal if d == 0 else at >= d, score, NEG)
                )
            top = functools.reduce(
                jnp.maximum, [jnp.max(s, -1, keepdims=True) for s in scores]
            )
            total, mixed = 0.0, 0.0
            for d in range(hops):
                expo = jnp.exp(scores[d] - top)
                total = total + jnp.sum(expo, -1, keepdims=True)
                mixed = mixed + mm(expo.astype(low), kv_refs[d][...])
            sides.append(mixed * (1.0 / total))
            lse_all = jnp.where(lane == 2 * j + side, top + jnp.log(total), lse_all)
        o_ref[:, 128 * j : 128 * j + 128] = jnp.where(
            lo, pltpu.roll(sides[0], HEAD_SIZE, 1), sides[1]
        ).astype(low)
    lse_ref[...] = lse_all


def attend_back_body(at_ref, q_ref, go_ref, o_ref, lse_ref, cos_ref, sin_ref, *refs, hops):
    kv_refs, (gq_ref,), gkv_refs = refs[:hops], refs[hops : hops + 1], refs[hops + 1 :]
    at = at_ref[0]
    tokens = q_ref.shape[0]
    lane = iota((tokens, 128), 1)
    lo = lane < HEAD_SIZE
    causal = iota((tokens, tokens), 0) >= iota((tokens, tokens), 1)
    cosine, sine = cos_ref[...], sin_ref[...]
    lse_all = lse_ref[...]
    scale = HEAD_SIZE ** (-0.5)
    gkv = [jnp.zeros((tokens, 128), f32) for _ in range(hops)]
    for j in range(q_ref.shape[1] // 128):
        cols = slice(128 * j, 128 * j + 128)
        pair = q_ref[:, cols].astype(f32)
        go_pair = go_ref[:, cols].astype(low).astype(f32)
        weighed = go_pair * o_ref[:, cols].astype(f32)
        sides = []
        for side in range(2):
            query = pair if side == 0 else pltpu.roll(pair, HEAD_SIZE, 1)
            query = jnp.where(lo, query, 0.0).astype(low)
            grad = pltpu.roll(go_pair, HEAD_SIZE, 1) if side == 0 else go_pair
            grad = jnp.where(lo, 0.0, grad).astype(low)
            centre = jnp.sum(jnp.where(lo == (side == 0), weighed, 0.0), -1, keepdims=True)
            lse = jnp.sum(jnp.where(lane == 2 * j + side, lse_all, 0.0), -1, keepdims=True)
            gq = 0.0
            for d in range(hops):
                kv = kv_refs[d][...]
                score = mm_nt(query, kv)
                prob = jnp.exp(jnp.where(causal if d == 0 else at >= d, score, NEG) - lse)
                gprob = mm_nt(grad, kv)
                gscore = (prob * (gprob - centre)).astype(low)
                gq = gq + mm(gscore, kv)
                gkv[d] = gkv[d] + mm_tn(gscore, query) + mm_tn(prob.astype(low), grad)
            sides.append(gq * scale)
        joined = jnp.where(lo, sides[0], pltpu.roll(sides[1], HEAD_SIZE, 1))
        gq_ref[:, cols] = rotate(joined, cosine, -sine).astype(low)
    for d in range(hops):
        gkv_refs[d][...] = gkv[d].astype(low)


def keyval_sum_body(cos_ref, sin_ref, *refs):
    parts, (out_ref,) = refs[:-1], refs[-1:]
    total = parts[0][...].astype(f32)
    for part in parts[1:]:
        total = total + part[...].astype(f32)
    keep = iota(total.shape, 1) < HEAD_SIZE
    rotated = rotate(total, cos_ref[...], -sin_ref[...])
    out_ref[...] = jnp.where(keep, rotated, total).astype(low)


def decay_pair(logs, logs_t, first, keep):
    both = []
    for head in (first, first + 1):
        gap = logs[:, head : head + 1] - logs_t[head : head + 1, :]
        both.append(jnp.exp(jnp.where(keep, gap, NEG)))
    return both


def step_terms(step_ref, rows, heads_ref, heads):
    raw = step_ref[rows, :] + heads_ref[0:1, :]
    live = iota(raw.shape, 1) < heads
    steps = jnp.where(live, softplus(raw), 0.0)
    return jnp.where(live, raw, 0.0), steps


def lower_triangle(size):
    return iota((size, size), 0) >= iota((size, size), 1)


def scan_body(
    x_ref, bc_ref, step_ref, xt_ref, bct_ref, taps_ref, taps_bc_ref, heads_ref,
    v_ref, vbc_ref, y_ref, logs_ref, states_ref, send_ref,
    xe, bce, *, heads,
):
    tokens, channels = x_ref.shape
    xe[0:8, :] = xt_ref[...]
    xe[8:, :] = x_ref[...]
    bce[0:8, :] = bct_ref[...]
    bce[8:, :] = bc_ref[...]
    spread = head_map(channels)
    keep = lower_triangle(CBLK)
    triangle = jnp.where(keep, 1.0, 0.0)
    lo = iota((CBLK, 128), 1) < MP
    rate = heads_ref[1:2, :]
    state = None
    carry = jnp.zeros((1, 128), f32)
    total_decay = None
    for c in range(tokens // CBLK):
        rows = slice(CBLK * c, CBLK * c + CBLK)

        def conv(ext, taps):
            start = CBLK * c + 8 - (KC - 1)
            total = taps[KC : KC + 1, :] + taps[0:1, :] * ext[start : start + CBLK, :]
            for k in range(1, KC):
                total = total + taps[k : k + 1, :] * ext[start + k : start + k + CBLK, :]
            return total

        v = conv(xe, taps_ref)
        v_ref[rows, :] = v
        xs = v * sigmoid(v)
        vbc = conv(bce, taps_bc_ref)
        vbc_ref[rows, :] = vbc
        bc = (vbc * sigmoid(vbc)).astype(low)
        entry, read = bc[:, :NS], bc[:, NS:]
        _, steps = step_terms(step_ref, rows, heads_ref, heads)
        logs = jnp.dot(triangle, -steps * rate, precision=highest, preferred_element_type=f32)
        logs_t = logs.T
        total = logs[CBLK - 1 : CBLK, :]
        logs_ref[rows, :] = logs + carry
        carry = carry + total
        decays = expand(jnp.exp(logs), spread)
        steps_wide = expand(steps, spread)
        tails_wide = expand(jnp.exp(total - logs) * steps, spread)
        weighted = (xs * steps_wide).astype(low)
        inner = mm_nt(read, entry)
        if state is not None:
            incoming = decays * mm(read, state.astype(low))
        for j in range(channels // 128):
            cols = slice(128 * j, 128 * j + 128)
            left, right = decay_pair(logs, logs_t, 2 * j, keep)
            stacked = jnp.concatenate([(inner * left).astype(low), (inner * right).astype(low)], 0)
            result = mm(stacked, weighted[:, cols])
            out = jnp.where(lo, result[:CBLK], result[CBLK:])
            if state is not None:
                out = out + incoming[:, cols]
            y_ref[rows, cols] = out
        added = mm_tn(entry, (xs * tails_wide).astype(low))
        last = decays[CBLK - 1 : CBLK, :]
        state = added if state is None else last * state + added
        total_decay = last if total_decay is None else total_decay * last
        states_ref[NS * c : NS * c + NS, :] = state
    send_ref[0:NS, :] = state.astype(low)
    send_ref[NS:, :] = jnp.broadcast_to(total_decay, (send_ref.shape[0] - NS, channels)).astype(low)


def chained(refs):
    state = None
    for ref in reversed(refs):
        own = ref[0:NS, :].astype(f32)
        if state is None:
            state = own
        else:
            state = own + ref[NS : NS + 1, :].astype(f32) * state
    return state


def gate_body(z_ref, y_ref, v_ref, vbc_ref, logs_ref, heads_ref, *refs):
    earlier, (gated_ref, y_out, carried_ref) = refs[:-3], refs[-3:]
    tokens, channels = y_ref.shape
    spread = head_map(channels)
    skip = expand(heads_ref[...], spread)[2:3, :]
    carried = chained(earlier) if earlier else jnp.zeros((NS, channels), f32)
    carried_ref[...] = carried
    carried_low = carried.astype(low)
    for c in range(tokens // CBLK):
        rows = slice(CBLK * c, CBLK * c + CBLK)
        vc = vbc_ref[rows, NS:]
        read = (vc * sigmoid(vc)).astype(low)
        y = y_ref[rows, :] + expand(jnp.exp(logs_ref[rows, :]), spread) * mm(read, carried_low)
        y_out[rows, :] = y
        v = v_ref[rows, :]
        z = z_ref[rows, :]
        gated_ref[rows, :] = ((y + skip * (v * sigmoid(v))) * (z * sigmoid(z))).astype(low)


def gate_back_body(
    g_ref, z_ref, y_ref, v_ref, vbc_ref, logs_ref, heads_ref, sent_ref,
    dy_ref, dz_ref, send_ref, dskip_ref,
):
    tokens, channels = y_ref.shape
    spread = head_map(channels)
    skip = expand(heads_ref[...], spread)[2:3, :]
    state, dskip = 0.0, 0.0
    for c in range(tokens // CBLK):
        rows = slice(CBLK * c, CBLK * c + CBLK)
        vc = vbc_ref[rows, NS:]
        read = (vc * sigmoid(vc)).astype(low)
        v = v_ref[rows, :]
        xs = v * sigmoid(v)
        z = z_ref[rows, :]
        sig = sigmoid(z)
        grad = g_ref[rows, :].astype(f32)
        dy = grad * (z * sig)
        dz_ref[rows, :] = (grad * (y_ref[rows, :] + skip * xs) * silu_grad(z, sig)).astype(low)
        dy_ref[rows, :] = dy
        dskip = dskip + jnp.sum(dy * xs, 0, keepdims=True)
        faded = (dy * expand(jnp.exp(logs_ref[rows, :]), spread)).astype(low)
        state = state + mm_tn(read, faded)
    send_ref[0:NS, :] = state.astype(low)
    send_ref[NS:, :] = sent_ref[NS:, :]
    dskip_ref[...] = jnp.broadcast_to(dskip, dskip_ref.shape)


def scan_back_body(
    dy_ref, y_ref, v_ref, vbc_ref, x_ref, bc_ref, step_ref, xt_ref, bct_ref,
    taps_ref, taps_bc_ref, heads_ref, logs_ref, states_ref, carried_ref, *refs, heads,
):
    later, refs = refs[:-10], refs[-10:]
    dx_ref, dbc_ref, dstep_ref, edge_ref, head_ref, gx_ref, gbc_ref, gh_ref, dve, dbce = refs
    tokens, channels = y_ref.shape
    chunks = tokens // CBLK
    spread = head_map(channels)
    keep = lower_triangle(CBLK)
    triangle = jnp.where(keep, 1.0, 0.0)
    lo = iota((CBLK, 128), 1) < MP
    rate = heads_ref[1:2, :]
    skip = expand(heads_ref[...], spread)[2:3, :]
    dstate = chained(later) if later else jnp.zeros((NS, channels), f32)
    dve[0:8, :] = jnp.zeros((8, channels), f32)
    dve[8 + tokens :, :] = jnp.zeros((8, channels), f32)
    dbce[0:8, :] = jnp.zeros((8, 2 * NS), f32)
    dbce[8 + tokens :, :] = jnp.zeros((8, 2 * NS), f32)
    dbias, ddecay = 0.0, 0.0
    for c in reversed(range(chunks)):
        rows = slice(CBLK * c, CBLK * c + CBLK)
        v = v_ref[rows, :]
        sig = sigmoid(v)
        xs = v * sig
        vbc = vbc_ref[rows, :]
        sig_bc = sigmoid(vbc)
        bc = (vbc * sig_bc).astype(low)
        entry, read = bc[:, :NS], bc[:, NS:]
        raw, steps = step_terms(step_ref, rows, heads_ref, heads)
        logs = jnp.dot(triangle, -steps * rate, precision=highest, preferred_element_type=f32)
        logs_t = logs.T
        total = logs[CBLK - 1 : CBLK, :]
        decays = expand(jnp.exp(logs), spread)
        steps_wide = expand(steps, spread)
        tails_wide = expand(jnp.exp(total - logs), spread)
        last = decays[CBLK - 1 : CBLK, :]
        if c == 0:
            state = carried_ref[...]
        else:
            before = expand(jnp.exp(logs_ref[CBLK * c - 8 : CBLK * c, :]), spread)[7:8, :]
            state = states_ref[NS * (c - 1) : NS * c, :] + before * carried_ref[...]
        dy = dy_ref[rows, :]
        dy_low = dy.astype(low)
        w = xs * steps_wide
        w_low = w.astype(low)
        inner = mm_nt(read, entry)
        state_low = state.astype(low)
        dstate_low = dstate.astype(low)
        dw_later = tails_wide * mm(entry, dstate_low)
        faded = (dy * decays).astype(low)
        dread = mm_nt(faded, state_low)
        dentry = mm_nt((w * tails_wide).astype(low), dstate_low)
        dinner = 0.0
        pieces = []
        for j in range(channels // 128):
            cols = slice(128 * j, 128 * j + 128)
            left, right = decay_pair(logs, logs_t, 2 * j, keep)
            dy_pair, w_pair = dy_low[:, cols], w_low[:, cols]
            weights = jnp.concatenate([(inner * left).astype(low), (inner * right).astype(low)], 1)
            result = mm_tn(weights, dy_pair)
            pieces.append(jnp.where(lo, result[:CBLK], result[CBLK:]) + dw_later[:, cols])
            zero = jnp.zeros_like(dy_pair)
            parted = jnp.concatenate([jnp.where(lo, dy_pair, zero), jnp.where(lo, zero, dy_pair)], 0)
            dweights = mm_nt(parted, w_pair)
            dinner = dinner + dweights[:CBLK] * left + dweights[CBLK:] * right
        dw = jnp.concatenate(pieces, 1)
        dinner_low = dinner.astype(low)
        dread = dread + mm(dinner_low, entry)
        dentry = dentry + mm_tn(dinner_low, read)
        dlogs = collect(dy * y_ref[rows, :] - w * dw, spread)
        dtotal = jnp.sum(w * dw_later, 0, keepdims=True) + last * jnp.sum(
            dstate * state, 0, keepdims=True
        )
        dtotal = collect(jnp.broadcast_to(dtotal, (8, channels)), spread)[0:1, :]
        dfall = (
            lax.dot_general(
                triangle, dlogs, (((0,), (0,)), ((), ())),
                precision=highest, preferred_element_type=f32,
            )
            + dtotal
        )
        dsteps = collect(xs * dw, spread) - rate * dfall
        ddecay = ddecay - rate * jnp.sum(steps * dfall, 0, keepdims=True)
        live = iota(raw.shape, 1) < heads
        draw = jnp.where(live, dsteps * sigmoid(raw), 0.0)
        dbias = dbias + jnp.sum(draw, 0, keepdims=True)
        dstep_ref[rows, :] = draw.astype(low)
        dve[8 + CBLK * c : 8 + CBLK * c + CBLK, :] = (steps_wide * dw + skip * dy) * silu_grad(v, sig)
        dbce[8 + CBLK * c : 8 + CBLK * c + CBLK, :] = jnp.concatenate(
            [dentry, dread], 1
        ) * silu_grad(vbc, sig_bc)
        dstate = last * dstate + mm_tn(read, faded)
    gh_ref[0:1, :] = dbias
    gh_ref[1:2, :] = ddecay
    gh_ref[2:, :] = jnp.zeros((gh_ref.shape[0] - 2, 128), f32)

    def conv_back(ext, taps, out_ref, cols, grads_ref, pre_ref, tail_ref):
        def spread_rows(start, count):
            total = taps[0:1, :] * ext[start + KC - 1 : start + KC - 1 + count, :]
            for k in range(1, KC):
                at = start + KC - 1 - k
                total = total + taps[k : k + 1, :] * ext[at : at + count, :]
            return total

        head_ref[:, cols] = spread_rows(0, 8)
        grads = [0.0] * (KC + 1)
        for c in range(chunks):
            at = CBLK * c
            dpre = spread_rows(8 + at, CBLK)
            out_ref[at : at + CBLK, :] = dpre.astype(low)
            if c == chunks - 1:
                edge_ref[:, cols] = dpre[CBLK - 8 :, :]
        for k in range(KC):
            shift = KC - 1 - k
            main = jnp.sum(pre_ref[...] * ext[8 + shift : 8 + shift + tokens, :], 0, keepdims=True)
            edge = jnp.sum(tail_ref[...] * ext[shift : shift + 8, :], 0, keepdims=True)
            grads[k] = main + edge
        grads[KC] = jnp.sum(ext[8 : 8 + tokens, :], 0, keepdims=True)
        for k in range(KC + 1):
            grads_ref[k : k + 1, :] = grads[k]
        grads_ref[KC + 1 :, :] = jnp.zeros((grads_ref.shape[0] - KC - 1, ext.shape[1]), f32)

    conv_back(dve, taps_ref, dx_ref, slice(0, channels), gx_ref, x_ref, xt_ref)
    bc_cols = slice(channels, channels + 2 * NS)
    conv_back(dbce, taps_bc_ref, dbc_ref, bc_cols, gbc_ref, bc_ref, bct_ref)


def block(height, width, col=0):
    return pl.BlockSpec((height, width), lambda s: (s, col))


def whole(shape):
    return pl.BlockSpec(shape, lambda s: (0, 0))


def shaped(rows, cols, dtype):
    return jax.ShapeDtypeStruct((rows, cols), dtype)


def run(body, seqs, inputs, outputs, scratch=(), at=None, flops=0):
    arrays = [a for a, _ in inputs]
    specs = [s for _, s in inputs]
    if at is not None:
        arrays = [at] + arrays
        specs = [pl.BlockSpec(memory_space=pltpu.SMEM)] + specs
    moved = sum(a.size * a.dtype.itemsize for a in arrays)
    return pl.pallas_call(
        body,
        grid=(seqs,),
        in_specs=specs,
        out_specs=[block(r, c) for r, c, _ in outputs],
        out_shape=[shaped(seqs * r, c, d) for r, c, d in outputs],
        scratch_shapes=list(scratch),
        compiler_params=vmem_params(),
        cost_estimate=pl.CostEstimate(flops=flops, bytes_accessed=moved, transcendentals=0),
    )(*arrays)


def prep(pre, cosine, sine, seqs, tokens, q_at, q_cols, kv_at):
    return run(
        prep_body,
        seqs,
        [
            (pre, block(tokens, q_cols, q_at // q_cols)),
            (pre, block(tokens, 128, kv_at // 128)),
            (cosine, block(tokens, 128)),
            (sine, block(tokens, 128)),
        ],
        [(tokens, q_cols, low), (tokens, 128, low)],
    )


def attend(queries, keyvals, at, seqs, tokens):
    hops, cols = len(keyvals), queries.shape[1]
    work = 4 * seqs * tokens * tokens * hops * (cols // HEAD_SIZE) * 256
    return run(
        functools.partial(attend_body, hops=hops),
        seqs,
        [(queries, block(tokens, cols))] + [(kv, block(tokens, 128)) for kv in keyvals],
        [(tokens, cols, low), (tokens, 128, f32)],
        at=at,
        flops=work,
    )


def attend_back(queries, keyvals, grads, grad_at, outs, lse, cosine, sine, at, seqs, tokens):
    hops, cols = len(keyvals), queries.shape[1]
    work = 10 * seqs * tokens * tokens * hops * (cols // HEAD_SIZE) * 256
    return run(
        functools.partial(attend_back_body, hops=hops),
        seqs,
        [
            (queries, block(tokens, cols)),
            (grads, block(tokens, cols, grad_at // cols)),
            (outs, block(tokens, cols)),
            (lse, block(tokens, 128)),
            (cosine, block(tokens, 128)),
            (sine, block(tokens, 128)),
        ]
        + [(kv, block(tokens, 128)) for kv in keyvals],
        [(tokens, cols, low)] + [(tokens, 128, low)] * hops,
        at=at,
        flops=work,
    )


def keyval_sum(parts, cosine, sine, seqs, tokens):
    return run(
        keyval_sum_body,
        seqs,
        [(a, block(tokens, 128)) for a in (cosine, sine, *parts)],
        [(tokens, 128, low)],
    )[0]


SENT = NS + 16


def scan(pre, tails, taps, taps_bc, per_head, seqs, tokens, channels, heads):
    step_at = pre.shape[1] // 128 - 1
    return run(
        functools.partial(scan_body, heads=heads),
        seqs,
        [
            (pre, block(tokens, channels, 1)),
            (pre, block(tokens, 2 * NS, 2 * channels // (2 * NS))),
            (pre, block(tokens, 128, step_at)),
            (tails, block(8, channels)),
            (tails, block(8, 2 * NS, channels // (2 * NS))),
            (taps, whole(taps.shape)),
            (taps_bc, whole(taps_bc.shape)),
            (per_head, whole(per_head.shape)),
        ],
        [
            (tokens, channels, f32),
            (tokens, 2 * NS, f32),
            (tokens, channels, f32),
            (tokens, 128, f32),
            (tokens // CBLK * NS, channels, f32),
            (SENT, channels, low),
        ],
        scratch=[pltpu.VMEM((tokens + 8, channels), f32), pltpu.VMEM((tokens + 8, 2 * NS), f32)],
        flops=8 * seqs * tokens * CBLK * channels,
    )


def gate(pre, y, v, vbc, logs, per_head, earlier, seqs, tokens, channels):
    return run(
        gate_body,
        seqs,
        [
            (pre, block(tokens, channels, 0)),
            (y, block(tokens, channels)),
            (v, block(tokens, channels)),
            (vbc, block(tokens, 2 * NS)),
            (logs, block(tokens, 128)),
            (per_head, whole(per_head.shape)),
        ]
        + [(a, block(SENT, channels)) for a in earlier],
        [(tokens, channels, low), (tokens, channels, f32), (NS, channels, f32)],
        flops=4 * seqs * tokens * CBLK * channels,
    )


def gate_back(grads, pre, y, v, vbc, logs, per_head, sent, seqs, tokens, channels):
    return run(
        gate_back_body,
        seqs,
        [
            (grads, block(tokens, channels, 0)),
            (pre, block(tokens, channels, 0)),
            (y, block(tokens, channels)),
            (v, block(tokens, channels)),
            (vbc, block(tokens, 2 * NS)),
            (logs, block(tokens, 128)),
            (per_head, whole(per_head.shape)),
            (sent, block(SENT, channels)),
        ],
        [
            (tokens, channels, f32),
            (tokens, channels, low),
            (SENT, channels, low),
            (8, channels, f32),
        ],
        flops=4 * seqs * tokens * CBLK * channels,
    )


def scan_back(
    dy, y, v, vbc, pre, tails, taps, taps_bc, per_head, logs, states, carried, later,
    seqs, tokens, channels, heads,
):
    step_at = pre.shape[1] // 128 - 1
    return run(
        functools.partial(scan_back_body, heads=heads),
        seqs,
        [
            (dy, block(tokens, channels)),
            (y, block(tokens, channels)),
            (v, block(tokens, channels)),
            (vbc, block(tokens, 2 * NS)),
            (pre, block(tokens, channels, 1)),
            (pre, block(tokens, 2 * NS, 2 * channels // (2 * NS))),
            (pre, block(tokens, 128, step_at)),
            (tails, block(8, channels)),
            (tails, block(8, 2 * NS, channels // (2 * NS))),
            (taps, whole(taps.shape)),
            (taps_bc, whole(taps_bc.shape)),
            (per_head, whole(per_head.shape)),
            (logs, block(tokens, 128)),
            (states, block(tokens // CBLK * NS, channels)),
            (carried, block(NS, channels)),
        ]
        + [(a, block(SENT, channels)) for a in later],
        [
            (tokens, channels, low),
            (tokens, 2 * NS, low),
            (tokens, 128, low),
            (8, channels + 2 * NS, f32),
            (8, channels + 2 * NS, f32),
            (8, channels, f32),
            (8, 2 * NS, f32),
            (8, 128, f32),
        ],
        scratch=[
            pltpu.VMEM((tokens + 16, channels), f32),
            pltpu.VMEM((tokens + 16, 2 * NS), f32),
        ],
        flops=30 * seqs * tokens * CBLK * channels,
    )


def passed_along(block, axis, distance):
    devices = range(lax.axis_size(axis))
    route = [(i - distance, i) for i in devices if i - distance in devices]
    return lax.ppermute(block, axis, route)


def pair_sum(part):
    if lax.axis_size("tp") != 2:
        return lax.psum(part, "tp")
    mine = part.astype(low)
    other = lax.ppermute(mine, "tp", [(0, 1), (1, 0)])
    return mine.astype(f32) + other.astype(f32)


def rms_norm(values, gain):
    return values * lax.rsqrt(jnp.mean(values * values, -1, keepdims=True) + eps_norm) * gain


def angle_tables(positions):
    half = HEAD_SIZE // 2
    freqs = rope_base ** (-2.0 * jnp.arange(half, dtype=f32) / HEAD_SIZE)
    angles = positions.reshape(-1, 1).astype(f32) * freqs
    cosine, sine = jnp.cos(angles), jnp.sin(angles)
    return jnp.tile(cosine, (1, 4)), jnp.concatenate([-sine, sine, -sine, sine], 1)


def per_device(
    hidden_in,
    positions,
    valid_mask,
    teacher,
    cotangent,
    mixer_gain,
    query_weight,
    keyvalue_projection_weight,
    attnout_weight,
    stream_weight,
    state_weight,
    step_weight,
    conv_stream,
    bias_stream,
    conv_state,
    bias_state,
    step_bias,
    decay_log,
    skip_scale,
    mambaout_weight,
    ffn_gain,
    gateup_weight,
    down_weight,
):
    seqs, tokens, width = hidden_in.shape
    owners = ("dp", "ctx")
    rows = query_weight.shape[0]
    q_cols = query_weight.shape[1]
    kv_cols = keyvalue_projection_weight.shape[2]
    channels = stream_weight.shape[2]
    bc_cols = state_weight.shape[1]
    heads = step_weight.shape[1]
    hidden_units = gateup_weight.shape[2]
    step_cols = 128
    hops = lax.axis_size("ctx")

    tallies = jnp.sum(valid_mask.reshape(seqs * tokens // CBLK, CBLK), -1).astype(low)
    spare = jnp.zeros((rows, step_cols - heads), low)
    spare = spare.at[0, : tallies.shape[0]].set(tallies)
    mixer_shard = jnp.concatenate(
        [
            stream_weight.reshape(rows, 2 * channels),
            state_weight,
            query_weight,
            keyvalue_projection_weight.reshape(rows, 2 * kv_cols),
            step_weight,
            spare,
        ],
        1,
    )
    mixer_full = lax.all_gather(mixer_shard, owners, axis=0, tiled=True)
    ffn_shard = jnp.concatenate(
        [
            gateup_weight.reshape(rows, 2 * hidden_units),
            down_weight.T,
            mambaout_weight.T,
            attnout_weight.T,
        ],
        1,
    )
    ffn_full = lax.all_gather(ffn_shard, owners, axis=0, tiled=True)
    gateup_full = ffn_full[:, : 2 * hidden_units]
    down_full = ffn_full[:, 2 * hidden_units : 3 * hidden_units]
    out_full_w = ffn_full[:, 3 * hidden_units :]

    edges = [0]
    for size in (channels, channels, bc_cols, q_cols, kv_cols, kv_cols, heads):
        edges.append(edges[-1] + size)
    all_cols = mixer_full.shape[1]
    counts = mixer_full.reshape(-1, rows, all_cols)[:, 0, edges[7] : edges[7] + tallies.shape[0]]
    valid_total = jnp.sum(counts.astype(f32))

    at = lax.axis_index("ctx").astype(jnp.int32).reshape(1)
    cosine, sine = angle_tables(positions)

    def taps_of(taps, bias):
        spare_rows = jnp.zeros((8 - KC - 1, taps.shape[1]), f32)
        return jnp.concatenate([taps, bias[None], spare_rows], 0)

    taps, taps_bc = taps_of(conv_stream, bias_stream), taps_of(conv_state, bias_state)
    per_head = jnp.pad(
        jnp.stack([step_bias, jnp.exp(decay_log), skip_scale]), ((0, 5), (0, 128 - heads))
    )

    hidden = hidden_in.astype(f32)
    normed = rms_norm(hidden, mixer_gain).astype(low).reshape(seqs * tokens, width)
    pre = jnp.dot(normed, mixer_full, preferred_element_type=f32)

    def last_rows(array):
        return array.reshape(seqs, tokens, -1)[:, tokens - 8 :].reshape(seqs * 8, -1)

    tails = passed_along(last_rows(pre[:, channels : edges[3]]), "ctx", 1)
    queries, keyval = prep(pre, cosine, sine, seqs, tokens, edges[3], q_cols, edges[4])
    keyvals = [keyval] + [passed_along(keyval, "ctx", d) for d in range(1, hops)]
    v, vbc, y_own, logs, states, sent = scan(
        pre, tails, taps, taps_bc, per_head, seqs, tokens, channels, heads
    )
    earlier = [passed_along(sent, "ctx", d) for d in range(1, hops)]
    attended, lse = attend(queries, keyvals, at, seqs, tokens)
    gated, y, carried = gate(
        pre, y_own, v, vbc, logs, per_head, earlier, seqs, tokens, channels
    )
    mixers = jnp.concatenate([gated, attended], -1)
    by_seq = lambda array: array.reshape(seqs, tokens, -1)

    mask_float = valid_mask.astype(f32)[..., None]
    loss_scale = 1.0 / (valid_total * width)
    squares_local = jnp.zeros((), f32)
    each = range(seqs)
    resid, normed_two, gateup, inner, out_full = [], [], [], [], []
    mixed = [
        pair_sum(
            jnp.einsum("ti,di->td", by_seq(mixers)[s], out_full_w, preferred_element_type=f32)
        )
        for s in each
    ]
    for s in each:
        resid.append(hidden[s] + mixed[s])
        normed_two.append(rms_norm(resid[s], ffn_gain).astype(low))
        gateup.append(jnp.dot(normed_two[s], gateup_full, preferred_element_type=f32))
        inner.append(
            (jax.nn.silu(gateup[s][:, :hidden_units]) * gateup[s][:, hidden_units:]).astype(low)
        )
    down = [
        pair_sum(jnp.einsum("tf,df->td", inner[s], down_full, preferred_element_type=f32))
        for s in each
    ]
    out_grad, down_in, gateup_low = [], [], []

    def swiglu_flat(both):
        return jax.nn.silu(both[:, :hidden_units]) * both[:, hidden_units:]

    for s in each:
        out_full.append(resid[s] + down[s])
        diff = out_full[s] - teacher[s].astype(f32)
        squares_local = squares_local + jnp.sum(mask_float[s] * diff * diff)
        out_grad.append(cotangent[s].astype(f32) + mask_float[s] * 2.0 * diff * loss_scale)
        down_in.append(out_grad[s].astype(low))
        inner_grad = jnp.einsum("td,df->tf", down_in[s], down_full, preferred_element_type=f32)
        gateup_low.append(jax.vjp(swiglu_flat, gateup[s])[1](inner_grad)[0].astype(low))
    normed_two_part = [
        jnp.einsum("tc,dc->td", gateup_low[s], gateup_full, preferred_element_type=f32)
        for s in each
    ]
    normed_two_grad = [pair_sum(normed_two_part[s]) for s in each]
    block_out = jnp.stack(out_full).astype(low)

    def wgrad(left, right):
        return jnp.einsum("td,tc->dc", left, right, preferred_element_type=f32).astype(low)

    join = lambda parts: jnp.concatenate(parts, 0)
    ffn_terms = jnp.concatenate(
        [
            wgrad(join(normed_two), join(gateup_low)),
            wgrad(join(down_in), join(inner)),
        ],
        1,
    )
    ffn_reduced = lax.psum_scatter(ffn_terms, owners, scatter_dimension=0, tiled=True)

    resid_grad, ffn_gain_grad = [], 0.0
    for s in each:
        back = jax.vjp(rms_norm, resid[s], ffn_gain)[1](normed_two_grad[s])
        resid_grad.append(out_grad[s] + back[0])
        ffn_gain_grad = ffn_gain_grad + back[1]
    resid_grad = jnp.concatenate(resid_grad, 0)
    mixed_low = resid_grad.astype(low)
    out_wgrad = wgrad(mixed_low, mixers)
    mixers_grad = jnp.dot(mixed_low, out_full_w, preferred_element_type=f32)

    dy, dz, sent_back, skip_rows = gate_back(
        mixers_grad, pre, y, v, vbc, logs, per_head, sent, seqs, tokens, channels
    )
    later = [passed_along(sent_back, "ctx", -d) for d in range(1, hops)]
    query_back, *keyval_parts = attend_back(
        queries, keyvals, mixers_grad, channels, attended, lse, cosine, sine, at, seqs, tokens
    )
    keyval_parts = [keyval_parts[0]] + [
        passed_along(keyval_parts[d], "ctx", -d) for d in range(1, hops)
    ]
    dx, dbc, dstep, edge, head, conv_rows, conv_bc_rows, head_rows = scan_back(
        dy, y, v, vbc, pre, tails, taps, taps_bc, per_head, logs, states, carried, later,
        seqs, tokens, channels, heads,
    )
    keyval_back = keyval_sum(keyval_parts, cosine, sine, seqs, tokens)
    mended = (edge + passed_along(head, "ctx", -1)).astype(low)
    pre_grad = jnp.concatenate([dz, dx, dbc, query_back, keyval_back, dstep], -1)
    for s in each:
        pre_grad = lax.dynamic_update_slice(
            pre_grad, mended[8 * s : 8 * s + 8], (tokens * (s + 1) - 8, channels)
        )
    mixer_terms = jnp.concatenate([wgrad(normed, pre_grad), out_wgrad], 1)
    mixer_reduced = lax.psum_scatter(mixer_terms, owners, scatter_dimension=0, tiled=True)
    normed_part = jnp.einsum("tc,dc->td", pre_grad, mixer_full, preferred_element_type=f32)
    hidden_rows = hidden.reshape(seqs * tokens, width)
    _, norm_one_back = jax.vjp(rms_norm, hidden_rows, mixer_gain)
    mixer_gain_grad = norm_one_back(normed_part)[1]
    normed_grad = join([pair_sum(by_seq(normed_part)[s]) for s in each])
    input_grad = (resid_grad + norm_one_back(normed_grad)[0]).astype(low)

    tp_index = lax.axis_index("tp")
    tp_count = lax.axis_size("tp")

    def widen(piece, axis_dim):
        shape_full = list(piece.shape)
        shape_full[axis_dim] = piece.shape[axis_dim] * tp_count
        blank = jnp.zeros(tuple(shape_full), f32)
        return lax.dynamic_update_slice_in_dim(
            blank, piece, tp_index * piece.shape[axis_dim], axis_dim
        )

    def narrow(wide, axis_dim, piece_size):
        return lax.dynamic_slice_in_dim(wide, tp_index * piece_size, piece_size, axis_dim)

    over_seqs = lambda array: jnp.sum(array.reshape(seqs, 8, -1), 0)
    conv_sum, conv_bc_sum, head_sum = map(over_seqs, (conv_rows, conv_bc_rows, head_rows))
    skip_grad = jnp.sum(over_seqs(skip_rows)[0].reshape(heads, MP), -1)
    summed = lax.psum(
        (
            mixer_gain_grad,
            ffn_gain_grad / tp_count,
            widen(conv_sum[: KC + 1], 1),
            conv_bc_sum[: KC + 1],
            widen(jnp.stack([head_sum[0, :heads], head_sum[1, :heads], skip_grad]), 1),
            squares_local / tp_count,
        ),
        ("dp", "ctx", "tp"),
    )
    conv_total = narrow(summed[2], 1, channels)
    head_total = narrow(summed[4], 1, heads)
    loss = summed[5] * loss_scale
    reduced = mixer_reduced.astype(f32)
    ffn_reduced = ffn_reduced.astype(f32)
    piece = [reduced[:, edges[i] : edges[i + 1]] for i in range(7)]
    state_reduced = pair_sum(piece[2])
    out_reduced = reduced[:, all_cols:]
    return (
        block_out,
        loss,
        input_grad.reshape(seqs, tokens, width),
        summed[0],
        piece[3],
        jnp.stack([piece[4], piece[5]], 1),
        out_reduced[:, channels:].T,
        reduced[:, : 2 * channels].reshape(rows, 2, channels),
        state_reduced,
        piece[6],
        conv_total[:KC],
        conv_total[KC],
        summed[3][:KC],
        summed[3][KC],
        head_total[0],
        head_total[1],
        head_total[2],
        out_reduced[:, :channels].T,
        summed[1],
        ffn_reduced[:, : 2 * hidden_units].reshape(rows, 2, hidden_units),
        ffn_reduced[:, 2 * hidden_units :].T,
    )


def solution(mesh):
    return jax.shard_map(
        per_device,
        mesh=mesh,
        in_specs=(
            P("dp", "ctx", None),
            P("dp", "ctx"),
            P("dp", "ctx"),
            P("dp", "ctx", None),
            P("dp", "ctx", None),
            P(),
            P(("dp", "ctx"), "tp"),
            P(("dp", "ctx"), None, "tp"),
            P("tp", ("dp", "ctx")),
            P(("dp", "ctx"), None, "tp"),
            P(("dp", "ctx"), None),
            P(("dp", "ctx"), "tp"),
            P(None, "tp"),
            P("tp"),
            P(),
            P(),
            P("tp"),
            P("tp"),
            P("tp"),
            P("tp", ("dp", "ctx")),
            P(),
            P(("dp", "ctx"), None, "tp"),
            P("tp", ("dp", "ctx")),
        ),
        out_specs=(
            P("dp", "ctx", None),
            P(),
            P("dp", "ctx", None),
            P(),
            P(("dp", "ctx"), "tp"),
            P(("dp", "ctx"), None, "tp"),
            P("tp", ("dp", "ctx")),
            P(("dp", "ctx"), None, "tp"),
            P(("dp", "ctx"), None),
            P(("dp", "ctx"), "tp"),
            P(None, "tp"),
            P("tp"),
            P(),
            P(),
            P("tp"),
            P("tp"),
            P("tp"),
            P("tp", ("dp", "ctx")),
            P(),
            P(("dp", "ctx"), None, "tp"),
            P("tp", ("dp", "ctx")),
        ),
        check_vma=False,
    )
```

time: 710 us -> 555 us (0.78)
  matrix products: 198 us -> 71.5 us
  other arithmetic: 137 us -> 47.7 us
  Pallas kernels: 0 us -> 76.8 us
  local copies, waits for them, and re-layouts: 82.9 us -> 44.3 us
  starting transfers between devices: 18.9 us -> 36.8 us
  blocking collectives: 61.3 us -> 68.8 us
    dot_general x34 -> x5, matrix products: 159 us -> 26.1 us  [the longest x1 7.92 us: per_device(): jnp.einsum('tc,dc->td', pre_grad, mixer_full, preferred_element_type=f32)]
    pallas_call x0 -> x8, Pallas kernels: none -> 76.8 us  [run(): pl.pallas_call(body, grid=(seqs,), in_specs=specs, out_specs=[block(r, c)...]
    ppermute x4 -> x14, waiting for transfers between devices: 0.17 us -> 53.3 us  [passed_along(): return lax.ppermute(block, axis, route)]
    reduce_sum x11 -> x6, other arithmetic: 36.5 us -> 0.25 us  [the longest x1 0.12 us: per_device(): jnp.sum(valid_mask.reshape(seqs * tokens // CBLK, CBLK), -1).astype(low)]
    another operation x8 -> x2, other arithmetic: 31.6 us -> 0.61 us  [the longest x1 0.6 us: per_device(): jnp.stack([step_bias, jnp.exp(decay_log), skip_scale])]
    ppermute x9, waiting for transfers between devices: 114 us -> 83.5 us  [pair_sum(): other = lax.ppermute(mine, 'tp', [(0, 1), (1, 0)])]
    psum x1, blocking collectives: 41.6 us -> 68.8 us  [per_device(): lax.psum((mixer_gain_grad, ffn_gain_grad / tp_count, widen(conv_sum[:KC +...]
    all_gather x2 -> x0, blocking collectives: 19.7 us -> none  [the longest x1 13.8 us: per_device(): keyval_all = lax.all_gather(keyval_send, 'ctx', axis=1, tiled=True)]
  transfers between devices with their start and end apart: 21 -> 27, of which waited for: 11 -> 12; matrix products, arithmetic and copies ran while one was open for 40% -> 19% of each run, Pallas kernels for 0% -> 14%
where the time goes in v2:
time: 555 us; the launch traced here: 550 us
  waiting for transfers between devices  185 us (33%)
  Pallas kernels  76.8 us (14%)
  matrix products  71.5 us (13%)
  blocking collectives  68.8 us (12%)
  other arithmetic  47.7 us (9%)
  local copies, waits for them, and re-layouts  44.3 us (8%)
  starting transfers between devices  36.8 us (7%)
  between operations  19 us (3%)
    ppermute x9, waiting for transfers between devices, pair_sum(): other = lax.ppermute(mine, 'tp', [(0, 1), (1, 0)])  83.5 us
    pallas_call x8, Pallas kernels, run(): pl.pallas_call(body, grid=(seqs,), in_specs=specs, out_specs=[block(r, c)...  76.8 us
    psum x1, blocking collectives, per_device(): lax.psum((mixer_gain_grad, ffn_gain_grad / tp_count, widen(conv_sum[:KC +...  68.8 us
    ppermute x14, waiting for transfers between devices, passed_along(): return lax.ppermute(block, axis, route)  53.3 us
    all_gather x1, waiting for transfers between devices, per_device(): mixer_full = lax.all_gather(mixer_shard, owners, axis=0, tiled=True)  47.8 us
    dot_general x4, matrix products, wgrad(): jnp.einsum('td,tc->dc', left, right, preferred_element_type=f32).astype(low)  26.4 us
    ppermute x14, starting transfers between devices, passed_along(): return lax.ppermute(block, axis, route)  25.7 us
    unnamed x167, local copies, waits for them, and re-layouts  24.7 us
  transfers between devices with their start and end apart: 27, of which 12 were waited for; matrix products, arithmetic and copies ran while one was open for 19% of the time, Pallas kernels for 14%

profile of v2, /device:TPU:0, one launch (start us, length us, event | category | flops | bytes accessed | tf_op | source)
XLA Modules:
  0.0 549.6 jit_solution(14442224484158032754)
XLA Ops:
  10.8 1.6 concatenate.51
  13.5 1.5 fusion.70
  19.2 1.6 multiply_convert_fusion
  20.7 47.8 %all-gather.3.cloned.1.call-done = bf16[1024,2304]{1,0:T(8,128)(2,1)} async-done(((bf16[64,2304]{1,0:T(8,128)(2,1)}), bf16[1024,2304]{1,0:T(8,128)(2,1)}) %all-gather.3.cloned.1.call-update) | async-done | bytes 4718608 | tf_op jit(solution)/shard_map/all_gather | solution.py:734
  68.5 6.6 %fusion.81.x_ref.bc_ref.step_ref.z_ref.q_ref.kv_ref = f32[768,2304]{1,0:T(8,128)S(1)} fusion(bf16[768,1024]{1,0:T(8,128)(2,1)} %bitcast.119, bf16[1024,2304]{1,0:T(8,128)(2,1)} %all-gather.3.cloned.1.call-done), kind=kOutput, calls=%fused_computation.178 | convolution fusion | flops 3623878656 | bytes 13369344 | tf_op jit(solution)/shard_map/dot_general | solution.py:770
  75.1 2.4 slice.217
  77.6 1.4 copy-done
  79.0 2.7 shard_map.384
  81.7 2.2 collective-permute-start.4
  83.9 2.5 collective-permute-start.5
  91.4 10.6 %shard_map.382 = (f32[768,768]{1,0:T(8,128)}, f32[768,256]{1,0:T(8,128)}, f32[768,768]{1,0:T(8,128)}, f32[768,128]{1,0:T(8,128)}, f32[768,768]{1,0:T(8,128)}, /*index=5*/bf16[288,768]{1,0:T(8,128)(2,1)}) custom-call(f32[768,2304]{1,0:T(8,128)} %copy-done, f32[768,2304]{1,0:T(8,128)} %copy-done, f32[768,2304]{1,0:T(8,128)} %copy-done, f32[16,1024]{1,0:T(8,128)} %copy-done.26, ...), custom_call_target="tpu_custom_call" | custom-call | flops 603979776 | bytes 21401600 | tf_op jit(solution)/shard_map/pallas_call | solution.py:471
  102.0 3.2 collective-permute-start.1
  105.2 4.3 collective-permute-start.2
  109.5 1.6 collective-permute-start.3
  111.9 9.9 %shard_map.385 = (bf16[768,256]{1,0:T(8,128)(2,1)}, f32[768,128]{1,0:T(8,128)}) custom-call(s32[1]{0:T(128)} %bitcast.9.at_ref, bf16[768,256]{1,0:T(8,128)(2,1)} %get-tuple-element.69.q_ref, bf16[768,128]{1,0:T(8,128)(2,1)} %get-tuple-element.70.refs_0_, bf16[768,128]{1,0:T(8,128)(2,1)} %copy-done.70, bf16[768,128]{1,0:T(8,128)(2,1)} %copy-done.71, ...), custom_call_target="tpu_custom_call" | custom-call | flops 4831838208 | bytes 1179652 | tf_op jit(solution)/shard_map/pallas_call | solution.py:471
  121.8 8.0 %collective-permute-done.2.refs_1_ = bf16[288,768]{1,0:T(8,128)(2,1)S(1)} collective-permute-done((bf16[288,768]{1,0:T(8,128)(2,1)}, bf16[288,768]{1,0:T(8,128)(2,1)S(1)}, u32[]{:S(2)}, u32[]{:S(2)}) %collective-permute-start.2) | collective-permute-done | bytes 442400 | tf_op jit(solution)/shard_map/ppermute | solution.py:660
  129.8 15.2 %collective-permute-done.3.refs_2_ = bf16[288,768]{1,0:T(8,128)(2,1)S(1)} collective-permute-done((bf16[288,768]{1,0:T(8,128)(2,1)}, bf16[288,768]{1,0:T(8,128)(2,1)S(1)}, u32[]{:S(2)}, u32[]{:S(2)}) %collective-permute-start.3) | collective-permute-done | bytes 442400 | tf_op jit(solution)/shard_map/ppermute | solution.py:660
  145.7 6.0 %shard_map.383 = (bf16[768,768]{1,0:T(8,128)(2,1)}, f32[768,768]{1,0:T(8,128)}, f32[256,768]{1,0:T(8,128)}) custom-call(f32[768,2304]{1,0:T(8,128)} %copy-done, f32[768,768]{1,0:T(8,128)} %get-tuple-element.63.y_ref, f32[768,768]{1,0:T(8,128)} %get-tuple-element.64.v_ref, f32[768,256]{1,0:T(8,128)} %get-tuple-element.65.vbc_ref, ...), custom_call_target="tpu_custom_call" | custom-call | flops 301989888 | bytes 14307328 | tf_op jit(solution)/shard_map/pallas_call | solution.py:471
  151.7 1.5 constant_dynamic-update-slice_fusion.1
  153.3 3.2 fusion.50
  156.5 1.8 collective-permute-start.7
  158.3 2.6 fusion.53
  161.8 15.3 %collective-permute-done.7 = bf16[384,1024]{1,0:T(8,128)(2,1)S(1)} collective-permute-done((bf16[384,1024]{1,0:T(8,128)(2,1)S(1)}, bf16[384,1024]{1,0:T(8,128)(2,1)S(1)}, u32[]{:S(2)}, u32[]{:S(2)}) %collective-permute-start.7) | collective-permute-done | bytes 786464 | tf_op jit(solution)/shard_map/ppermute | solution.py:667
  177.0 15.3 %collective-permute-done.9 = bf16[384,1024]{1,0:T(8,128)(2,1)S(1)} collective-permute-done((bf16[384,1024]{1,0:T(8,128)(2,1)S(1)}, bf16[384,1024]{1,0:T(8,128)(2,1)S(1)}, u32[]{:S(2)}, u32[]{:S(2)}) %collective-permute-start.9) | collective-permute-done | bytes 786464 | tf_op jit(solution)/shard_map/ppermute | solution.py:667
  193.4 1.8 fusion.13
  196.9 1.9 convolution_convert_fusion.5
  198.8 1.7 collective-permute-start.8
  200.5 1.8 fusion.11
  204.1 1.9 convolution_convert_fusion.4
  206.3 1.5 fusion.71
  208.5 11.1 %collective-permute-done.8 = bf16[384,1024]{1,0:T(8,128)(2,1)} collective-permute-done((bf16[384,1024]{1,0:T(8,128)(2,1)}, bf16[384,1024]{1,0:T(8,128)(2,1)}, u32[]{:S(2)}, u32[]{:S(2)}) %collective-permute-start.8) | collective-permute-done | bytes 786464 | tf_op jit(solution)/shard_map/ppermute | solution.py:667
  219.6 14.3 %collective-permute-done.10 = bf16[384,1024]{1,0:T(8,128)(2,1)} collective-permute-done((bf16[384,1024]{1,0:T(8,128)(2,1)}, bf16[384,1024]{1,0:T(8,128)(2,1)}, u32[]{:S(2)}, u32[]{:S(2)}) %collective-permute-start.10) | collective-permute-done | bytes 786464 | tf_op jit(solution)/shard_map/ppermute | solution.py:667
  233.9 5.2 fusion.66
  239.2 11.7 %convolution_convert_fusion.2 = bf16[1024,1024]{1,0:T(8,128)(2,1)S(1)} fusion(bf16[384,1024]{1,0:T(8,128)(2,1)S(1)} %get-tuple-element.208, bf16[384,1024]{1,0:T(8,128)(2,1)S(1)} %get-tuple-element.207, bf16[384,1024]{1,0:T(8,128)(2,1)S(1)} %copy-done.37, bf16[384,1024]{1,0:T(8,128)(2,1)S(1)} %copy-done.35), kind=kOutput, calls=%fused_computation.34 | convolution fusion | flops 1617952768 | bytes 5242880 | tf_op jit(solution)/shard_map/td,tc->dc/dot_general | solution.py:832
  250.9 1.5 fusion.69
  252.6 1.7 copy-done.15
  254.2 1.5 fusion.68
  257.6 3.7 convolution_convert_fusion.1
  261.3 3.2 pad_maximum_fusion.1
  264.6 4.6 fusion.47
  269.2 1.8 collective-permute-start.12
  271.0 4.0 fusion.44
  275.6 14.2 %collective-permute-done.12 = bf16[384,1024]{1,0:T(8,128)(2,1)S(1)} collective-permute-done((bf16[384,1024]{1,0:T(8,128)(2,1)S(1)}, bf16[384,1024]{1,0:T(8,128)(2,1)S(1)}, u32[]{:S(2)}, u32[]{:S(2)}) %collective-permute-start.12) | collective-permute-done | bytes 786464 | tf_op jit(solution)/shard_map/ppermute | solution.py:667
  289.8 13.4 %collective-permute-done.11 = bf16[384,1024]{1,0:T(8,128)(2,1)S(1)} collective-permute-done((bf16[384,1024]{1,0:T(8,128)(2,1)S(1)}, bf16[384,1024]{1,0:T(8,128)(2,1)S(1)}, u32[]{:S(2)}, u32[]{:S(2)}) %collective-permute-start.11) | collective-permute-done | bytes 786464 | tf_op jit(solution)/shard_map/ppermute | solution.py:667
  303.2 4.5 multiply_reduce_fusion.2
  307.7 3.3 fusion.28
  311.0 3.8 fusion.25
  314.8 5.7 %fusion.15.g_ref.go_ref = f32[768,1024]{1,0:T(8,128)} fusion(bf16[1024,4096]{1,0:T(8,128)(2,1)} %all-gather.5.cloned.1.call-done, f32[384,1024]{1,0:T(8,128)S(1)} %get-tuple-element.205, f32[384,1024]{1,0:T(8,128)S(1)} %get-tuple-element.203), kind=kOutput, calls=%fused_computation.36 | convolution fusion | flops 1613758464 | bytes 8388608 | tf_op jit(solution)/shard_map/dot_general | solution.py:852
  320.5 18.9 %shard_map.388 = (bf16[768,256]{1,0:T(8,128)(2,1)}, bf16[768,128]{1,0:T(8,128)(2,1)}, bf16[768,128]{1,0:T(8,128)(2,1)}, bf16[768,128]{1,0:T(8,128)(2,1)}, bf16[768,128]{1,0:T(8,128)(2,1)}) custom-call(s32[1]{0:T(128)} %bitcast.9.at_ref, bf16[768,256]{1,0:T(8,128)(2,1)} %get-tuple-element.69.q_ref, f32[768,1024]{1,0:T(8,128)} %fusion.15.g_ref.go_ref, ...), custom_call_target="tpu_custom_call" | custom-call | flops 12079595520 | bytes 5898244 | tf_op jit(solution)/shard_map/pallas_call | solution.py:471
  340.7 7.6 %shard_map.386 = (f32[768,768]{1,0:T(8,128)}, bf16[768,768]{1,0:T(8,128)(2,1)}, bf16[288,768]{1,0:T(8,128)(2,1)}, f32[16,768]{1,0:T(8,128)}) custom-call(f32[768,1024]{1,0:T(8,128)} %fusion.15.g_ref.go_ref, f32[768,2304]{1,0:T(8,128)} %copy-done, f32[768,768]{1,0:T(8,128)} %get-tuple-element.72.y_ref, f32[768,768]{1,0:T(8,128)} %get-tuple-element.64.v_ref, ...), custom_call_target="tpu_custom_call" | custom-call | flops 301989888 | bytes 16568320 | tf_op jit(solution)/shard_map/pallas_call | solution.py:471
  355.0 3.2 convolution_convert_fusion.3
  359.4 26.5 %collective-permute-done.17.refs_2_ = bf16[768,128]{1,0:T(8,128)(2,1)S(1)} collective-permute-done((bf16[768,128]{1,0:T(8,128)(2,1)}, bf16[768,128]{1,0:T(8,128)(2,1)S(1)}, u32[]{:S(2)}, u32[]{:S(2)}) %collective-permute-start.17) | collective-permute-done | bytes 196640 | tf_op jit(solution)/shard_map/ppermute | solution.py:660
  385.9 3.4 collective-permute-done.18.refs_3_
  389.3 2.7 shard_map.389
  392.8 18.5 %shard_map.387 = (bf16[768,768]{1,0:T(8,128)(2,1)}, bf16[768,256]{1,0:T(8,128)(2,1)}, bf16[768,128]{1,0:T(8,128)(2,1)}, f32[16,1024]{1,0:T(8,128)}, f32[16,1024]...) custom-call(f32[768,768]{1,0:T(8,128)} %get-tuple-element.74.dy_ref, ...), custom_call_target="tpu_custom_call" | custom-call | flops 2264924160 | bytes 34131968 | tf_op jit(solution)/shard_map/pallas_call | solution.py:471
  412.7 2.5 constant_dynamic-update-slice_fusion.6
  419.6 7.8 %convolution_convert_fusion = bf16[1024,2304]{1,0:T(8,128)(2,1)} fusion(bf16[768,1024]{1,0:T(8,128)(2,1)S(1)} %bitcast.120, bf16[768,2304]{1,0:T(8,128)(2,1)} %slice_dynamic-update-slice_fusion.1), kind=kOutput, calls=%fused_computation.2 | convolution fusion | flops 3626237952 | bytes 9830400 | tf_op jit(solution)/shard_map/td,tc->dc/dot_general | solution.py:832
  427.5 5.6 %pad_maximum_fusion = bf16[1024,3328]{1,0:T(8,128)(2,1)} fusion(bf16[1024,1024]{1,0:T(8,128)(2,1)S(1)} %copy-done.20, bf16[1024,2304]{1,0:T(8,128)(2,1)} %convolution_convert_fusion), kind=kLoop, calls=%fused_computation | loop fusion | flops 13631488 | bytes 13631488 | tf_op jit(solution)/shard_map/concatenate | solution.py:875
  438.0 2.1 pad_maximum_fusion.2
  440.3 7.9 %fusion.79 = (bf16[768,1024]{1,0:T(8,128)(2,1)S(1)}, f32[1024]{0:T(1024)S(1)}) fusion(f32[768]{0:T(1024)S(1)} %rsqrt.46, bf16[2,384,1024]{2,1,0:T(8,128)(2,1)S(1)} %copy-done.2, bf16[768,2304]{1,0:T(8,128)(2,1)} %slice_dynamic-update-slice_fusion.1, bf16[1024,2304]{1,0:T(8,128)(2,1)} %all-gather.3.cloned.1.call-done), kind=kOutput, calls=%fused_computation.176 | convolution fusion | flops 3627809792 | bytes 11410432 | tf_op jit(solution)/shard_map/tc,dc->td/dot_general | solution.py:877
  451.6 68.8 %all-reduce.6 = (f32[]{:T(128)}, f32[1024]{0:T(1024)}, f32[5,1536]{1,0:T(8,128)S(1)}, f32[5,256]{1,0:T(8,128)S(1)}, f32[3,24]{1,0:T(4,128)S(1)}, /*index=5*/f32[1024]{0:T(1024)}) all-reduce(f32[]{:T(128)S(6)} %div.79, f32[1024]{0:T(1024)S(1)} %get-tuple-element.202, ...), channel_id=1, replica_groups=mesh['dp'=4,'ctx'=4,'tp'=2] {'dp','ctx','tp'}, use_global_device_ids=true, to_apply=%region_6.7 | all-reduce | flops 11081 | bytes 88648 | tf_op jit(solution)/shard_map/psum | solution.py:901
  524.1 2.0 convert_add_fusion.3
  528.7 2.0 fusion.1
  536.3 2.4 collective-permute-start.22
  (285 shorter events, 60.6 us)
Async XLA Ops:
  7.2 5.3 copy-start.45
  7.2 5.3 copy-start.57
  7.2 5.3 copy-start.50
  7.2 5.3 copy-start.49
  7.2 61.3 %all-gather.3.cloned.1.call-start = ((), (), s32[]{:S(2)}) async-start(), calls=%async_computation.2 | async-start | bytes 5013504 | tf_op jit(solution)/shard_map/all_gather | solution.py:734
  8.3 5.2 copy-start.65
  8.3 5.2 copy-start.66
  12.4 140.9 %all-gather.5.cloned.1.call-start = ((), (), s32[]{:S(2)}) async-start(), calls=%async_computation.3 | async-start | bytes 8912896 | tf_op jit(solution)/shard_map/all_gather | solution.py:744
  13.4 517.3 %reduce-scatter.5.cloned.1.call-start = ((), (), s32[]{:S(2)}) async-start(), calls=%async_computation.5 | async-start | bytes 6684672 | tf_op jit(solution)/shard_map/reduce_scatter | solution.py:842
  75.1 3.9 copy-start
  79.0 10.8 %copy-start.68 = (f32[12]{0:T(128)S(1)}, f32[12]{0:T(128)}, u32[]{:S(2)}) copy-start(f32[12]{0:T(128)} %param.43) | copy-start | bytes 148
  79.0 10.8 %copy-start.69 = (f32[12]{0:T(128)S(1)}, f32[12]{0:T(128)}, u32[]{:S(2)}) copy-start(f32[12]{0:T(128)} %param.41) | copy-start | bytes 148
  81.7 27.8 %collective-permute-start.4 = (bf16[768,128]{1,0:T(8,128)(2,1)}, bf16[768,128]{1,0:T(8,128)(2,1)S(1)}, u32[]{:S(2)}, u32[]{:S(2)}) collective-permute-start(bf16[768,128]{1,0:T(8,128)(2,1)} %get-tuple-element.70.refs_0_), channel_id=1, source_target_pairs={{0,2},{2,4},{4,6},{1,3},{3,5},{5,7},{8,10},{10,12},{12,14},{9,11},... | collective-permute-start | bytes 589832 | tf_op jit(solution)/shard_map/ppermute | solution.py:660
  83.9 27.2 %collective-permute-start.5 = (bf16[768,128]{1,0:T(8,128)(2,1)}, bf16[768,128]{1,0:T(8,128)(2,1)S(1)}, u32[]{:S(2)}, u32[]{:S(2)}) collective-permute-start(bf16[768,128]{1,0:T(8,128)(2,1)} %get-tuple-element.70.refs_0_), channel_id=1, source_target_pairs={{0,4},{2,6},{1,5},{3,7},{8,12},{10,14},{9,13},{11,15},{16,20},{18,... | collective-permute-start | bytes 589832 | tf_op jit(solution)/shard_map/ppermute | solution.py:660
  86.4 24.7 %collective-permute-start.6 = (bf16[768,128]{1,0:T(8,128)(2,1)}, bf16[768,128]{1,0:T(8,128)(2,1)S(1)}, u32[]{:S(2)}, u32[]{:S(2)}) collective-permute-start(bf16[768,128]{1,0:T(8,128)(2,1)} %get-tuple-element.70.refs_0_), channel_id=1, source_target_pairs={{0,6},{1,7},{8,14},{9,15},{16,22},{17,23},{24,30},{25,31}} | collective-permute-start | bytes 589832 | tf_op jit(solution)/shard_map/ppermute | solution.py:660
  88.6 2.2 collective-permute-start
  102.0 19.8 %collective-permute-start.1 = (bf16[288,768]{1,0:T(8,128)(2,1)}, bf16[288,768]{1,0:T(8,128)(2,1)S(1)}, u32[]{:S(2)}, u32[]{:S(2)}) collective-permute-start(bf16[288,768]{1,0:T(8,128)(2,1)} %get-tuple-element.67.sent_ref), channel_id=1, source_target_pairs={{0,2},{2,4},{4,6},{1,3},{3,5},{5,7},{8,10},{10,12},{12,14},{9,11},... | collective-permute-start | bytes 1327112 | tf_op jit(solution)/shard_map/ppermute | solution.py:660
  105.2 24.6 %collective-permute-start.2 = (bf16[288,768]{1,0:T(8,128)(2,1)}, bf16[288,768]{1,0:T(8,128)(2,1)S(1)}, u32[]{:S(2)}, u32[]{:S(2)}) collective-permute-start(bf16[288,768]{1,0:T(8,128)(2,1)} %get-tuple-element.67.sent_ref), channel_id=1, source_target_pairs={{0,4},{2,6},{1,5},{3,7},{8,12},{10,14},{9,13},{11,15},{16,20},{18,... | collective-permute-start | bytes 1327112 | tf_op jit(solution)/shard_map/ppermute | solution.py:660
  109.5 35.4 %collective-permute-start.3 = (bf16[288,768]{1,0:T(8,128)(2,1)}, bf16[288,768]{1,0:T(8,128)(2,1)S(1)}, u32[]{:S(2)}, u32[]{:S(2)}) collective-permute-start(bf16[288,768]{1,0:T(8,128)(2,1)} %get-tuple-element.67.sent_ref), channel_id=1, source_target_pairs={{0,6},{1,7},{8,14},{9,15},{16,22},{17,23},{24,30},{25,31}} | collective-permute-start | bytes 1327112 | tf_op jit(solution)/shard_map/ppermute | solution.py:660
  121.8 23.2 %copy-start.39 = (bf16[288,768]{1,0:T(8,128)(2,1)}, bf16[288,768]{1,0:T(8,128)(2,1)S(1)}, u32[]{:S(2)}) copy-start(bf16[288,768]{1,0:T(8,128)(2,1)S(1)} %collective-permute-done.1.refs_0_) | copy-start | bytes 1327108
  129.8 15.2 %copy-start.40 = (bf16[288,768]{1,0:T(8,128)(2,1)}, bf16[288,768]{1,0:T(8,128)(2,1)S(1)}, u32[]{:S(2)}) copy-start(bf16[288,768]{1,0:T(8,128)(2,1)S(1)} %collective-permute-done.2.refs_1_) | copy-start | bytes 1327108
  153.3 5.0 copy-start.27
  156.5 4.9 copy-start.2
  156.5 20.5 %collective-permute-start.7 = (bf16[384,1024]{1,0:T(8,128)(2,1)S(1)}, bf16[384,1024]{1,0:T(8,128)(2,1)S(1)}, u32[]{:S(2)}, u32[]{:S(2)}) collective-permute-start(bf16[384,1024]{1,0:T(8,128)(2,1)S(1)} %fusion.50), channel_id=1, source_target_pairs={{0,1},{1,0},{2,3},{3,2},{4,5},{5,4},{6,7},{7,6},{8,9},{9,8},{10,11... | collective-permute-start | bytes 2359304 | tf_op jit(solution)/shard_map/ppermute | solution.py:667
  160.9 31.4 %collective-permute-start.9 = (bf16[384,1024]{1,0:T(8,128)(2,1)S(1)}, bf16[384,1024]{1,0:T(8,128)(2,1)S(1)}, u32[]{:S(2)}, u32[]{:S(2)}) collective-permute-start(bf16[384,1024]{1,0:T(8,128)(2,1)S(1)} %fusion.53), channel_id=1, source_target_pairs={{0,1},{1,0},{2,3},{3,2},{4,5},{5,4},{6,7},{7,6},{8,9},{9,8},{10,11... | collective-permute-start | bytes 2359304 | tf_op jit(solution)/shard_map/ppermute | solution.py:667
  161.3 32.0 %slice-start = ((s8[8388608]{0:T(1024)(128)(4,1)}), s8[4194304]{0:T(1024)(128)(4,1)S(1)}, s32[]{:S(2)}) async-start(s8[8388608]{0:T(1024)(128)(4,1)} %bitcast.136), calls=%async_computation.6 | async-start | bytes 8388608
  161.7 31.3 %copy-start.51 = (f32[1024]{0:T(1024)S(1)}, f32[1024]{0:T(1024)}, u32[]{:S(2)}) copy-start(f32[1024]{0:T(1024)} %param.45) | copy-start | bytes 12292
  161.7 31.6 %slice-start.1 = ((s8[8388608]{0:T(1024)(128)(4,1)}), s8[4194304]{0:T(1024)(128)(4,1)S(1)}, s32[]{:S(2)}) async-start(s8[8388608]{0:T(1024)(128)(4,1)} %bitcast.136), calls=%async_computation.7 | async-start | bytes 8388608
  193.4 7.2 %copy-start.31 = (bf16[384,1024]{1,0:T(8,128)(2,1)}, bf16[384,1024]{1,0:T(8,128)(2,1)S(1)}, u32[]{:S(2)}) copy-start(bf16[384,1024]{1,0:T(8,128)(2,1)S(1)} %get-tuple-element.223) | copy-start | bytes 2359300
  198.8 20.8 %collective-permute-start.8 = (bf16[384,1024]{1,0:T(8,128)(2,1)}, bf16[384,1024]{1,0:T(8,128)(2,1)}, u32[]{:S(2)}, u32[]{:S(2)}) collective-permute-start(bf16[384,1024]{1,0:T(8,128)(2,1)} %convolution_convert_fusion.5), channel_id=1, source_target_pairs={{0,1},{1,0},{2,3},{3,2},{4,5},{5,4},{6,7},{7,6},{8,9},{9,8},{10,11... | collective-permute-start | bytes 2359304 | tf_op jit(solution)/shard_map/ppermute | solution.py:667
  206.0 28.0 %collective-permute-start.10 = (bf16[384,1024]{1,0:T(8,128)(2,1)}, bf16[384,1024]{1,0:T(8,128)(2,1)}, u32[]{:S(2)}, u32[]{:S(2)}) collective-permute-start(bf16[384,1024]{1,0:T(8,128)(2,1)} %convolution_convert_fusion.4), channel_id=1, source_target_pairs={{0,1},{1,0},{2,3},{3,2},{4,5},{5,4},{6,7},{7,6},{8,9},{9,8},{10,11... | collective-permute-start | bytes 2359304 | tf_op jit(solution)/shard_map/ppermute | solution.py:667
  208.5 30.6 %copy-start.35 = (bf16[384,1024]{1,0:T(8,128)(2,1)S(1)}, bf16[384,1024]{1,0:T(8,128)(2,1)}, u32[]{:S(2)}) copy-start(bf16[384,1024]{1,0:T(8,128)(2,1)} %copy-done.34) | copy-start | bytes 2359300
  208.5 30.6 %copy-start.37 = (bf16[384,1024]{1,0:T(8,128)(2,1)S(1)}, bf16[384,1024]{1,0:T(8,128)(2,1)}, u32[]{:S(2)}) copy-start(bf16[384,1024]{1,0:T(8,128)(2,1)} %copy-done.36) | copy-start | bytes 2359300
  233.9 16.9 %slice-start.2 = ((s8[8388608]{0:T(1024)(128)(4,1)}), s8[4194304]{0:T(1024)(128)(4,1)S(1)}, s32[]{:S(2)}) async-start(s8[8388608]{0:T(1024)(128)(4,1)} %bitcast.138), calls=%async_computation.8 | async-start | bytes 8388608
  239.1 11.7 %copy-start.17 = (f32[384,2048]{1,0:T(8,128)S(1)}, f32[384,2048]{1,0:T(8,128)}, u32[]{:S(2)}) copy-start(f32[384,2048]{1,0:T(8,128)} %copy-done.16) | copy-start | bytes 9437188
  239.2 11.7 %slice-start.3 = ((s8[8388608]{0:T(1024)(128)(4,1)}), s8[4194304]{0:T(1024)(128)(4,1)S(1)}, s32[]{:S(2)}) async-start(s8[8388608]{0:T(1024)(128)(4,1)} %bitcast.138), calls=%async_computation.9 | async-start | bytes 8388608
  264.6 269.2 %reduce-scatter.3.cloned.1.call-start = ((), (), s32[]{:S(2)}) async-start(), calls=%async_computation.4 | async-start | bytes 7241728 | tf_op jit(solution)/shard_map/reduce_scatter | solution.py:876
  264.6 6.4 %copy-start.24 = (bf16[384,2048]{1,0:T(8,128)(2,1)S(1)}, bf16[384,2048]{1,0:T(8,128)(2,1)}, u32[]{:S(2)}) copy-start(bf16[384,2048]{1,0:T(8,128)(2,1)} %copy-done.23) | copy-start | bytes 4718596
  269.2 34.0 %copy-start.4 = (f32[384,1024]{1,0:T(8,128)S(1)}, f32[384,1024]{1,0:T(8,128)}, u32[]{:S(2)}) copy-start(f32[384,1024]{1,0:T(8,128)} %copy-done.3) | copy-start | bytes 4718596
  269.2 34.0 %copy-start.5 = (bf16[2,384,1024]{2,1,0:T(8,128)(2,1)S(1)}, bf16[2,384,1024]{2,1,0:T(8,128)(2,1)}, u32[]{:S(2)}) copy-start(bf16[2,384,1024]{2,1,0:T(8,128)(2,1)} %param.28) | copy-start | bytes 4718596
  269.2 20.5 %collective-permute-start.12 = (bf16[384,1024]{1,0:T(8,128)(2,1)S(1)}, bf16[384,1024]{1,0:T(8,128)(2,1)S(1)}, u32[]{:S(2)}, u32[]{:S(2)}) collective-permute-start(bf16[384,1024]{1,0:T(8,128)(2,1)S(1)} %fusion.47), channel_id=1, source_target_pairs={{0,1},{1,0},{2,3},{3,2},{4,5},{5,4},{6,7},{7,6},{8,9},{9,8},{10,11... | collective-permute-start | bytes 2359304 | tf_op jit(solution)/shard_map/ppermute | solution.py:667
  275.0 32.7 %copy-start.7 = (bf16[2,384,1024]{2,1,0:T(8,128)(2,1)S(1)}, bf16[2,384,1024]{2,1,0:T(8,128)(2,1)}, u32[]{:S(2)}) copy-start(bf16[2,384,1024]{2,1,0:T(8,128)(2,1)} %param.29) | copy-start | bytes 4718596
  275.0 28.2 %collective-permute-start.11 = (bf16[384,1024]{1,0:T(8,128)(2,1)S(1)}, bf16[384,1024]{1,0:T(8,128)(2,1)S(1)}, u32[]{:S(2)}, u32[]{:S(2)}) collective-permute-start(bf16[384,1024]{1,0:T(8,128)(2,1)S(1)} %fusion.44), channel_id=1, source_target_pairs={{0,1},{1,0},{2,3},{3,2},{4,5},{5,4},{6,7},{7,6},{8,9},{9,8},{10,11... | collective-permute-start | bytes 2359304 | tf_op jit(solution)/shard_map/ppermute | solution.py:667
  311.0 44.0 %copy-start.8 = (f32[384,1024]{1,0:T(8,128)}, f32[384,1024]{1,0:T(8,128)S(1)}, u32[]{:S(2)}) copy-start(f32[384,1024]{1,0:T(8,128)S(1)} %get-tuple-element.205) | copy-start | bytes 4718596
  314.8 40.2 %copy-start.10 = (f32[384,1024]{1,0:T(8,128)}, f32[384,1024]{1,0:T(8,128)S(1)}, u32[]{:S(2)}) copy-start(f32[384,1024]{1,0:T(8,128)S(1)} %get-tuple-element.203) | copy-start | bytes 4718596
  339.4 14.1 %collective-permute-start.16 = (bf16[768,128]{1,0:T(8,128)(2,1)}, bf16[768,128]{1,0:T(8,128)(2,1)S(1)}, u32[]{:S(2)}, u32[]{:S(2)}) collective-permute-start(bf16[768,128]{1,0:T(8,128)(2,1)} %get-tuple-element.83), channel_id=1, source_target_pairs={{2,0},{4,2},{6,4},{3,1},{5,3},{7,5},{10,8},{12,10},{14,12},{11,9},... | collective-permute-start | bytes 589832 | tf_op jit(solution)/shard_map/ppermute | solution.py:660
  340.7 14.3 %copy-start.28 = (bf16[768,1024]{1,0:T(8,128)(2,1)S(1)}, bf16[768,1024]{1,0:T(8,128)(2,1)}, u32[]{:S(2)}) copy-start(bf16[768,1024]{1,0:T(8,128)(2,1)} %copy-done.27) | copy-start | bytes 4718596
  348.3 43.7 %collective-permute-start.13 = (bf16[288,768]{1,0:T(8,128)(2,1)}, bf16[288,768]{1,0:T(8,128)(2,1)S(1)}, u32[]{:S(2)}, u32[]{:S(2)}) collective-permute-start(bf16[288,768]{1,0:T(8,128)(2,1)} %get-tuple-element.77), channel_id=1, source_target_pairs={{2,0},{4,2},{6,4},{3,1},{5,3},{7,5},{10,8},{12,10},{14,12},{11,9},... | collective-permute-start | bytes 1327112 | tf_op jit(solution)/shard_map/ppermute | solution.py:660
  349.6 42.4 %collective-permute-start.14 = (bf16[288,768]{1,0:T(8,128)(2,1)}, bf16[288,768]{1,0:T(8,128)(2,1)}, u32[]{:S(2)}, u32[]{:S(2)}) collective-permute-start(bf16[288,768]{1,0:T(8,128)(2,1)} %get-tuple-element.77), channel_id=1, source_target_pairs={{4,0},{6,2},{5,1},{7,3},{12,8},{14,10},{13,9},{15,11},{20,16},{22,... | collective-permute-start | bytes 1327112 | tf_op jit(solution)/shard_map/ppermute | solution.py:660
  350.9 41.1 %collective-permute-start.15 = (bf16[288,768]{1,0:T(8,128)(2,1)}, bf16[288,768]{1,0:T(8,128)(2,1)}, u32[]{:S(2)}, u32[]{:S(2)}) collective-permute-start(bf16[288,768]{1,0:T(8,128)(2,1)} %get-tuple-element.77), channel_id=1, source_target_pairs={{6,0},{7,1},{14,8},{15,9},{22,16},{23,17},{30,24},{31,25}} | collective-permute-start | bytes 1327112 | tf_op jit(solution)/shard_map/ppermute | solution.py:660
  352.2 33.7 %collective-permute-start.17 = (bf16[768,128]{1,0:T(8,128)(2,1)}, bf16[768,128]{1,0:T(8,128)(2,1)S(1)}, u32[]{:S(2)}, u32[]{:S(2)}) collective-permute-start(bf16[768,128]{1,0:T(8,128)(2,1)} %get-tuple-element.84), channel_id=1, source_target_pairs={{4,0},{6,2},{5,1},{7,3},{12,8},{14,10},{13,9},{15,11},{20,16},{22,... | collective-permute-start | bytes 589832 | tf_op jit(solution)/shard_map/ppermute | solution.py:660
  353.5 4.7 copy-start.46
  353.6 4.7 copy-start.25
  353.6 35.7 %collective-permute-start.18 = (bf16[768,128]{1,0:T(8,128)(2,1)}, bf16[768,128]{1,0:T(8,128)(2,1)}, u32[]{:S(2)}, u32[]{:S(2)}) collective-permute-start(bf16[768,128]{1,0:T(8,128)(2,1)} %get-tuple-element.85), channel_id=1, source_target_pairs={{6,0},{7,1},{14,8},{15,9},{22,16},{23,17},{30,24},{31,25}} | collective-permute-start | bytes 589832 | tf_op jit(solution)/shard_map/ppermute | solution.py:660
  385.9 3.4 copy-start.47
  411.3 4.0 copy-start.44
  411.3 7.1 %collective-permute-start.19 = (f32[16,1024]{1,0:T(8,128)}, f32[16,1024]{1,0:T(8,128)S(1)}, u32[]{:S(2)}, u32[]{:S(2)}) collective-permute-start(f32[16,1024]{1,0:T(8,128)} %get-tuple-element.88), channel_id=1, source_target_pairs={{2,0},{4,2},{6,4},{3,1},{5,3},{7,5},{10,8},{12,10},{14,12},{11,9},... | collective-permute-start | bytes 196616 | tf_op jit(solution)/shard_map/ppermute | solution.py:660
  412.7 3.4 copy-start.43
  412.7 4.2 copy-start.33
  415.2 4.4 copy-start.21
  419.6 7.8 %copy-start.20 = (bf16[1024,1024]{1,0:T(8,128)(2,1)S(1)}, bf16[1024,1024]{1,0:T(8,128)(2,1)}, u32[]{:S(2)}) copy-start(bf16[1024,1024]{1,0:T(8,128)(2,1)} %convolution_convert_fusion.3) | copy-start | bytes 6291460
  449.5 74.6 %collective-permute-start.20 = (bf16[384,1024]{1,0:T(8,128)(2,1)}, bf16[384,1024]{1,0:T(8,128)(2,1)}, u32[]{:S(2)}, u32[]{:S(2)}) collective-permute-start(bf16[384,1024]{1,0:T(8,128)(2,1)} %get-tuple-element.213), channel_id=1, source_target_pairs={{0,1},{1,0},{2,3},{3,2},{4,5},{5,4},{6,7},{7,6},{8,9},{9,8},{10,11... | collective-permute-start | bytes 2359304 | tf_op jit(solution)/shard_map/ppermute | solution.py:667
  450.9 73.2 %collective-permute-start.21 = (bf16[384,1024]{1,0:T(8,128)(2,1)}, bf16[384,1024]{1,0:T(8,128)(2,1)}, u32[]{:S(2)}, u32[]{:S(2)}) collective-permute-start(bf16[384,1024]{1,0:T(8,128)(2,1)} %get-tuple-element.214), channel_id=1, source_target_pairs={{0,1},{1,0},{2,3},{3,2},{4,5},{5,4},{6,7},{7,6},{8,9},{9,8},{10,11... | collective-permute-start | bytes 2359304 | tf_op jit(solution)/shard_map/ppermute | solution.py:667
  536.3 4.8 collective-permute-start.22
  (41 other events, 75.6 us)
Sparse Core Ops, SparseCore 0:
  12.5 55.9 all-gather.2
  71.2 73.4 all-gather.4
  264.7 93.4 reduce-scatter.4
  433.2 87.9 reduce-scatter.2

commit v3 on v2

--- a/solution.py
+++ b/solution.py
@@ -295,7 +295,7 @@
 
 def gate_back_body(
     g_ref, z_ref, y_ref, v_ref, vbc_ref, logs_ref, heads_ref, sent_ref,
-    dy_ref, dz_ref, send_ref, dskip_ref,
+    dy_ref, dz_ref, dskip_ref, send_ref,
 ):
     tokens, channels = y_ref.shape
     spread = head_map(channels)
@@ -426,14 +426,15 @@
                 total = total + taps[k : k + 1, :] * ext[at : at + count, :]
             return total
 
-        head_ref[:, cols] = spread_rows(0, 8)
+        head_ref[0:8, cols] = jnp.zeros((8, ext.shape[1]), f32)
+        head_ref[8:16, cols] = spread_rows(0, 8)
         grads = [0.0] * (KC + 1)
         for c in range(chunks):
             at = CBLK * c
             dpre = spread_rows(8 + at, CBLK)
             out_ref[at : at + CBLK, :] = dpre.astype(low)
             if c == chunks - 1:
-                edge_ref[:, cols] = dpre[CBLK - 8 :, :]
+                edge_ref[:, cols] = dpre[CBLK - 16 :, :]
         for k in range(KC):
             shift = KC - 1 - k
             main = jnp.sum(pre_ref[...] * ext[8 + shift : 8 + shift + tokens, :], 0, keepdims=True)
@@ -449,8 +450,8 @@
     conv_back(dbce, taps_bc_ref, dbc_ref, bc_cols, gbc_ref, bc_ref, bct_ref)
 
 
-def block(height, width, col=0):
-    return pl.BlockSpec((height, width), lambda s: (s, col))
+def block(height, width, col=0, first=0):
+    return pl.BlockSpec((height, width), lambda s: (first + s, col))
 
 
 def whole(shape):
@@ -461,20 +462,36 @@
     return jax.ShapeDtypeStruct((rows, cols), dtype)
 
 
-def run(body, seqs, inputs, outputs, scratch=(), at=None, flops=0):
+def run(body, seqs, inputs, outputs, scratch=(), at=None, flops=0, shared=()):
     arrays = [a for a, _ in inputs]
     specs = [s for _, s in inputs]
     if at is not None:
         arrays = [at] + arrays
         specs = [pl.BlockSpec(memory_space=pltpu.SMEM)] + specs
     moved = sum(a.size * a.dtype.itemsize for a in arrays)
+    out_specs = [block(r, c) for r, c, _ in outputs]
+    out_shape = [shaped(seqs * r, c, d) for r, c, d in outputs]
+    aliases, count = {}, len(arrays)
+    for r, c, d, total, first, previous in shared:
+        if previous is not None:
+            aliases[len(arrays)] = len(out_shape)
+            arrays.append(previous)
+            specs.append(pl.BlockSpec(memory_space=pl.ANY))
+        out_specs.append(block(r, c, 0, first))
+        out_shape.append(shaped(total * r, c, d))
+    kept = len(aliases)
+
+    def inner(*refs):
+        body(*refs[:count], *refs[count + kept :])
+
     return pl.pallas_call(
-        body,
+        inner,
         grid=(seqs,),
         in_specs=specs,
-        out_specs=[block(r, c) for r, c, _ in outputs],
-        out_shape=[shaped(seqs * r, c, d) for r, c, d in outputs],
+        out_specs=out_specs,
+        out_shape=out_shape,
         scratch_shapes=list(scratch),
+        input_output_aliases=aliases,
         compiler_params=vmem_params(),
         cost_estimate=pl.CostEstimate(flops=flops, bytes_accessed=moved, transcendentals=0),
     )(*arrays)
@@ -507,24 +524,27 @@
     )
 
 
-def attend_back(queries, keyvals, grads, grad_at, outs, lse, cosine, sine, at, seqs, tokens):
+def attend_back(
+    queries, keyvals, grads, grad_at, outs, lse, cosine, sine, at, first, seqs, tokens, previous
+):
     hops, cols = len(keyvals), queries.shape[1]
-    work = 10 * seqs * tokens * tokens * hops * (cols // HEAD_SIZE) * 256
+    work = 10 * tokens * tokens * hops * (cols // HEAD_SIZE) * 256
     return run(
         functools.partial(attend_back_body, hops=hops),
-        seqs,
+        1,
         [
-            (queries, block(tokens, cols)),
+            (queries, block(tokens, cols, 0, first)),
             (grads, block(tokens, cols, grad_at // cols)),
-            (outs, block(tokens, cols)),
-            (lse, block(tokens, 128)),
-            (cosine, block(tokens, 128)),
-            (sine, block(tokens, 128)),
+            (outs, block(tokens, cols, 0, first)),
+            (lse, block(tokens, 128, 0, first)),
+            (cosine, block(tokens, 128, 0, first)),
+            (sine, block(tokens, 128, 0, first)),
         ]
-        + [(kv, block(tokens, 128)) for kv in keyvals],
-        [(tokens, cols, low)] + [(tokens, 128, low)] * hops,
+        + [(kv, block(tokens, 128, 0, first)) for kv in keyvals],
+        [(tokens, cols, low)],
         at=at,
         flops=work,
+        shared=[(tokens, 128, low, seqs, first, p) for p in previous],
     )
 
 
@@ -540,15 +560,37 @@
 SENT = NS + 16
 
 
-def scan(pre, tails, taps, taps_bc, per_head, seqs, tokens, channels, heads):
-    step_at = pre.shape[1] // 128 - 1
+class Columns:
+    def __init__(self, channels, q_cols):
+        self.channels = channels
+        self.x, self.z, self.q = 0, channels, 2 * channels
+        self.bc = self.q + q_cols
+        self.kv = self.bc + 2 * NS
+        self.step = self.kv + 128
+        self.total = self.step + 128
+
+    def x_block(self, tokens, first=0):
+        return block(tokens, self.channels, 0, first)
+
+    def z_block(self, tokens, first=0):
+        return block(tokens, self.channels, 1, first)
+
+    def bc_block(self, tokens, first=0):
+        return block(tokens, 2 * NS, self.bc // (2 * NS), first)
+
+    def step_block(self, tokens, first=0):
+        return block(tokens, 128, self.step // 128, first)
+
+
+def scan(pre, cols, tails, taps, taps_bc, per_head, seqs, tokens, heads):
+    channels = cols.channels
     return run(
         functools.partial(scan_body, heads=heads),
         seqs,
         [
-            (pre, block(tokens, channels, 1)),
-            (pre, block(tokens, 2 * NS, 2 * channels // (2 * NS))),
-            (pre, block(tokens, 128, step_at)),
+            (pre, cols.x_block(tokens)),
+            (pre, cols.bc_block(tokens)),
+            (pre, cols.step_block(tokens)),
             (tails, block(8, channels)),
             (tails, block(8, 2 * NS, channels // (2 * NS))),
             (taps, whole(taps.shape)),
@@ -568,80 +610,82 @@
     )
 
 
-def gate(pre, y, v, vbc, logs, per_head, earlier, seqs, tokens, channels):
+def gate(pre, cols, y, v, vbc, logs, per_head, earlier, first, tokens):
+    channels = cols.channels
     return run(
         gate_body,
-        seqs,
+        1,
         [
-            (pre, block(tokens, channels, 0)),
-            (y, block(tokens, channels)),
-            (v, block(tokens, channels)),
-            (vbc, block(tokens, 2 * NS)),
-            (logs, block(tokens, 128)),
+            (pre, cols.z_block(tokens, first)),
+            (y, block(tokens, channels, 0, first)),
+            (v, block(tokens, channels, 0, first)),
+            (vbc, block(tokens, 2 * NS, 0, first)),
+            (logs, block(tokens, 128, 0, first)),
             (per_head, whole(per_head.shape)),
         ]
-        + [(a, block(SENT, channels)) for a in earlier],
+        + [(a, block(SENT, channels, 0, first)) for a in earlier],
         [(tokens, channels, low), (tokens, channels, f32), (NS, channels, f32)],
-        flops=4 * seqs * tokens * CBLK * channels,
-    )
-
-
-def gate_back(grads, pre, y, v, vbc, logs, per_head, sent, seqs, tokens, channels):
+        flops=4 * tokens * CBLK * channels,
+    )
+
+
+def gate_back(grads, pre, cols, y, v, vbc, logs, per_head, sent, first, seqs, tokens, previous):
+    channels = cols.channels
     return run(
         gate_back_body,
-        seqs,
+        1,
         [
-            (grads, block(tokens, channels, 0)),
-            (pre, block(tokens, channels, 0)),
+            (grads, block(tokens, channels)),
+            (pre, cols.z_block(tokens, first)),
             (y, block(tokens, channels)),
-            (v, block(tokens, channels)),
-            (vbc, block(tokens, 2 * NS)),
-            (logs, block(tokens, 128)),
+            (v, block(tokens, channels, 0, first)),
+            (vbc, block(tokens, 2 * NS, 0, first)),
+            (logs, block(tokens, 128, 0, first)),
             (per_head, whole(per_head.shape)),
-            (sent, block(SENT, channels)),
+            (sent, block(SENT, channels, 0, first)),
         ],
         [
             (tokens, channels, f32),
             (tokens, channels, low),
-            (SENT, channels, low),
             (8, channels, f32),
         ],
-        flops=4 * seqs * tokens * CBLK * channels,
+        flops=4 * tokens * CBLK * channels,
+        shared=[(SENT, channels, low, seqs, first, previous)],
     )
 
 
 def scan_back(
-    dy, y, v, vbc, pre, tails, taps, taps_bc, per_head, logs, states, carried, later,
-    seqs, tokens, channels, heads,
+    dy, y, v, vbc, pre, cols, tails, taps, taps_bc, per_head, logs, states, carried, later,
+    first, tokens, heads,
 ):
-    step_at = pre.shape[1] // 128 - 1
+    channels = cols.channels
     return run(
         functools.partial(scan_back_body, heads=heads),
-        seqs,
+        1,
         [
             (dy, block(tokens, channels)),
             (y, block(tokens, channels)),
-            (v, block(tokens, channels)),
-            (vbc, block(tokens, 2 * NS)),
-            (pre, block(tokens, channels, 1)),
-            (pre, block(tokens, 2 * NS, 2 * channels // (2 * NS))),
-            (pre, block(tokens, 128, step_at)),
-            (tails, block(8, channels)),
-            (tails, block(8, 2 * NS, channels // (2 * NS))),
+            (v, block(tokens, channels, 0, first)),
+            (vbc, block(tokens, 2 * NS, 0, first)),
+            (pre, cols.x_block(tokens, first)),
+            (pre, cols.bc_block(tokens, first)),
+            (pre, cols.step_block(tokens, first)),
+            (tails, block(8, channels, 0, first)),
+            (tails, block(8, 2 * NS, channels // (2 * NS), first)),
             (taps, whole(taps.shape)),
             (taps_bc, whole(taps_bc.shape)),
             (per_head, whole(per_head.shape)),
-            (logs, block(tokens, 128)),
-            (states, block(tokens // CBLK * NS, channels)),
+            (logs, block(tokens, 128, 0, first)),
+            (states, block(tokens // CBLK * NS, channels, 0, first)),
             (carried, block(NS, channels)),
         ]
-        + [(a, block(SENT, channels)) for a in later],
+        + [(a, block(SENT, channels, 0, first)) for a in later],
         [
             (tokens, channels, low),
             (tokens, 2 * NS, low),
             (tokens, 128, low),
-            (8, channels + 2 * NS, f32),
-            (8, channels + 2 * NS, f32),
+            (16, channels + 2 * NS, f32),
+            (16, channels + 2 * NS, f32),
             (8, channels, f32),
             (8, 2 * NS, f32),
             (8, 128, f32),
@@ -650,22 +694,177 @@
             pltpu.VMEM((tokens + 16, channels), f32),
             pltpu.VMEM((tokens + 16, 2 * NS), f32),
         ],
-        flops=30 * seqs * tokens * CBLK * channels,
-    )
-
-
-def passed_along(block, axis, distance):
+        flops=30 * tokens * CBLK * channels,
+    )
+
+
+TILE = 256
+
+
+def hold(held, first_tile, rows, parts):
+    col = first_tile * TILE
+    for part in parts:
+        width = min(part.shape[1], TILE)
+        for at in range(0, part.shape[1], width):
+            inside = col % TILE
+            held[col // TILE, rows, inside : inside + width] = part[:, at : at + width]
+            col += width
+
+
+def early_grads_body(left_ref, weight_ref, *refs, seqs):
+    pieces, (wgrad_ref, part_ref, held) = refs[:-3], refs[-3:]
+    tile = pl.program_id(0)
+    tokens = held.shape[1] // seqs
+
+    @pl.when(tile == 0)
+    def _():
+        for s in range(seqs):
+            hold(held, 0, slice(tokens * s, tokens * (s + 1)), pieces[2 * s : 2 * s + 2])
+        part_ref[...] = jnp.zeros_like(part_ref)
+
+    grads = held[tile]
+    wgrad_ref[...] = mm(left_ref[...], grads).astype(low)
+    part_ref[...] += mm_nt(grads, weight_ref[...])
+
+
+def late_grads_body(left_ref, weight_ref, start_ref, keyval_ref, *refs, seqs):
+    pieces, (wgrad_ref, part_ref, held, total) = refs[:-4], refs[-4:]
+    tile = pl.program_id(0)
+    tokens = held.shape[1] // seqs
+
+    @pl.when(tile == 0)
+    def _():
+        for s in range(seqs):
+            dx, dbc, dstep, edge, head = pieces[5 * s : 5 * s + 5]
+            rows = slice(tokens * s, tokens * (s + 1))
+            hold(held, 0, rows, (dx, dbc, keyval_ref.at[rows, :], dstep))
+            mended = (edge[...] + head[16 * s : 16 * s + 16, :]).astype(low)
+            for at in range(0, mended.shape[1], TILE):
+                held[at // TILE, tokens * (s + 1) - 16 : tokens * (s + 1), :] = mended[
+                    :, at : at + TILE
+                ]
+        total[...] = start_ref[...]
+
+    grads = held[tile]
+    wgrad_ref[...] = mm(left_ref[...], grads).astype(low)
+    total[...] += mm_nt(grads, weight_ref[...])
+
+    @pl.when(tile == pl.num_programs(0) - 1)
+    def _():
+        part_ref[...] = total[...].astype(low)
+
+
+def tiled_grads(body, left, weight, tile_of, tiles, arrays, part_dtype, scratch):
+    width, rows = left.shape
+    return pl.pallas_call(
+        body,
+        grid=(tiles,),
+        in_specs=[whole(left.shape), pl.BlockSpec((width, TILE), lambda t: (0, tile_of(t)))]
+        + [whole(a.shape) for a in arrays],
+        out_specs=[pl.BlockSpec((width, TILE), lambda t: (0, t)), whole((rows, width))],
+        out_shape=[shaped(width, tiles * TILE, low), shaped(rows, width, part_dtype)],
+        scratch_shapes=[pltpu.VMEM((tiles, rows, TILE), low), *scratch],
+        compiler_params=vmem_params(),
+        cost_estimate=pl.CostEstimate(
+            flops=4 * rows * tiles * TILE * width,
+            bytes_accessed=4 * width * tiles * TILE,
+            transcendentals=0,
+        ),
+    )(left, weight, *arrays)
+
+
+def early_grads(left, weight, cols, pieces, seqs):
+    first = cols.z // TILE
+    tiles = (cols.bc - cols.z) // TILE
+    return tiled_grads(
+        functools.partial(early_grads_body, seqs=seqs),
+        left, weight, lambda t: t + first, tiles, [a for p in pieces for a in p], f32, [],
+    )
+
+
+def late_grads(left, weight, cols, start, keyval, pieces, seqs):
+    before = cols.z // TILE
+    skipped = (cols.bc - cols.z) // TILE
+    return tiled_grads(
+        functools.partial(late_grads_body, seqs=seqs),
+        left,
+        weight,
+        lambda t: jnp.where(t < before, t, t + skipped),
+        cols.total // TILE - skipped,
+        [start, keyval] + [a for p in pieces for a in p],
+        low,
+        [pltpu.VMEM(start.shape, f32)],
+    )
+
+
+def passed_along(array, axis, distance):
     devices = range(lax.axis_size(axis))
     route = [(i - distance, i) for i in devices if i - distance in devices]
-    return lax.ppermute(block, axis, route)
-
-
-def pair_sum(part):
-    if lax.axis_size("tp") != 2:
-        return lax.psum(part, "tp")
+    return lax.ppermute(array, axis, route)
+
+
+def after(array, *others):
+    return lax.optimization_barrier((array, *others))[0]
+
+
+def swapped(array, axis, distance):
+    devices = range(lax.axis_size(axis))
+    return lax.ppermute(array, axis, [(i, i ^ distance) for i in devices])
+
+
+def offer(part):
     mine = part.astype(low)
-    other = lax.ppermute(mine, "tp", [(0, 1), (1, 0)])
+    return mine, swapped(mine, "tp", 1)
+
+
+def summed_pair(mine, other):
     return mine.astype(f32) + other.astype(f32)
+
+
+def sum_over(array, axes):
+    for axis in axes:
+        distance = 1
+        while distance < lax.axis_size(axis):
+            array = array + swapped(array, axis, distance)
+            distance *= 2
+    return array
+
+
+def place(axis, distance=0):
+    return lax.axis_index(axis).astype(jnp.uint32) ^ jnp.uint32(distance)
+
+
+def place(axis, distance=0):
+    return lax.axis_index(axis).astype(jnp.uint32) ^ jnp.uint32(distance)
+
+
+def picked(array, at, dim):
+    return lax.dynamic_index_in_dim(array, at, dim, False)
+
+
+def core_sum(terms):
+    dp, ctx = lax.axis_size("dp"), lax.axis_size("ctx")
+    rows, cols = terms.shape[0] // (dp * ctx), terms.shape[1]
+    one = jnp.uint32(1)
+    pieces = terms.reshape(dp, ctx // 2, 2, rows, cols)
+    got = swapped(picked(pieces, place("ctx", 1) & one, 2), "ctx", 1)
+    return (picked(pieces, place("ctx") & one, 2).astype(f32) + got.astype(f32)).astype(low)
+
+
+def spread(held, axis, dim, shift):
+    own = picked(held, place(axis) >> jnp.uint32(shift), dim)
+    sends = [
+        picked(held, place(axis, d << shift) >> jnp.uint32(shift), dim)
+        for d in range(1, held.shape[dim])
+    ]
+    return own, sends, [swapped(a, axis, (d + 1) << shift) for d, a in enumerate(sends)]
+
+
+def added(own, got):
+    total = own.astype(f32)
+    for block_in in got:
+        total = total + block_in.astype(f32)
+    return total
 
 
 def rms_norm(values, gain):
@@ -716,41 +915,38 @@
     hidden_units = gateup_weight.shape[2]
     step_cols = 128
     hops = lax.axis_size("ctx")
+    each = range(seqs)
 
     tallies = jnp.sum(valid_mask.reshape(seqs * tokens // CBLK, CBLK), -1).astype(low)
     spare = jnp.zeros((rows, step_cols - heads), low)
     spare = spare.at[0, : tallies.shape[0]].set(tallies)
     mixer_shard = jnp.concatenate(
         [
-            stream_weight.reshape(rows, 2 * channels),
+            stream_weight[:, 1],
+            stream_weight[:, 0],
+            query_weight,
             state_weight,
-            query_weight,
             keyvalue_projection_weight.reshape(rows, 2 * kv_cols),
             step_weight,
             spare,
-        ],
-        1,
-    )
-    mixer_full = lax.all_gather(mixer_shard, owners, axis=0, tiled=True)
-    ffn_shard = jnp.concatenate(
-        [
-            gateup_weight.reshape(rows, 2 * hidden_units),
-            down_weight.T,
             mambaout_weight.T,
             attnout_weight.T,
         ],
         1,
     )
+    cols = Columns(channels, q_cols)
+    all_cols = cols.total
+    mixer_both = lax.all_gather(mixer_shard, owners, axis=0, tiled=True)
+    mixer_full, out_full_w = mixer_both[:, :all_cols], mixer_both[:, all_cols:]
+    ffn_shard = jnp.concatenate(
+        [gateup_weight.reshape(rows, 2 * hidden_units), down_weight.T], 1
+    )
     ffn_full = lax.all_gather(ffn_shard, owners, axis=0, tiled=True)
     gateup_full = ffn_full[:, : 2 * hidden_units]
-    down_full = ffn_full[:, 2 * hidden_units : 3 * hidden_units]
-    out_full_w = ffn_full[:, 3 * hidden_units :]
-
-    edges = [0]
-    for size in (channels, channels, bc_cols, q_cols, kv_cols, kv_cols, heads):
-        edges.append(edges[-1] + size)
-    all_cols = mixer_full.shape[1]
-    counts = mixer_full.reshape(-1, rows, all_cols)[:, 0, edges[7] : edges[7] + tallies.shape[0]]
+    down_full = ffn_full[:, 2 * hidden_units :]
+
+    counts = mixer_both.reshape(-1, rows, mixer_both.shape[1])
+    counts = counts[:, 0, cols.step + heads : cols.step + heads + tallies.shape[0]]
     valid_total = jnp.sum(counts.astype(f32))
 
     at = lax.axis_index("ctx").astype(jnp.int32).reshape(1)
@@ -767,119 +963,139 @@
 
     hidden = hidden_in.astype(f32)
     normed = rms_norm(hidden, mixer_gain).astype(low).reshape(seqs * tokens, width)
+    normed, normed_t = lax.optimization_barrier((normed, normed.T))
     pre = jnp.dot(normed, mixer_full, preferred_element_type=f32)
 
     def last_rows(array):
         return array.reshape(seqs, tokens, -1)[:, tokens - 8 :].reshape(seqs * 8, -1)
 
-    tails = passed_along(last_rows(pre[:, channels : edges[3]]), "ctx", 1)
-    queries, keyval = prep(pre, cosine, sine, seqs, tokens, edges[3], q_cols, edges[4])
+    ends = last_rows(pre)
+    ends = jnp.concatenate([ends[:, : cols.z], ends[:, cols.bc : cols.kv]], 1)
+    tails = passed_along(ends, "ctx", 1)
+    queries, keyval = prep(pre, cosine, sine, seqs, tokens, cols.q, q_cols, cols.kv)
     keyvals = [keyval] + [passed_along(keyval, "ctx", d) for d in range(1, hops)]
     v, vbc, y_own, logs, states, sent = scan(
-        pre, tails, taps, taps_bc, per_head, seqs, tokens, channels, heads
+        pre, cols, tails, taps, taps_bc, per_head, seqs, tokens, heads
     )
     earlier = [passed_along(sent, "ctx", d) for d in range(1, hops)]
-    attended, lse = attend(queries, keyvals, at, seqs, tokens)
-    gated, y, carried = gate(
-        pre, y_own, v, vbc, logs, per_head, earlier, seqs, tokens, channels
-    )
-    mixers = jnp.concatenate([gated, attended], -1)
-    by_seq = lambda array: array.reshape(seqs, tokens, -1)
+    attended, lse = attend(after(queries, sent), keyvals, at, seqs, tokens)
+    y, carried, mixers, offers = [], [], [], []
+    for s in each:
+        here = gate(pre, cols, y_own, v, vbc, logs, per_head, earlier, s, tokens)
+        y.append(here[1])
+        carried.append(here[2])
+        mixers.append(
+            jnp.concatenate([here[0], attended[tokens * s : tokens * (s + 1)]], -1)
+        )
+        offers.append(
+            offer(jnp.einsum("ti,di->td", mixers[s], out_full_w, preferred_element_type=f32))
+        )
 
     mask_float = valid_mask.astype(f32)[..., None]
     loss_scale = 1.0 / (valid_total * width)
     squares_local = jnp.zeros((), f32)
-    each = range(seqs)
-    resid, normed_two, gateup, inner, out_full = [], [], [], [], []
-    mixed = [
-        pair_sum(
-            jnp.einsum("ti,di->td", by_seq(mixers)[s], out_full_w, preferred_element_type=f32)
-        )
-        for s in each
-    ]
+    resid, normed_two, gateup, inner = [], [], [], []
+    down_offers = []
     for s in each:
-        resid.append(hidden[s] + mixed[s])
+        mine, other = offers[s]
+        other = after(other, offers[-1][0], *(d[0] for d in down_offers))
+        resid.append(hidden[s] + summed_pair(mine, other))
         normed_two.append(rms_norm(resid[s], ffn_gain).astype(low))
         gateup.append(jnp.dot(normed_two[s], gateup_full, preferred_element_type=f32))
         inner.append(
             (jax.nn.silu(gateup[s][:, :hidden_units]) * gateup[s][:, hidden_units:]).astype(low)
         )
-    down = [
-        pair_sum(jnp.einsum("tf,df->td", inner[s], down_full, preferred_element_type=f32))
-        for s in each
-    ]
-    out_grad, down_in, gateup_low = [], [], []
+        down_offers.append(
+            offer(jnp.einsum("tf,df->td", inner[s], down_full, preferred_element_type=f32))
+        )
+    out_full, out_grad, down_in, gateup_low, back_offers = [], [], [], [], []
 
     def swiglu_flat(both):
         return jax.nn.silu(both[:, :hidden_units]) * both[:, hidden_units:]
 
     for s in each:
-        out_full.append(resid[s] + down[s])
+        mine, other = down_offers[s]
+        other = after(other, down_offers[-1][0], *(d[0] for d in back_offers))
+        out_full.append(resid[s] + summed_pair(mine, other))
         diff = out_full[s] - teacher[s].astype(f32)
         squares_local = squares_local + jnp.sum(mask_float[s] * diff * diff)
         out_grad.append(cotangent[s].astype(f32) + mask_float[s] * 2.0 * diff * loss_scale)
         down_in.append(out_grad[s].astype(low))
         inner_grad = jnp.einsum("td,df->tf", down_in[s], down_full, preferred_element_type=f32)
         gateup_low.append(jax.vjp(swiglu_flat, gateup[s])[1](inner_grad)[0].astype(low))
-    normed_two_part = [
-        jnp.einsum("tc,dc->td", gateup_low[s], gateup_full, preferred_element_type=f32)
-        for s in each
-    ]
-    normed_two_grad = [pair_sum(normed_two_part[s]) for s in each]
+        back_offers.append(
+            offer(jnp.einsum("tc,dc->td", gateup_low[s], gateup_full, preferred_element_type=f32))
+        )
     block_out = jnp.stack(out_full).astype(low)
 
     def wgrad(left, right):
         return jnp.einsum("td,tc->dc", left, right, preferred_element_type=f32).astype(low)
 
     join = lambda parts: jnp.concatenate(parts, 0)
-    ffn_terms = jnp.concatenate(
-        [
-            wgrad(join(normed_two), join(gateup_low)),
-            wgrad(join(down_in), join(inner)),
-        ],
-        1,
-    )
+    ffn_wgrads = [
+        wgrad(join(normed_two), join(gateup_low)),
+        wgrad(join(down_in), join(inner)),
+    ]
+
+    ffn_terms = jnp.concatenate(ffn_wgrads, 1)
     ffn_reduced = lax.psum_scatter(ffn_terms, owners, scatter_dimension=0, tiled=True)
 
-    resid_grad, ffn_gain_grad = [], 0.0
+    resid_grad, mixed_low, ffn_gain_grad = [], [], 0.0
+    dy, dz, skip_rows, mixers_grads = [], [], [], []
+    sent_back = None
     for s in each:
-        back = jax.vjp(rms_norm, resid[s], ffn_gain)[1](normed_two_grad[s])
+        mine, other = back_offers[s]
+        other = after(other, ffn_terms, *([sent_back] if s else []))
+        back = jax.vjp(rms_norm, resid[s], ffn_gain)[1](summed_pair(mine, other))
         resid_grad.append(out_grad[s] + back[0])
         ffn_gain_grad = ffn_gain_grad + back[1]
-    resid_grad = jnp.concatenate(resid_grad, 0)
-    mixed_low = resid_grad.astype(low)
-    out_wgrad = wgrad(mixed_low, mixers)
-    mixers_grad = jnp.dot(mixed_low, out_full_w, preferred_element_type=f32)
-
-    dy, dz, sent_back, skip_rows = gate_back(
-        mixers_grad, pre, y, v, vbc, logs, per_head, sent, seqs, tokens, channels
-    )
+        mixed_low.append(resid_grad[s].astype(low))
+        mixers_grads.append(jnp.dot(mixed_low[s], out_full_w, preferred_element_type=f32))
+        *here, sent_back = gate_back(
+            mixers_grads[s], pre, cols, y[s], v, vbc, logs, per_head, sent, s, seqs, tokens,
+            sent_back,
+        )
+        dy.append(here[0])
+        dz.append(here[1])
+        skip_rows.append(here[2])
     later = [passed_along(sent_back, "ctx", -d) for d in range(1, hops)]
-    query_back, *keyval_parts = attend_back(
-        queries, keyvals, mixers_grad, channels, attended, lse, cosine, sine, at, seqs, tokens
-    )
+    query_back, keyval_parts = [], [None] * hops
+    for s in each:
+        gq, *keyval_parts = attend_back(
+            queries, keyvals, after(mixers_grads[s], sent_back), channels, attended, lse,
+            cosine, sine, at, s, seqs, tokens, keyval_parts,
+        )
+        query_back.append(gq)
     keyval_parts = [keyval_parts[0]] + [
         passed_along(keyval_parts[d], "ctx", -d) for d in range(1, hops)
     ]
-    dx, dbc, dstep, edge, head, conv_rows, conv_bc_rows, head_rows = scan_back(
-        dy, y, v, vbc, pre, tails, taps, taps_bc, per_head, logs, states, carried, later,
-        seqs, tokens, channels, heads,
-    )
+    out_wgrad = wgrad(join(mixed_low), join(mixers))
+    early_terms, part = early_grads(
+        after(normed_t, *later), mixer_both, cols, [[dz[s], query_back[s]] for s in each], seqs
+    )
+    early_terms = jnp.concatenate([early_terms, out_wgrad], 1)
+    early_reduced = lax.psum_scatter(early_terms, owners, scatter_dimension=0, tiled=True)
+    scan_backs = []
+    for s in each:
+        scan_backs.append(
+            scan_back(
+                after(dy[s], early_terms), y[s], v, vbc, pre, cols, tails, taps, taps_bc, per_head,
+                logs, states, carried[s], later, s, tokens, heads,
+            )
+        )
     keyval_back = keyval_sum(keyval_parts, cosine, sine, seqs, tokens)
-    mended = (edge + passed_along(head, "ctx", -1)).astype(low)
-    pre_grad = jnp.concatenate([dz, dx, dbc, query_back, keyval_back, dstep], -1)
-    for s in each:
-        pre_grad = lax.dynamic_update_slice(
-            pre_grad, mended[8 * s : 8 * s + 8], (tokens * (s + 1) - 8, channels)
-        )
-    mixer_terms = jnp.concatenate([wgrad(normed, pre_grad), out_wgrad], 1)
-    mixer_reduced = lax.psum_scatter(mixer_terms, owners, scatter_dimension=0, tiled=True)
-    normed_part = jnp.einsum("tc,dc->td", pre_grad, mixer_full, preferred_element_type=f32)
-    hidden_rows = hidden.reshape(seqs * tokens, width)
-    _, norm_one_back = jax.vjp(rms_norm, hidden_rows, mixer_gain)
-    mixer_gain_grad = norm_one_back(normed_part)[1]
-    normed_grad = join([pair_sum(by_seq(normed_part)[s]) for s in each])
-    input_grad = (resid_grad + norm_one_back(normed_grad)[0]).astype(low)
+    head = passed_along(join([scan_backs[s][4] for s in each]), "ctx", -1)
+    late_terms, part = late_grads(
+        normed_t, mixer_both, cols, after(part, ffn_reduced), keyval_back,
+        [[*scan_backs[s][:4], head] for s in each], seqs,
+    )
+    part = [part[tokens * s : tokens * (s + 1)] for s in each]
+    part_other = [swapped(p, "tp", 1) for p in part]
+    own, sends, got = spread(core_sum(late_terms), "ctx", 1, 1)
+
+    hidden_rows = [hidden[s] for s in each]
+    norm_one_back = [jax.vjp(rms_norm, hidden_rows[s], mixer_gain)[1] for s in each]
+    mixer_gain_grad = sum(norm_one_back[s](part[s].astype(f32))[1] for s in each)
 
     tp_index = lax.axis_index("tp")
     tp_count = lax.axis_size("tp")
@@ -895,39 +1111,55 @@
     def narrow(wide, axis_dim, piece_size):
         return lax.dynamic_slice_in_dim(wide, tp_index * piece_size, piece_size, axis_dim)
 
-    over_seqs = lambda array: jnp.sum(array.reshape(seqs, 8, -1), 0)
-    conv_sum, conv_bc_sum, head_sum = map(over_seqs, (conv_rows, conv_bc_rows, head_rows))
-    skip_grad = jnp.sum(over_seqs(skip_rows)[0].reshape(heads, MP), -1)
-    summed = lax.psum(
-        (
-            mixer_gain_grad,
-            ffn_gain_grad / tp_count,
-            widen(conv_sum[: KC + 1], 1),
-            conv_bc_sum[: KC + 1],
-            widen(jnp.stack([head_sum[0, :heads], head_sum[1, :heads], skip_grad]), 1),
-            squares_local / tp_count,
-        ),
-        ("dp", "ctx", "tp"),
-    )
+    conv_sum, conv_bc_sum, head_sum = (
+        sum(scan_backs[s][i] for s in each) for i in (5, 6, 7)
+    )
+    skip_grad = jnp.sum(sum(skip_rows[s][0] for s in each).reshape(heads, MP), -1)
+    small = [
+        mixer_gain_grad,
+        ffn_gain_grad / tp_count,
+        widen(conv_sum[: KC + 1], 1),
+        conv_bc_sum[: KC + 1],
+        widen(jnp.stack([head_sum[0, :heads], head_sum[1, :heads], skip_grad]), 1),
+        (squares_local / tp_count).reshape(1),
+    ]
+    flat = jnp.concatenate([a.reshape(-1) for a in small])
+    fill = -flat.shape[0] % 1024
+    flat = after(jnp.pad(flat, (0, fill)).reshape(-1, 128), *sends)
+    flat = sum_over(flat, ("ctx",))
+    held = after(added(own, got).astype(low), part_other[0], flat)
+    own, sends, got = spread(held, "dp", 0, 0)
+    flat = sum_over(after(flat, *sends), ("tp", "dp"))
+    late_reduced = added(own, [after(got[0], flat), *got[1:]])
+    flat = flat.reshape(-1)
+    input_grad = []
+    for s in each:
+        other = part_other[s] if s == 0 else after(part_other[s], *sends)
+        back = norm_one_back[s](summed_pair(part[s], other))[0]
+        input_grad.append((resid_grad[s] + back).astype(low))
+    summed, start = [], 0
+    for a in small:
+        summed.append(flat[start : start + a.size].reshape(a.shape))
+        start += a.size
     conv_total = narrow(summed[2], 1, channels)
     head_total = narrow(summed[4], 1, heads)
-    loss = summed[5] * loss_scale
-    reduced = mixer_reduced.astype(f32)
+    loss = summed[5][0] * loss_scale
     ffn_reduced = ffn_reduced.astype(f32)
-    piece = [reduced[:, edges[i] : edges[i + 1]] for i in range(7)]
-    state_reduced = pair_sum(piece[2])
-    out_reduced = reduced[:, all_cols:]
+    early_reduced = after(early_reduced, late_reduced).astype(f32)
+    out_reduced = early_reduced[:, channels + q_cols :]
+    state_reduced = summed_pair(*offer(late_reduced[:, channels : channels + bc_cols]))
+    rest = late_reduced[:, channels + bc_cols :]
     return (
         block_out,
         loss,
-        input_grad.reshape(seqs, tokens, width),
+        jnp.stack(input_grad),
         summed[0],
-        piece[3],
-        jnp.stack([piece[4], piece[5]], 1),
+        early_reduced[:, channels : channels + q_cols],
+        jnp.stack([rest[:, :kv_cols], rest[:, kv_cols : 2 * kv_cols]], 1),
         out_reduced[:, channels:].T,
-        reduced[:, : 2 * channels].reshape(rows, 2, channels),
+        jnp.stack([early_reduced[:, :channels], late_reduced[:, :channels]], 1),
         state_reduced,
-        piece[6],
+        rest[:, 2 * kv_cols : 2 * kv_cols + heads],
         conv_total[:KC],
         conv_total[KC],
         summed[3][:KC],

time: 555 us -> 497 us (0.90)
  blocking collectives: 68.8 us -> 0 us
  Pallas kernels: 76.8 us -> 109 us
  waiting for transfers between devices: 185 us -> 156 us
  matrix products: 71.5 us -> 50.5 us
  starting transfers between devices: 36.8 us -> 55.9 us
  other arithmetic: 47.7 us -> 56.1 us
    psum x1 -> x0, blocking collectives: 68.8 us -> none  [per_device(): lax.psum((mixer_gain_grad, ffn_gain_grad / tp_count, widen(conv_sum[:KC +...]
    ppermute x23 -> x33, waiting for transfers between devices: 137 us -> 82.9 us  [the longest x19 70.2 us: swapped(): return lax.ppermute(array, axis, [(i, i ^ distance) for i in devices])]
    pallas_call x8 -> x14, Pallas kernels: 76.8 us -> 109 us  [the longest x12 89.1 us: run(): pl.pallas_call(inner, grid=(seqs,), in_specs=specs, out_specs=out_specs,...]
    ppermute x23 -> x33, starting transfers between devices: 36.7 us -> 55.5 us  [the longest x19 28.9 us: swapped(): return lax.ppermute(array, axis, [(i, i ^ distance) for i in devices])]
    dot_general x4 -> x3, matrix products: 26.4 us -> 8.89 us  [wgrad(): jnp.einsum('td,tc->dc', left, right, preferred_element_type=f32).astype(low)]
    reduce_scatter x1, waiting for transfers between devices: 0.01 us -> 14 us  [per_device(): lax.psum_scatter(early_terms, owners, scatter_dimension=0, tiled=True)]
    unnamed x167 -> x151, local copies, waits for them, and re-layouts: 24.7 us -> 12.3 us
    all_gather x1, waiting for transfers between devices: 47.8 us -> 59.2 us  [per_device(): mixer_both = lax.all_gather(mixer_shard, owners, axis=0, tiled=True)]
  transfers between devices with their start and end apart: 27 -> 37, of which waited for: 12 -> 13; matrix products, arithmetic and copies ran while one was open for 19% -> 24% of each run, Pallas kernels for 14% -> 20%
where the time goes in v3:
time: 497 us; the launch traced here: 489 us
  waiting for transfers between devices  156 us (31%)
  Pallas kernels  109 us (22%)
  other arithmetic  56.1 us (11%)
  starting transfers between devices  55.9 us (11%)
  matrix products  50.5 us (10%)
  local copies, waits for them, and re-layouts  42.3 us (9%)
  between operations  19.4 us (4%)
    pallas_call x12, Pallas kernels, run(): pl.pallas_call(inner, grid=(seqs,), in_specs=specs, out_specs=out_specs,...  89.1 us
    ppermute x19, waiting for transfers between devices, swapped(): return lax.ppermute(array, axis, [(i, i ^ distance) for i in devices])  70.2 us
    all_gather x1, waiting for transfers between devices, per_device(): mixer_both = lax.all_gather(mixer_shard, owners, axis=0, tiled=True)  59.2 us
    ppermute x19, starting transfers between devices, swapped(): return lax.ppermute(array, axis, [(i, i ^ distance) for i in devices])  28.9 us
    ppermute x14, starting transfers between devices, passed_along(): return lax.ppermute(array, axis, route)  26.6 us
    pallas_call x2, Pallas kernels, tiled_grads(): pl.pallas_call(body, grid=(tiles,), in_specs=[whole(left.shape), pl.Block...  19.5 us
    reduce_scatter x1, waiting for transfers between devices, per_device(): lax.psum_scatter(early_terms, owners, scatter_dimension=0, tiled=True)  14 us
    ppermute x14, waiting for transfers between devices, passed_along(): return lax.ppermute(array, axis, route)  12.7 us
  transfers between devices with their start and end apart: 37, of which 13 were waited for; matrix products, arithmetic and copies ran while one was open for 24% of the time, Pallas kernels for 20%

profile of v3, /device:TPU:0, one launch (start us, length us, event | category | flops | bytes accessed | tf_op | source)
XLA Modules:
  0.0 488.9 jit_solution(10497579628891282556)
XLA Ops:
  11.2 1.9 concatenate.56
  21.8 59.2 %all-gather.3.cloned.1.call-done.weight_ref = bf16[1024,3328]{1,0:T(8,128)(2,1)} async-done(((bf16[64,3328]{1,0:T(8,128)(2,1)}), bf16[1024,3328]{1,0:T(8,128)(2,1)}) %all-gather.3.cloned.1.call-update) | async-done | bytes 6815760 | tf_op jit(solution)/shard_map/all_gather | solution.py:939
  80.9 6.7 %fusion.refs_0_.refs_1_.refs_2_.refs_4_.refs_5_.refs_6_ = f32[768,2304]{1,0:T(8,128)S(1)} fusion(bf16[768,1024]{0,1:T(8,128)(2,1)} %copy.95, bf16[1024,3328]{1,0:T(8,128)(2,1)} %all-gather.3.cloned.1.call-done.weight_ref), kind=kOutput, calls=%fused_computation.1 | convolution fusion | flops 3623878656 | bytes 13369344 | tf_op jit(solution)/shard_map/dot_general | solution.py:967
  87.7 2.9 copy-done
  90.5 2.7 shard_map.384
  93.2 2.2 collective-permute-start.4
  95.4 2.5 collective-permute-start.5
  102.0 10.6 %shard_map.382 = (f32[768,768]{1,0:T(8,128)}, f32[768,256]{1,0:T(8,128)}, f32[768,768]{1,0:T(8,128)}, f32[768,128]{1,0:T(8,128)}, f32[768,768]{1,0:T(8,128)}, /*index=5*/bf16[288,768]{1,0:T(8,128)(2,1)}) custom-call(f32[768,2304]{1,0:T(8,128)} %copy-done, f32[768,2304]{1,0:T(8,128)} %copy-done, f32[768,2304]{1,0:T(8,128)} %copy-done, f32[16,1024]{1,0:T(8,128)} %copy-done.28, ...), custom_call_target="tpu_custom_call" | custom-call | flops 603979776 | bytes 21401600 | tf_op jit(solution)/shard_map/pallas_call | solution.py:487
  112.6 4.1 collective-permute-start.1
  116.7 4.3 collective-permute-start.2
  123.1 10.3 %shard_map.385 = (bf16[768,256]{1,0:T(8,128)(2,1)}, f32[768,128]{1,0:T(8,128)}) custom-call(s32[1]{0:T(128)} %bitcast.14.refs_0_, bf16[768,256]{1,0:T(8,128)(2,1)} %get-tuple-element.116.refs_1_, bf16[768,128]{1,0:T(8,128)(2,1)} %get-tuple-element.117.refs_2_.refs_7_, bf16[768,128]{1,0:T(8,128)(2,1)} %copy-done.69, bf16[768,128]{1,0:T(8,128)(2,1)} %copy-done.70, ...), custom_call_target="tpu_custom_call" | custom-call | flops 4831838208 | bytes 1179652 | tf_op jit(solution)/shard_map/pallas_call | solution.py:487
  134.5 4.0 collective-permute-done.2.refs_7_
  138.5 8.6 %collective-permute-done.3.refs_8_ = bf16[288,768]{1,0:T(8,128)(2,1)S(1)} collective-permute-done((bf16[288,768]{1,0:T(8,128)(2,1)}, bf16[288,768]{1,0:T(8,128)(2,1)S(1)}, u32[]{:S(2)}, u32[]{:S(2)}) %collective-permute-start.3) | collective-permute-done | bytes 442400 | tf_op jit(solution)/shard_map/ppermute | solution.py:803
  147.9 4.7 shard_map.383
  152.6 3.9 convolution_convert_fusion.6
  160.8 4.6 shard_map.386
  165.4 3.7 convolution_convert_fusion.5
  169.4 7.9 %collective-permute-done.7 = bf16[384,1024]{1,0:T(8,128)(2,1)} collective-permute-done((bf16[384,1024]{1,0:T(8,128)(2,1)}, bf16[384,1024]{1,0:T(8,128)(2,1)}, u32[]{:S(2)}, u32[]{:S(2)}) %collective-permute-start.7) | collective-permute-done | bytes 786464 | tf_op jit(solution)/shard_map/ppermute | solution.py:812
  181.3 4.4 fusion.11
  189.0 5.1 %collective-permute-done.9 = bf16[384,1024]{1,0:T(8,128)(2,1)} collective-permute-done((bf16[384,1024]{1,0:T(8,128)(2,1)}, bf16[384,1024]{1,0:T(8,128)(2,1)}, u32[]{:S(2)}, u32[]{:S(2)}) %collective-permute-start.9) | collective-permute-done | bytes 786464 | tf_op jit(solution)/shard_map/ppermute | solution.py:812
  194.1 2.0 multiply_reduce_fusion.5
  196.3 1.8 fusion.9
  201.4 9.5 %collective-permute-done.8 = bf16[384,1024]{1,0:T(8,128)(2,1)S(1)} collective-permute-done((bf16[384,1024]{1,0:T(8,128)(2,1)S(1)}, bf16[384,1024]{1,0:T(8,128)(2,1)S(1)}, u32[]{:S(2)}, u32[]{:S(2)}) %collective-permute-start.8) | collective-permute-done | bytes 786464 | tf_op jit(solution)/shard_map/ppermute | solution.py:812
  213.6 2.7 fusion.53
  216.3 9.9 %collective-permute-done.10 = bf16[384,1024]{1,0:T(8,128)(2,1)S(1)} collective-permute-done((bf16[384,1024]{1,0:T(8,128)(2,1)S(1)}, bf16[384,1024]{1,0:T(8,128)(2,1)S(1)}, u32[]{:S(2)}, u32[]{:S(2)}) %collective-permute-start.10) | collective-permute-done | bytes 786464 | tf_op jit(solution)/shard_map/ppermute | solution.py:812
  227.1 1.8 convolution_convert_fusion.2
  231.7 3.7 convolution_convert_fusion
  235.5 3.2 pad_maximum_fusion
  240.8 5.5 %fusion.56 = bf16[384,1024]{1,0:T(8,128)(2,1)} fusion(bf16[384,2048]{1,0:T(8,128)(2,1)} %copy-done.36, bf16[1024,3072]{1,0:T(8,128)(2,1)} %all-gather.5.cloned.1.call-done), kind=kOutput, calls=%fused_computation.106 | convolution fusion | flops 1611005952 | bytes 6553600 | tf_op jit(solution)/shard_map/tc,dc->td/dot_general | solution.py:1027
  246.6 13.2 %collective-permute-done.12 = bf16[384,1024]{1,0:T(8,128)(2,1)} collective-permute-done((bf16[384,1024]{1,0:T(8,128)(2,1)}, bf16[384,1024]{1,0:T(8,128)(2,1)}, u32[]{:S(2)}, u32[]{:S(2)}) %collective-permute-start.12) | collective-permute-done | bytes 786464 | tf_op jit(solution)/shard_map/ppermute | solution.py:812
  259.8 3.0 multiply_reduce_fusion.4
  262.9 3.7 fusion.100
  266.6 4.0 fusion.67.refs_0_.refs_2_
  270.6 5.2 %shard_map.387 = (f32[384,768]{1,0:T(8,128)}, bf16[384,768]{1,0:T(8,128)(2,1)}, f32[8,768]{1,0:T(8,128)}, bf16[288,768]{1,0:T(8,128)(2,1)}) custom-call(f32[384,1024]{1,0:T(8,128)} %fusion.67.refs_0_.refs_2_, f32[768,2304]{1,0:T(8,128)} %copy-done, f32[384,768]{1,0:T(8,128)} %get-tuple-element.126.refs_2_.refs_1_, ...), custom_call_target="tpu_custom_call" | custom-call | flops 150994944 | bytes 13815808 | tf_op jit(solution)/shard_map/pallas_call | solution.py:487
  275.8 3.2 multiply_reduce_fusion.3
  279.1 3.9 fusion.98
  283.0 4.0 fusion.65.refs_0_.refs_2_
  287.0 5.2 %shard_map.388 = (f32[384,768]{1,0:T(8,128)}, bf16[384,768]{1,0:T(8,128)(2,1)}, f32[8,768]{1,0:T(8,128)}, bf16[288,768]{1,0:T(8,128)(2,1)}) custom-call(f32[384,1024]{1,0:T(8,128)} %fusion.65.refs_0_.refs_2_, f32[768,2304]{1,0:T(8,128)} %copy-done, f32[384,768]{1,0:T(8,128)} %get-tuple-element.129.refs_2_.refs_1_, ...), custom_call_target="tpu_custom_call", output_to_operand_aliasing={{3}: (8, {})} | custom-call | flops 150994944 | bytes 13815808 | tf_op jit(solution)/shard_map/pallas_call | solution.py:487
  296.5 10.4 %shard_map.389 = (bf16[384,256]{1,0:T(8,128)(2,1)}, bf16[768,128]{1,0:T(8,128)(2,1)}, bf16[768,128]{1,0:T(8,128)(2,1)}, bf16[768,128]{1,0:T(8,128)(2,1)}, bf16[768,128]{1,0:T(8,128)(2,1)}) custom-call(s32[1]{0:T(128)} %bitcast.14.refs_0_, bf16[768,256]{1,0:T(8,128)(2,1)} %get-tuple-element.116.refs_1_, f32[384,1024]{1,0:T(8,128)} %fusion.67.refs_0_.refs_2_, ...), custom_call_target="tpu_custom_call" | custom-call | flops 6039797760 | bytes 4325380 | tf_op jit(solution)/shard_map/pallas_call | solution.py:487
  306.9 10.8 %shard_map.390 = (bf16[384,256]{1,0:T(8,128)(2,1)}, bf16[768,128]{1,0:T(8,128)(2,1)}, bf16[768,128]{1,0:T(8,128)(2,1)}, bf16[768,128]{1,0:T(8,128)(2,1)}, bf16[768,128]{1,0:T(8,128)(2,1)}) custom-call(s32[1]{0:T(128)} %bitcast.14.refs_0_, ...), custom_call_target="tpu_custom_call", output_to_operand_aliasing={{1}: (11, {}), {2}: (12, {}), {3}: (13, {}), {4}: (14, {})} | custom-call | flops 6039797760 | bytes 4325380 | tf_op jit(solution)/shard_map/pallas_call | solution.py:487
  320.3 3.3 convolution_convert_fusion.1
  325.0 8.9 %shard_map.391 = (bf16[1024,1024]{1,0:T(8,128)(2,1)}, f32[768,1024]{1,0:T(8,128)}) custom-call(bf16[1024,768]{1,0:T(8,128)(2,1)} %bitcast.165, bf16[1024,3328]{1,0:T(8,128)(2,1)} %all-gather.3.cloned.1.call-done.weight_ref, bf16[384,768]{1,0:T(8,128)(2,1)} %get-tuple-element.132.refs_0_, bf16[384,256]{1,0:T(8,128)(2,1)} %get-tuple-element.135.refs_1_, ...), custom_call_target="tpu_custom_call" | custom-call | flops 3221225472 | bytes 4194304 | tf_op jit(solution)/shard_map/pallas_call | solution.py:759
  334.0 4.0 pad_maximum_fusion.1
  338.0 11.1 %shard_map.393 = (bf16[384,768]{1,0:T(8,128)(2,1)}, bf16[384,256]{1,0:T(8,128)(2,1)}, bf16[384,128]{1,0:T(8,128)(2,1)}, f32[16,1024]{1,0:T(8,128)}, f32[16,1024]...) custom-call(f32[384,768]{1,0:T(8,128)} %get-tuple-element.151.refs_0_, ...), custom_call_target="tpu_custom_call" | custom-call | flops 1132462080 | bytes 31379456 | tf_op jit(solution)/shard_map/pallas_call | solution.py:487
  349.1 11.4 %shard_map.394 = (bf16[384,768]{1,0:T(8,128)(2,1)}, bf16[384,256]{1,0:T(8,128)(2,1)}, bf16[384,128]{1,0:T(8,128)(2,1)}, f32[16,1024]{1,0:T(8,128)}, f32[16,1024]...) custom-call(f32[384,768]{1,0:T(8,128)} %get-tuple-element.160.refs_0_, ...), custom_call_target="tpu_custom_call" | custom-call | flops 1132462080 | bytes 31379456 | tf_op jit(solution)/shard_map/pallas_call | solution.py:487
  364.1 2.3 shard_map.392.keyval_ref
  366.4 10.6 %shard_map.395 = (bf16[1024,1280]{1,0:T(8,128)(2,1)}, bf16[768,1024]{1,0:T(8,128)(2,1)}) custom-call(bf16[1024,768]{1,0:T(8,128)(2,1)} %bitcast.166, bf16[1024,3328]{1,0:T(8,128)(2,1)} %all-gather.3.cloned.1.call-done.weight_ref, f32[768,1024]{1,0:T(8,128)} %get-tuple-element.144.start_ref, bf16[768,128]{1,0:T(8,128)(2,1)} %shard_map.392.keyval_ref, ...), custom_call_target="tpu_custom_call" | custom-call | flops 4026531840 | bytes 5242880 | tf_op jit(solution)/shard_map/pallas_call | solution.py:759
  377.0 3.0 constant_dynamic-slice_fusion.1
  381.1 3.4 collective-permute-start.20
  387.9 2.7 fusion.102
  390.6 1.9 collective-permute-start.24
  392.5 3.0 fusion.13
  395.5 2.0 dynamic-slice_bitcast_fusion
  399.4 2.8 pad_maximum_fusion.2
  404.6 2.3 reshape.327
  406.9 8.0 %collective-permute-done.22 = f32[88,128]{1,0:T(8,128)S(1)} collective-permute-done((f32[88,128]{1,0:T(8,128)S(1)}, f32[88,128]{1,0:T(8,128)S(1)}, u32[]{:S(2)}, u32[]{:S(2)}) %collective-permute-start.22) | collective-permute-done | bytes 45088 | tf_op jit(solution)/shard_map/ppermute | solution.py:812
  417.3 3.3 collective-permute-start.31
  421.9 5.9 %collective-permute-done.28 = bf16[384,1024]{1,0:T(8,128)(2,1)} collective-permute-done((bf16[384,1024]{1,0:T(8,128)(2,1)}, bf16[384,1024]{1,0:T(8,128)(2,1)}, u32[]{:S(2)}, u32[]{:S(2)}) %collective-permute-start.28) | collective-permute-done | bytes 786464 | tf_op jit(solution)/shard_map/ppermute | solution.py:812
  427.9 2.1 multiply_reduce_fusion.2
  431.8 2.3 fusion.73
  434.1 5.1 %collective-permute-done.26 = f32[88,128]{1,0:T(8,128)S(1)} collective-permute-done((f32[88,128]{1,0:T(8,128)S(1)}, f32[88,128]{1,0:T(8,128)S(1)}, u32[]{:S(2)}, u32[]{:S(2)}) %collective-permute-start.26) | collective-permute-done | bytes 45088 | tf_op jit(solution)/shard_map/ppermute | solution.py:812
  439.2 6.2 %collective-permute-start.27 = (f32[88,128]{1,0:T(8,128)S(1)}, f32[88,128]{1,0:T(8,128)S(1)}, u32[]{:S(2)}, u32[]{:S(2)}) collective-permute-start(f32[88,128]{1,0:T(8,128)S(1)} %add.244), channel_id=1, source_target_pairs={{0,16},{8,24},{16,0},{24,8},{1,17},{9,25},{17,1},{25,9},{2,18},{10... | collective-permute-start | bytes 135176 | tf_op jit(solution)/shard_map/ppermute | solution.py:812
  446.7 5.6 %collective-permute-done.27 = f32[88,128]{1,0:T(8,128)S(1)} collective-permute-done((f32[88,128]{1,0:T(8,128)S(1)}, f32[88,128]{1,0:T(8,128)S(1)}, u32[]{:S(2)}, u32[]{:S(2)}) %collective-permute-start.27) | collective-permute-done | bytes 45088 | tf_op jit(solution)/shard_map/ppermute | solution.py:812
  458.6 14.0 %reduce-scatter.5.cloned.1.call-done = bf16[64,2048]{1,0:T(8,128)(2,1)} async-done(((bf16[1024,2048]{1,0:T(8,128)(2,1)}), bf16[64,2048]{1,0:T(8,128)(2,1)}) %reduce-scatter.5.cloned.1.call-update) | async-done | bytes 262160 | tf_op jit(solution)/shard_map/reduce_scatter | solution.py:1077
  (321 shorter events, 83.5 us)
Async XLA Ops:
  7.2 73.7 %all-gather.3.cloned.1.call-start = ((), (), s32[]{:S(2)}) async-start(), calls=%async_computation.2 | async-start | bytes 7241728 | tf_op jit(solution)/shard_map/all_gather | solution.py:939
  13.1 168.2 %all-gather.5.cloned.1.call-start = ((), (), s32[]{:S(2)}) async-start(), calls=%async_computation.3 | async-start | bytes 6684672 | tf_op jit(solution)/shard_map/all_gather | solution.py:944
  14.0 352.4 %reduce-scatter.3.cloned.1.call-start = ((), (), s32[]{:S(2)}) async-start(), calls=%async_computation.4 | async-start | bytes 6684672 | tf_op jit(solution)/shard_map/reduce_scatter | solution.py:1041
  90.5 10.2 %copy-start.66 = (f32[12]{0:T(128)S(1)}, f32[12]{0:T(128)}, u32[]{:S(2)}) copy-start(f32[12]{0:T(128)} %param.43) | copy-start | bytes 148
  90.5 10.2 %copy-start.67 = (f32[12]{0:T(128)S(1)}, f32[12]{0:T(128)}, u32[]{:S(2)}) copy-start(f32[12]{0:T(128)} %param.41) | copy-start | bytes 148
  93.2 27.8 %collective-permute-start.4 = (bf16[768,128]{1,0:T(8,128)(2,1)}, bf16[768,128]{1,0:T(8,128)(2,1)S(1)}, u32[]{:S(2)}, u32[]{:S(2)}) collective-permute-start(bf16[768,128]{1,0:T(8,128)(2,1)} %get-tuple-element.117.refs_2_.refs_7_), channel_id=1, source_target_pairs={{0,2},{2,4},{4,6},{1,3},{3,5},{5,7},{8,10},{10,12},{12,14},{9,11},... | collective-permute-start | bytes 589832 | tf_op jit(solution)/shard_map/ppermute | solution.py:803
  95.4 27.0 %collective-permute-start.5 = (bf16[768,128]{1,0:T(8,128)(2,1)}, bf16[768,128]{1,0:T(8,128)(2,1)S(1)}, u32[]{:S(2)}, u32[]{:S(2)}) collective-permute-start(bf16[768,128]{1,0:T(8,128)(2,1)} %get-tuple-element.117.refs_2_.refs_7_), channel_id=1, source_target_pairs={{0,4},{2,6},{1,5},{3,7},{8,12},{10,14},{9,13},{11,15},{16,20},{18,... | collective-permute-start | bytes 589832 | tf_op jit(solution)/shard_map/ppermute | solution.py:803
  97.9 24.5 %collective-permute-start.6 = (bf16[768,128]{1,0:T(8,128)(2,1)}, bf16[768,128]{1,0:T(8,128)(2,1)S(1)}, u32[]{:S(2)}, u32[]{:S(2)}) collective-permute-start(bf16[768,128]{1,0:T(8,128)(2,1)} %get-tuple-element.117.refs_2_.refs_7_), channel_id=1, source_target_pairs={{0,6},{1,7},{8,14},{9,15},{16,22},{17,23},{24,30},{25,31}} | collective-permute-start | bytes 589832 | tf_op jit(solution)/shard_map/ppermute | solution.py:803
  99.2 2.2 collective-permute-start
  112.6 21.8 %collective-permute-start.1 = (bf16[288,768]{1,0:T(8,128)(2,1)}, bf16[288,768]{1,0:T(8,128)(2,1)S(1)}, u32[]{:S(2)}, u32[]{:S(2)}) collective-permute-start(bf16[288,768]{1,0:T(8,128)(2,1)} %get-tuple-element.113.refs_7_), channel_id=1, source_target_pairs={{0,2},{2,4},{4,6},{1,3},{3,5},{5,7},{8,10},{10,12},{12,14},{9,11},... | collective-permute-start | bytes 1327112 | tf_op jit(solution)/shard_map/ppermute | solution.py:803
  116.7 21.7 %collective-permute-start.2 = (bf16[288,768]{1,0:T(8,128)(2,1)}, bf16[288,768]{1,0:T(8,128)(2,1)S(1)}, u32[]{:S(2)}, u32[]{:S(2)}) collective-permute-start(bf16[288,768]{1,0:T(8,128)(2,1)} %get-tuple-element.113.refs_7_), channel_id=1, source_target_pairs={{0,4},{2,6},{1,5},{3,7},{8,12},{10,14},{9,13},{11,15},{16,20},{18,... | collective-permute-start | bytes 1327112 | tf_op jit(solution)/shard_map/ppermute | solution.py:803
  121.0 26.1 %collective-permute-start.3 = (bf16[288,768]{1,0:T(8,128)(2,1)}, bf16[288,768]{1,0:T(8,128)(2,1)S(1)}, u32[]{:S(2)}, u32[]{:S(2)}) collective-permute-start(bf16[288,768]{1,0:T(8,128)(2,1)} %get-tuple-element.113.refs_7_), channel_id=1, source_target_pairs={{0,6},{1,7},{8,14},{9,15},{16,22},{17,23},{24,30},{25,31}} | collective-permute-start | bytes 1327112 | tf_op jit(solution)/shard_map/ppermute | solution.py:803
  134.4 18.1 %copy-start.44 = (bf16[384,256]{1,0:T(8,128)(2,1)}, bf16[384,256]{1,0:T(8,128)(2,1)S(1)}, u32[]{:S(2)}) copy-start(bf16[384,256]{1,0:T(8,128)(2,1)S(1)} %get-tuple-element.287) | copy-start | bytes 589828
  134.5 31.0 %copy-start.46 = (bf16[384,256]{1,0:T(8,128)(2,1)}, bf16[384,256]{1,0:T(8,128)(2,1)S(1)}, u32[]{:S(2)}) copy-start(bf16[384,256]{1,0:T(8,128)(2,1)S(1)} %get-tuple-element.288) | copy-start | bytes 589828
  134.5 12.6 %copy-start.33 = (bf16[288,768]{1,0:T(8,128)(2,1)}, bf16[288,768]{1,0:T(8,128)(2,1)S(1)}, u32[]{:S(2)}) copy-start(bf16[288,768]{1,0:T(8,128)(2,1)S(1)} %collective-permute-done.1.refs_6_) | copy-start | bytes 1327108
  156.5 20.8 %collective-permute-start.7 = (bf16[384,1024]{1,0:T(8,128)(2,1)}, bf16[384,1024]{1,0:T(8,128)(2,1)}, u32[]{:S(2)}, u32[]{:S(2)}) collective-permute-start(bf16[384,1024]{1,0:T(8,128)(2,1)} %convolution_convert_fusion.6), channel_id=1, source_target_pairs={{0,1},{1,0},{2,3},{3,2},{4,5},{5,4},{6,7},{7,6},{8,9},{9,8},{10,11... | collective-permute-start | bytes 2359304 | tf_op jit(solution)/shard_map/ppermute | solution.py:812
  169.1 11.1 %copy-start.48 = (f32[1024]{0:T(1024)S(1)}, f32[1024]{0:T(1024)}, u32[]{:S(2)}) copy-start(f32[1024]{0:T(1024)} %param.45) | copy-start | bytes 12292
  169.1 25.0 %collective-permute-start.9 = (bf16[384,1024]{1,0:T(8,128)(2,1)}, bf16[384,1024]{1,0:T(8,128)(2,1)}, u32[]{:S(2)}, u32[]{:S(2)}) collective-permute-start(bf16[384,1024]{1,0:T(8,128)(2,1)} %convolution_convert_fusion.5), channel_id=1, source_target_pairs={{0,1},{1,0},{2,3},{3,2},{4,5},{5,4},{6,7},{7,6},{8,9},{9,8},{10,11... | collective-permute-start | bytes 2359304 | tf_op jit(solution)/shard_map/ppermute | solution.py:812
  187.2 23.7 %copy-start.16 = (bf16[384,1024]{1,0:T(8,128)(2,1)}, bf16[384,1024]{1,0:T(8,128)(2,1)S(1)}, u32[]{:S(2)}) copy-start(bf16[384,1024]{1,0:T(8,128)(2,1)S(1)} %convolution_convert_fusion.4) | copy-start | bytes 2359300
  187.2 23.7 %collective-permute-start.8 = (bf16[384,1024]{1,0:T(8,128)(2,1)S(1)}, bf16[384,1024]{1,0:T(8,128)(2,1)S(1)}, u32[]{:S(2)}, u32[]{:S(2)}) collective-permute-start(bf16[384,1024]{1,0:T(8,128)(2,1)S(1)} %convolution_convert_fusion.4), channel_id=1, source_target_pairs={{0,1},{1,0},{2,3},{3,2},{4,5},{5,4},{6,7},{7,6},{8,9},{9,8},{10,11... | collective-permute-start | bytes 2359304 | tf_op jit(solution)/shard_map/ppermute | solution.py:812
  196.1 30.1 %copy-start.1 = (f32[384,1024]{1,0:T(8,128)}, f32[384,1024]{1,0:T(8,128)S(1)}, u32[]{:S(2)}) copy-start(f32[384,1024]{1,0:T(8,128)S(1)} %get-tuple-element.277) | copy-start | bytes 4718596
  198.6 12.3 %copy-start.4 = (f32[384,1024]{1,0:T(8,128)S(1)}, f32[384,1024]{1,0:T(8,128)}, u32[]{:S(2)}) copy-start(f32[384,1024]{1,0:T(8,128)} %copy-done.3) | copy-start | bytes 4718596
  198.6 12.3 %copy-start.10 = (bf16[2,384,1024]{2,1,0:T(8,128)(2,1)S(1)}, bf16[2,384,1024]{2,1,0:T(8,128)(2,1)}, u32[]{:S(2)}) copy-start(bf16[2,384,1024]{2,1,0:T(8,128)(2,1)} %param.28) | copy-start | bytes 4718596
  198.6 12.3 %copy-start.20 = (bf16[2,384,1024]{2,1,0:T(8,128)(2,1)S(1)}, bf16[2,384,1024]{2,1,0:T(8,128)(2,1)}, u32[]{:S(2)}) copy-start(bf16[2,384,1024]{2,1,0:T(8,128)(2,1)} %param.29) | copy-start | bytes 4718596
  199.6 26.5 %copy-start.12 = (bf16[384,1024]{1,0:T(8,128)(2,1)}, bf16[384,1024]{1,0:T(8,128)(2,1)S(1)}, u32[]{:S(2)}) copy-start(bf16[384,1024]{1,0:T(8,128)(2,1)S(1)} %convolution_convert_fusion.3) | copy-start | bytes 2359300
  199.6 26.5 %collective-permute-start.10 = (bf16[384,1024]{1,0:T(8,128)(2,1)S(1)}, bf16[384,1024]{1,0:T(8,128)(2,1)S(1)}, u32[]{:S(2)}, u32[]{:S(2)}) collective-permute-start(bf16[384,1024]{1,0:T(8,128)(2,1)S(1)} %convolution_convert_fusion.3), channel_id=1, source_target_pairs={{0,1},{1,0},{2,3},{3,2},{4,5},{5,4},{6,7},{7,6},{8,9},{9,8},{10,11... | collective-permute-start | bytes 2359304 | tf_op jit(solution)/shard_map/ppermute | solution.py:812
  238.7 234.0 %reduce-scatter.5.cloned.1.call-start = ((), (), s32[]{:S(2)}) async-start(), calls=%async_computation.5 | async-start | bytes 4456448 | tf_op jit(solution)/shard_map/reduce_scatter | solution.py:1077
  238.9 20.9 %collective-permute-start.12 = (bf16[384,1024]{1,0:T(8,128)(2,1)}, bf16[384,1024]{1,0:T(8,128)(2,1)}, u32[]{:S(2)}, u32[]{:S(2)}) collective-permute-start(bf16[384,1024]{1,0:T(8,128)(2,1)} %fusion.53), channel_id=1, source_target_pairs={{0,1},{1,0},{2,3},{3,2},{4,5},{5,4},{6,7},{7,6},{8,9},{9,8},{10,11... | collective-permute-start | bytes 2359304 | tf_op jit(solution)/shard_map/ppermute | solution.py:812
  240.7 19.1 %copy-start.5 = (f32[384,1024]{1,0:T(8,128)S(1)}, f32[384,1024]{1,0:T(8,128)}, u32[]{:S(2)}) copy-start(f32[384,1024]{1,0:T(8,128)} %copy-done.3) | copy-start | bytes 4718596
  240.7 19.1 %copy-start.11 = (bf16[2,384,1024]{2,1,0:T(8,128)(2,1)S(1)}, bf16[2,384,1024]{2,1,0:T(8,128)(2,1)}, u32[]{:S(2)}) copy-start(bf16[2,384,1024]{2,1,0:T(8,128)(2,1)} %param.28) | copy-start | bytes 4718596
  240.7 19.1 %copy-start.17 = (bf16[384,1024]{1,0:T(8,128)(2,1)S(1)}, bf16[384,1024]{1,0:T(8,128)(2,1)}, u32[]{:S(2)}) copy-start(bf16[384,1024]{1,0:T(8,128)(2,1)} %copy-done.16) | copy-start | bytes 2359300
  240.7 19.1 %copy-start.19 = (bf16[384,1024]{1,0:T(8,128)(2,1)S(1)}, bf16[384,1024]{1,0:T(8,128)(2,1)}, u32[]{:S(2)}) copy-start(bf16[384,1024]{1,0:T(8,128)(2,1)} %copy-done.18) | copy-start | bytes 2359300
  240.7 19.1 %copy-start.26 = (bf16[384,1024]{1,0:T(8,128)(2,1)S(1)}, bf16[384,1024]{1,0:T(8,128)(2,1)}, u32[]{:S(2)}) copy-start(bf16[384,1024]{1,0:T(8,128)(2,1)} %fusion.53) | copy-start | bytes 2359300
  246.3 16.6 %copy-start.21 = (bf16[2,384,1024]{2,1,0:T(8,128)(2,1)S(1)}, bf16[2,384,1024]{2,1,0:T(8,128)(2,1)}, u32[]{:S(2)}) copy-start(bf16[2,384,1024]{2,1,0:T(8,128)(2,1)} %param.29) | copy-start | bytes 4718596
  246.3 29.5 %collective-permute-start.11 = (bf16[384,1024]{1,0:T(8,128)(2,1)}, bf16[384,1024]{1,0:T(8,128)(2,1)}, u32[]{:S(2)}, u32[]{:S(2)}) collective-permute-start(bf16[384,1024]{1,0:T(8,128)(2,1)} %fusion.56), channel_id=1, source_target_pairs={{0,1},{1,0},{2,3},{3,2},{4,5},{5,4},{6,7},{7,6},{8,9},{9,8},{10,11... | collective-permute-start | bytes 2359304 | tf_op jit(solution)/shard_map/ppermute | solution.py:812
  292.2 31.4 %collective-permute-start.13 = (bf16[288,768]{1,0:T(8,128)(2,1)}, bf16[288,768]{1,0:T(8,128)(2,1)S(1)}, u32[]{:S(2)}, u32[]{:S(2)}) collective-permute-start(bf16[288,768]{1,0:T(8,128)(2,1)} %get-tuple-element.130), channel_id=1, source_target_pairs={{2,0},{4,2},{6,4},{3,1},{5,3},{7,5},{10,8},{12,10},{14,12},{11,9},... | collective-permute-start | bytes 1327112 | tf_op jit(solution)/shard_map/ppermute | solution.py:803
  293.5 31.5 %collective-permute-start.14 = (bf16[288,768]{1,0:T(8,128)(2,1)}, bf16[288,768]{1,0:T(8,128)(2,1)S(1)}, u32[]{:S(2)}, u32[]{:S(2)}) collective-permute-start(bf16[288,768]{1,0:T(8,128)(2,1)} %get-tuple-element.130), channel_id=1, source_target_pairs={{4,0},{6,2},{5,1},{7,3},{12,8},{14,10},{13,9},{15,11},{20,16},{22,... | collective-permute-start | bytes 1327112 | tf_op jit(solution)/shard_map/ppermute | solution.py:803
  294.8 30.2 %collective-permute-start.15 = (bf16[288,768]{1,0:T(8,128)(2,1)}, bf16[288,768]{1,0:T(8,128)(2,1)S(1)}, u32[]{:S(2)}, u32[]{:S(2)}) collective-permute-start(bf16[288,768]{1,0:T(8,128)(2,1)} %get-tuple-element.130), channel_id=1, source_target_pairs={{6,0},{7,1},{14,8},{15,9},{22,16},{23,17},{30,24},{31,25}} | collective-permute-start | bytes 1327112 | tf_op jit(solution)/shard_map/ppermute | solution.py:803
  306.9 13.4 %copy-start.38 = (bf16[384,1024]{1,0:T(8,128)(2,1)S(1)}, bf16[384,1024]{1,0:T(8,128)(2,1)}, u32[]{:S(2)}) copy-start(bf16[384,1024]{1,0:T(8,128)(2,1)} %copy-done.37) | copy-start | bytes 2359300
  306.9 13.4 %copy-start.45 = (bf16[384,256]{1,0:T(8,128)(2,1)S(1)}, bf16[384,256]{1,0:T(8,128)(2,1)}, u32[]{:S(2)}) copy-start(bf16[384,256]{1,0:T(8,128)(2,1)} %copy-done.44) | copy-start | bytes 589828
  306.9 13.4 %copy-start.47 = (bf16[384,256]{1,0:T(8,128)(2,1)S(1)}, bf16[384,256]{1,0:T(8,128)(2,1)}, u32[]{:S(2)}) copy-start(bf16[384,256]{1,0:T(8,128)(2,1)} %copy-done.46) | copy-start | bytes 589828
  317.7 45.6 %collective-permute-start.16 = (bf16[768,128]{1,0:T(8,128)(2,1)}, bf16[768,128]{1,0:T(8,128)(2,1)S(1)}, u32[]{:S(2)}, u32[]{:S(2)}) collective-permute-start(bf16[768,128]{1,0:T(8,128)(2,1)} %get-tuple-element.146), channel_id=1, source_target_pairs={{2,0},{4,2},{6,4},{3,1},{5,3},{7,5},{10,8},{12,10},{14,12},{11,9},... | collective-permute-start | bytes 589832 | tf_op jit(solution)/shard_map/ppermute | solution.py:803
  319.0 44.4 %collective-permute-start.17 = (bf16[768,128]{1,0:T(8,128)(2,1)}, bf16[768,128]{1,0:T(8,128)(2,1)S(1)}, u32[]{:S(2)}, u32[]{:S(2)}) collective-permute-start(bf16[768,128]{1,0:T(8,128)(2,1)} %get-tuple-element.147), channel_id=1, source_target_pairs={{4,0},{6,2},{5,1},{7,3},{12,8},{14,10},{13,9},{15,11},{20,16},{22,... | collective-permute-start | bytes 589832 | tf_op jit(solution)/shard_map/ppermute | solution.py:803
  323.7 10.3 %copy-start.30 = (bf16[288,768]{1,0:T(8,128)(2,1)}, bf16[288,768]{1,0:T(8,128)(2,1)S(1)}, u32[]{:S(2)}) copy-start(bf16[288,768]{1,0:T(8,128)(2,1)S(1)} %collective-permute-done.13.refs_15_) | copy-start | bytes 1327108
  323.7 39.7 %collective-permute-start.18 = (bf16[768,128]{1,0:T(8,128)(2,1)}, bf16[768,128]{1,0:T(8,128)(2,1)}, u32[]{:S(2)}, u32[]{:S(2)}) collective-permute-start(bf16[768,128]{1,0:T(8,128)(2,1)} %get-tuple-element.148), channel_id=1, source_target_pairs={{6,0},{7,1},{14,8},{15,9},{22,16},{23,17},{30,24},{31,25}} | collective-permute-start | bytes 589832 | tf_op jit(solution)/shard_map/ppermute | solution.py:803
  349.1 11.4 %copy-start.50 = (f32[16,1024]{1,0:T(8,128)S(1)}, f32[16,1024]{1,0:T(8,128)}, u32[]{:S(2)}) copy-start(f32[16,1024]{1,0:T(8,128)} %get-tuple-element.158) | copy-start | bytes 196612
  362.0 4.3 collective-permute-start.19
  381.1 11.4 %collective-permute-start.20 = (bf16[4,2,64,1280]{3,2,0,1:T(8,128)(2,1)}, bf16[4,2,64,1280]{3,2,0,1:T(8,128)(2,1)}, u32[]{:S(2)}, u32[]{:S(2)}) collective-permute-start(bf16[4,2,64,1280]{3,2,0,1:T(8,128)(2,1)} %bitcast.161), channel_id=1, source_target_pairs={{0,2},{2,0},{4,6},{6,4},{1,3},{3,1},{5,7},{7,5},{8,10},{10,8},{12,... | collective-permute-start | bytes 3932168 | tf_op jit(solution)/shard_map/ppermute | solution.py:812
  390.6 25.7 %collective-permute-start.24 = (bf16[384,1024]{1,0:T(8,128)(2,1)}, bf16[384,1024]{1,0:T(8,128)(2,1)}, u32[]{:S(2)}, u32[]{:S(2)}) collective-permute-start(bf16[384,1024]{1,0:T(8,128)(2,1)} %get-tuple-element.281), channel_id=1, source_target_pairs={{0,1},{1,0},{2,3},{3,2},{4,5},{5,4},{6,7},{7,6},{8,9},{9,8},{10,11... | collective-permute-start | bytes 2359304 | tf_op jit(solution)/shard_map/ppermute | solution.py:812
  397.5 17.4 %collective-permute-start.23 = (bf16[4,64,1280]{2,1,0:T(8,128)(2,1)}, bf16[4,64,1280]{2,1,0:T(8,128)(2,1)}, u32[]{:S(2)}, u32[]{:S(2)}) collective-permute-start(bf16[4,64,1280]{2,1,0:T(8,128)(2,1)} %dynamic-slice_bitcast_fusion), channel_id=1, source_target_pairs={{0,4},{2,6},{4,0},{6,2},{1,5},{3,7},{5,1},{7,3},{8,12},{10,14},{12... | collective-permute-start | bytes 1966088 | tf_op jit(solution)/shard_map/ppermute | solution.py:812
  399.4 3.0 collective-permute-start.21
  402.2 25.6 %collective-permute-start.28 = (bf16[384,1024]{1,0:T(8,128)(2,1)}, bf16[384,1024]{1,0:T(8,128)(2,1)}, u32[]{:S(2)}, u32[]{:S(2)}) collective-permute-start(bf16[384,1024]{1,0:T(8,128)(2,1)} %get-tuple-element.280), channel_id=1, source_target_pairs={{0,1},{1,0},{2,3},{3,2},{4,5},{5,4},{6,7},{7,6},{8,9},{9,8},{10,11... | collective-permute-start | bytes 2359304 | tf_op jit(solution)/shard_map/ppermute | solution.py:812
  402.4 12.5 %collective-permute-start.22 = (f32[88,128]{1,0:T(8,128)S(1)}, f32[88,128]{1,0:T(8,128)S(1)}, u32[]{:S(2)}, u32[]{:S(2)}) collective-permute-start(f32[88,128]{1,0:T(8,128)S(1)} %add.240), channel_id=1, source_target_pairs={{0,4},{2,6},{4,0},{6,2},{1,5},{3,7},{5,1},{7,3},{8,12},{10,14},{12... | collective-permute-start | bytes 135176 | tf_op jit(solution)/shard_map/ppermute | solution.py:812
  406.9 21.0 %copy-start.7 = (bf16[768,1024]{1,0:T(8,128)(2,1)S(1)}, bf16[768,1024]{1,0:T(8,128)(2,1)}, u32[]{:S(2)}) copy-start(bf16[768,1024]{1,0:T(8,128)(2,1)} %get-tuple-element.167) | copy-start | bytes 4718596
  406.9 21.0 %copy-start.52 = (f32[1024]{0:T(1024)S(1)}, f32[1024]{0:T(1024)}, u32[]{:S(2)}) copy-start(f32[1024]{0:T(1024)} %param.30) | copy-start | bytes 12292
  417.3 40.0 %collective-permute-start.31 = (bf16[64,1280]{1,0:T(8,128)(2,1)}, bf16[64,1280]{1,0:T(8,128)(2,1)S(1)}, u32[]{:S(2)}, u32[]{:S(2)}) collective-permute-start(bf16[64,1280]{1,0:T(8,128)(2,1)} %get-tuple-element.282), channel_id=1, source_target_pairs={{0,24},{8,16},{16,8},{24,0},{1,25},{9,17},{17,9},{25,1},{2,26},{10... | collective-permute-start | bytes 491528 | tf_op jit(solution)/shard_map/ppermute | solution.py:812
  420.6 36.7 %collective-permute-start.30 = (bf16[64,1280]{1,0:T(8,128)(2,1)}, bf16[64,1280]{1,0:T(8,128)(2,1)S(1)}, u32[]{:S(2)}, u32[]{:S(2)}) collective-permute-start(bf16[64,1280]{1,0:T(8,128)(2,1)} %get-tuple-element.283), channel_id=1, source_target_pairs={{0,16},{8,24},{16,0},{24,8},{1,17},{9,25},{17,1},{25,9},{2,18},{10... | collective-permute-start | bytes 491528 | tf_op jit(solution)/shard_map/ppermute | solution.py:812
  420.6 11.1 %copy-start.23 = (f32[384,1024]{1,0:T(8,128)S(1)}, f32[384,1024]{1,0:T(8,128)}, u32[]{:S(2)}) copy-start(f32[384,1024]{1,0:T(8,128)} %get-tuple-element.263) | copy-start | bytes 4718596
  420.7 11.1 %copy-start.24 = (f32[384,1024]{1,0:T(8,128)S(1)}, f32[384,1024]{1,0:T(8,128)}, u32[]{:S(2)}) copy-start(f32[384,1024]{1,0:T(8,128)} %get-tuple-element.261) | copy-start | bytes 4718596
  420.7 36.7 %collective-permute-start.29 = (bf16[64,1280]{1,0:T(8,128)(2,1)}, bf16[64,1280]{1,0:T(8,128)(2,1)}, u32[]{:S(2)}, u32[]{:S(2)}) collective-permute-start(bf16[64,1280]{1,0:T(8,128)(2,1)} %get-tuple-element.284), channel_id=1, source_target_pairs={{0,8},{8,0},{16,24},{24,16},{1,9},{9,1},{17,25},{25,17},{2,10},{10... | collective-permute-start | bytes 491528 | tf_op jit(solution)/shard_map/ppermute | solution.py:812
  421.7 8.3 %collective-permute-start.25 = (f32[88,128]{1,0:T(8,128)S(1)}, f32[88,128]{1,0:T(8,128)S(1)}, u32[]{:S(2)}, u32[]{:S(2)}) collective-permute-start(f32[88,128]{1,0:T(8,128)S(1)} %add.241), channel_id=1, source_target_pairs={{0,1},{1,0},{2,3},{3,2},{4,5},{5,4},{6,7},{7,6},{8,9},{9,8},{10,11... | collective-permute-start | bytes 135176 | tf_op jit(solution)/shard_map/ppermute | solution.py:812
  430.0 9.1 %collective-permute-start.26 = (f32[88,128]{1,0:T(8,128)S(1)}, f32[88,128]{1,0:T(8,128)S(1)}, u32[]{:S(2)}, u32[]{:S(2)}) collective-permute-start(f32[88,128]{1,0:T(8,128)S(1)} %add.243), channel_id=1, source_target_pairs={{0,8},{8,0},{16,24},{24,16},{1,9},{9,1},{17,25},{25,17},{2,10},{10... | collective-permute-start | bytes 135176 | tf_op jit(solution)/shard_map/ppermute | solution.py:812
  439.2 13.2 %collective-permute-start.27 = (f32[88,128]{1,0:T(8,128)S(1)}, f32[88,128]{1,0:T(8,128)S(1)}, u32[]{:S(2)}, u32[]{:S(2)}) collective-permute-start(f32[88,128]{1,0:T(8,128)S(1)} %add.244), channel_id=1, source_target_pairs={{0,16},{8,24},{16,0},{24,8},{1,17},{9,25},{17,1},{25,9},{2,18},{10... | collective-permute-start | bytes 135176 | tf_op jit(solution)/shard_map/ppermute | solution.py:812
  475.0 5.2 %collective-permute-start.32 = (bf16[64,256]{1,0:T(8,128)(2,1)S(1)}, bf16[64,256]{1,0:T(8,128)(2,1)S(1)}, u32[]{:S(2)}, u32[]{:S(2)}) collective-permute-start(bf16[64,256]{1,0:T(8,128)(2,1)S(1)} %slice.436), channel_id=1, source_target_pairs={{0,1},{1,0},{2,3},{3,2},{4,5},{5,4},{6,7},{7,6},{8,9},{9,8},{10,11... | collective-permute-start | bytes 98312 | tf_op jit(solution)/shard_map/ppermute | solution.py:812
  (46 other events, 140.3 us)
Sparse Core Ops, SparseCore 0:
  13.2 67.6 all-gather.2
  83.2 60.3 all-gather.4
  238.8 87.2 reduce-scatter.2
  387.0 85.6 reduce-scatter.4

commit v4 on v3

--- a/solution.py
+++ b/solution.py
@@ -263,14 +263,18 @@
     send_ref[NS:, :] = jnp.broadcast_to(total_decay, (send_ref.shape[0] - NS, channels)).astype(low)
 
 
-def chained(refs):
+def by_chip(refs):
+    return [refs[:1], *(refs[i : i + 2] for i in range(1, len(refs), 2))]
+
+
+def chained(groups):
     state = None
-    for ref in reversed(refs):
-        own = ref[0:NS, :].astype(f32)
+    for group in reversed(groups):
+        own = sum(ref[0:NS, :].astype(f32) for ref in group)
         if state is None:
             state = own
         else:
-            state = own + ref[NS : NS + 1, :].astype(f32) * state
+            state = own + sum(ref[NS : NS + 1, :].astype(f32) for ref in group) * state
     return state
 
 
@@ -279,7 +283,7 @@
     tokens, channels = y_ref.shape
     spread = head_map(channels)
     skip = expand(heads_ref[...], spread)[2:3, :]
-    carried = chained(earlier) if earlier else jnp.zeros((NS, channels), f32)
+    carried = chained(by_chip(earlier))
     carried_ref[...] = carried
     carried_low = carried.astype(low)
     for c in range(tokens // CBLK):
@@ -335,7 +339,7 @@
     lo = iota((CBLK, 128), 1) < MP
     rate = heads_ref[1:2, :]
     skip = expand(heads_ref[...], spread)[2:3, :]
-    dstate = chained(later) if later else jnp.zeros((NS, channels), f32)
+    dstate = chained(by_chip(later))
     dve[0:8, :] = jnp.zeros((8, channels), f32)
     dve[8 + tokens :, :] = jnp.zeros((8, channels), f32)
     dbce[0:8, :] = jnp.zeros((8, 2 * NS), f32)
@@ -701,99 +705,134 @@
 TILE = 256
 
 
-def hold(held, first_tile, rows, parts):
-    col = first_tile * TILE
-    for part in parts:
-        width = min(part.shape[1], TILE)
-        for at in range(0, part.shape[1], width):
-            inside = col % TILE
-            held[col // TILE, rows, inside : inside + width] = part[:, at : at + width]
-            col += width
-
-
-def early_grads_body(left_ref, weight_ref, *refs, seqs):
-    pieces, (wgrad_ref, part_ref, held) = refs[:-3], refs[-3:]
-    tile = pl.program_id(0)
-    tokens = held.shape[1] // seqs
-
-    @pl.when(tile == 0)
+def wide(rows, col=0, width=None):
+    return pl.BlockSpec((TILE, rows if width is None else width), lambda t: (t, col))
+
+
+def tall(array):
+    return pl.BlockSpec((array.shape[0], TILE), lambda t: (0, t))
+
+
+def tiled(body, width, arrays, specs, outputs, scratch, flops):
+    return pl.pallas_call(
+        body,
+        grid=(width // TILE,),
+        in_specs=specs,
+        out_specs=[spec for _, _, spec in outputs],
+        out_shape=[jax.ShapeDtypeStruct(shape, dtype) for shape, dtype, _ in outputs],
+        scratch_shapes=scratch,
+        compiler_params=vmem_params(),
+        cost_estimate=pl.CostEstimate(
+            flops=flops,
+            bytes_accessed=sum(a.size * a.dtype.itemsize for a in arrays),
+            transcendentals=0,
+        ),
+    )(*arrays)
+
+
+def early_grads_body(left_ref, wz_ref, wq_ref, *refs, seqs):
+    dz, dq, grads, gated = (refs[seqs * i : seqs * i + seqs] for i in range(4))
+    attended, out_ref, part_ref, held = refs[-4:]
+    tokens = held.shape[0] // seqs
+    z_cols = dz[0].shape[1]
+
+    @pl.when(pl.program_id(0) == 0)
     def _():
         for s in range(seqs):
-            hold(held, 0, slice(tokens * s, tokens * (s + 1)), pieces[2 * s : 2 * s + 2])
-        part_ref[...] = jnp.zeros_like(part_ref)
-
-    grads = held[tile]
-    wgrad_ref[...] = mm(left_ref[...], grads).astype(low)
-    part_ref[...] += mm_nt(grads, weight_ref[...])
-
-
-def late_grads_body(left_ref, weight_ref, start_ref, keyval_ref, *refs, seqs):
-    pieces, (wgrad_ref, part_ref, held, total) = refs[:-4], refs[-4:]
-    tile = pl.program_id(0)
-    tokens = held.shape[1] // seqs
-
-    @pl.when(tile == 0)
+            held[tokens * s : tokens * (s + 1), :z_cols] = dz[s][...]
+            held[tokens * s : tokens * (s + 1), z_cols:] = dq[s][...]
+
+    split = held.shape[1]
+    out_ref[:, :split] = mm(left_ref[...], held[...]).astype(low)
+    middle = split + z_cols
+    from_gated, from_attended = 0.0, 0.0
+    for s in range(seqs):
+        grad = grads[s][...]
+        from_gated = from_gated + mm_tn(grad, gated[s][...])
+        from_attended = from_attended + mm_tn(grad, attended[tokens * s : tokens * (s + 1), :])
+    out_ref[:, split:middle] = from_gated.astype(low)
+    out_ref[:, middle:] = from_attended.astype(low)
+    part_ref[...] = mm_nt(held[:, :z_cols], wz_ref[...]) + mm_nt(held[:, z_cols:], wq_ref[...])
+
+
+def early_grads(left, weight, cols, dz, dq, grads, gated, attended):
+    width, rows = left.shape
+    own = cols.bc - cols.z
+    out_cols = own + gated[0].shape[1] + attended.shape[1]
+    q_cols = cols.bc - cols.q
+    return tiled(
+        functools.partial(early_grads_body, seqs=len(dz)),
+        width,
+        [left, weight, weight, *dz, *dq, *grads, *gated, attended],
+        [
+            wide(rows),
+            wide(cols.channels, cols.z // cols.channels),
+            wide(q_cols, cols.q // q_cols),
+        ]
+        + [whole(a.shape) for a in (*dz, *dq)]
+        + [tall(a) for a in grads]
+        + [whole(a.shape) for a in (*gated, attended)],
+        [
+            ((width, out_cols), low, wide(out_cols)),
+            ((rows, width), f32, pl.BlockSpec((rows, TILE), lambda t: (0, t))),
+        ],
+        [pltpu.VMEM((rows, own), low)],
+        2 * rows * width * (own + out_cols),
+    )
+
+
+def late_grads_body(left_ref, wx_ref, wbc_ref, wrest_ref, start_ref, keyval_ref, head_ref, *refs, seqs):
+    dx, dbc, dstep, edge = (refs[seqs * i : seqs * i + seqs] for i in range(4))
+    out_ref, part_ref, held = refs[-3:]
+    tokens = held.shape[0] // seqs
+    channels = dx[0].shape[1]
+    conv_cols = channels + dbc[0].shape[1]
+
+    @pl.when(pl.program_id(0) == 0)
     def _():
         for s in range(seqs):
-            dx, dbc, dstep, edge, head = pieces[5 * s : 5 * s + 5]
             rows = slice(tokens * s, tokens * (s + 1))
-            hold(held, 0, rows, (dx, dbc, keyval_ref.at[rows, :], dstep))
-            mended = (edge[...] + head[16 * s : 16 * s + 16, :]).astype(low)
-            for at in range(0, mended.shape[1], TILE):
-                held[at // TILE, tokens * (s + 1) - 16 : tokens * (s + 1), :] = mended[
-                    :, at : at + TILE
-                ]
-        total[...] = start_ref[...]
-
-    grads = held[tile]
-    wgrad_ref[...] = mm(left_ref[...], grads).astype(low)
-    total[...] += mm_nt(grads, weight_ref[...])
-
-    @pl.when(tile == pl.num_programs(0) - 1)
-    def _():
-        part_ref[...] = total[...].astype(low)
-
-
-def tiled_grads(body, left, weight, tile_of, tiles, arrays, part_dtype, scratch):
+            held[rows, :channels] = dx[s][...]
+            held[rows, channels:conv_cols] = dbc[s][...]
+            held[rows, conv_cols : conv_cols + 128] = keyval_ref[rows, :]
+            held[rows, conv_cols + 128 :] = dstep[s][...]
+            held[tokens * (s + 1) - 16 : tokens * (s + 1), :conv_cols] = (
+                edge[s][...] + head_ref[16 * s : 16 * s + 16, :]
+            ).astype(low)
+
+    out_ref[...] = mm(left_ref[...], held[...]).astype(low)
+    part_ref[...] = (
+        start_ref[...]
+        + mm_nt(held[:, :channels], wx_ref[...])
+        + mm_nt(held[:, channels:conv_cols], wbc_ref[...])
+        + mm_nt(held[:, conv_cols:], wrest_ref[...])
+    ).astype(low)
+
+
+def late_grads(left, weight, cols, start, keyval, head, dx, dbc, dstep, edge):
     width, rows = left.shape
-    return pl.pallas_call(
-        body,
-        grid=(tiles,),
-        in_specs=[whole(left.shape), pl.BlockSpec((width, TILE), lambda t: (0, tile_of(t)))]
-        + [whole(a.shape) for a in arrays],
-        out_specs=[pl.BlockSpec((width, TILE), lambda t: (0, t)), whole((rows, width))],
-        out_shape=[shaped(width, tiles * TILE, low), shaped(rows, width, part_dtype)],
-        scratch_shapes=[pltpu.VMEM((tiles, rows, TILE), low), *scratch],
-        compiler_params=vmem_params(),
-        cost_estimate=pl.CostEstimate(
-            flops=4 * rows * tiles * TILE * width,
-            bytes_accessed=4 * width * tiles * TILE,
-            transcendentals=0,
-        ),
-    )(left, weight, *arrays)
-
-
-def early_grads(left, weight, cols, pieces, seqs):
-    first = cols.z // TILE
-    tiles = (cols.bc - cols.z) // TILE
-    return tiled_grads(
-        functools.partial(early_grads_body, seqs=seqs),
-        left, weight, lambda t: t + first, tiles, [a for p in pieces for a in p], f32, [],
-    )
-
-
-def late_grads(left, weight, cols, start, keyval, pieces, seqs):
-    before = cols.z // TILE
-    skipped = (cols.bc - cols.z) // TILE
-    return tiled_grads(
-        functools.partial(late_grads_body, seqs=seqs),
-        left,
-        weight,
-        lambda t: jnp.where(t < before, t, t + skipped),
-        cols.total // TILE - skipped,
-        [start, keyval] + [a for p in pieces for a in p],
-        low,
-        [pltpu.VMEM(start.shape, f32)],
+    own = cols.total - (cols.bc - cols.z)
+    bc_cols, rest = cols.kv - cols.bc, cols.total - cols.kv
+    return tiled(
+        functools.partial(late_grads_body, seqs=len(dx)),
+        width,
+        [left, weight, weight, weight, start, keyval, head, *dx, *dbc, *dstep, *edge],
+        [
+            wide(rows),
+            wide(cols.channels, 0),
+            wide(bc_cols, cols.bc // bc_cols),
+            wide(rest, cols.kv // rest),
+            tall(start),
+            whole(keyval.shape),
+            whole(head.shape),
+        ]
+        + [whole(a.shape) for a in (*dx, *dbc, *dstep, *edge)],
+        [
+            ((width, own), low, wide(own)),
+            ((rows, width), low, pl.BlockSpec((rows, TILE), lambda t: (0, t))),
+        ],
+        [pltpu.VMEM((rows, own), low)],
+        4 * rows * width * own,
     )
 
 
@@ -840,6 +879,23 @@
 
 def picked(array, at, dim):
     return lax.dynamic_index_in_dim(array, at, dim, False)
+
+
+def states_beside(sent, seqs, side):
+    chips = range(lax.axis_size("ctx") // 2)
+    near, far = (1, 0) if side < 0 else (0, 1)
+    got = lax.ppermute(sent, "ctx", [(2 * k + far, 2 * k + near) for k in chips])
+    own, got = (a.reshape(seqs, SENT, -1).astype(f32) for a in (sent, got))
+    is_decay = lax.broadcasted_iota(jnp.int32, (1, SENT, 1), 1) >= NS
+    got = jnp.where((lax.axis_index("ctx") & 1) == near, got, jnp.where(is_decay, 1.0, 0.0))
+    both = jnp.where(is_decay, own * got, own + own[:, NS : NS + 1] * got)
+    first, both = (a.astype(low).reshape(sent.shape) for a in (got, both))
+    beside = [first]
+    for d in chips[1:]:
+        for core in range(2):
+            route = [(2 * k + near, 2 * (k - side * d) + core) for k in chips if k - side * d in chips]
+            beside.append(lax.ppermute(both, "ctx", route))
+    return beside
 
 
 def core_sum(terms):
@@ -975,20 +1031,19 @@
     queries, keyval = prep(pre, cosine, sine, seqs, tokens, cols.q, q_cols, cols.kv)
     keyvals = [keyval] + [passed_along(keyval, "ctx", d) for d in range(1, hops)]
     v, vbc, y_own, logs, states, sent = scan(
-        pre, cols, tails, taps, taps_bc, per_head, seqs, tokens, heads
-    )
-    earlier = [passed_along(sent, "ctx", d) for d in range(1, hops)]
-    attended, lse = attend(after(queries, sent), keyvals, at, seqs, tokens)
-    y, carried, mixers, offers = [], [], [], []
+        after(pre, keyval), cols, tails, taps, taps_bc, per_head, seqs, tokens, heads
+    )
+    earlier = states_beside(after(sent, *keyvals[1:]), seqs, -1)
+    attended, lse = attend(after(queries, earlier[0]), keyvals, at, seqs, tokens)
+    gated, y, carried, offers = [], [], [], []
     for s in each:
         here = gate(pre, cols, y_own, v, vbc, logs, per_head, earlier, s, tokens)
         y.append(here[1])
         carried.append(here[2])
-        mixers.append(
-            jnp.concatenate([here[0], attended[tokens * s : tokens * (s + 1)]], -1)
-        )
+        gated.append(here[0])
+        mixers = jnp.concatenate([here[0], attended[tokens * s : tokens * (s + 1)]], -1)
         offers.append(
-            offer(jnp.einsum("ti,di->td", mixers[s], out_full_w, preferred_element_type=f32))
+            offer(jnp.einsum("ti,di->td", mixers, out_full_w, preferred_element_type=f32))
         )
 
     mask_float = valid_mask.astype(f32)[..., None]
@@ -1028,16 +1083,12 @@
         )
     block_out = jnp.stack(out_full).astype(low)
 
+    join = lambda parts: jnp.concatenate(parts, 0)
     def wgrad(left, right):
+        left, right = join(left), join(right)
         return jnp.einsum("td,tc->dc", left, right, preferred_element_type=f32).astype(low)
 
-    join = lambda parts: jnp.concatenate(parts, 0)
-    ffn_wgrads = [
-        wgrad(join(normed_two), join(gateup_low)),
-        wgrad(join(down_in), join(inner)),
-    ]
-
-    ffn_terms = jnp.concatenate(ffn_wgrads, 1)
+    ffn_terms = jnp.concatenate([wgrad(normed_two, gateup_low), wgrad(down_in, inner)], 1)
     ffn_reduced = lax.psum_scatter(ffn_terms, owners, scatter_dimension=0, tiled=True)
 
     resid_grad, mixed_low, ffn_gain_grad = [], [], 0.0
@@ -1058,22 +1109,20 @@
         dy.append(here[0])
         dz.append(here[1])
         skip_rows.append(here[2])
-    later = [passed_along(sent_back, "ctx", -d) for d in range(1, hops)]
+    later = states_beside(sent_back, seqs, 1)
     query_back, keyval_parts = [], [None] * hops
     for s in each:
         gq, *keyval_parts = attend_back(
-            queries, keyvals, after(mixers_grads[s], sent_back), channels, attended, lse,
+            queries, keyvals, after(mixers_grads[s], later[0]), channels, attended, lse,
             cosine, sine, at, s, seqs, tokens, keyval_parts,
         )
         query_back.append(gq)
     keyval_parts = [keyval_parts[0]] + [
         passed_along(keyval_parts[d], "ctx", -d) for d in range(1, hops)
     ]
-    out_wgrad = wgrad(join(mixed_low), join(mixers))
     early_terms, part = early_grads(
-        after(normed_t, *later), mixer_both, cols, [[dz[s], query_back[s]] for s in each], seqs
-    )
-    early_terms = jnp.concatenate([early_terms, out_wgrad], 1)
+        after(normed_t, *later), mixer_both, cols, dz, query_back, mixed_low, gated, attended
+    )
     early_reduced = lax.psum_scatter(early_terms, owners, scatter_dimension=0, tiled=True)
     scan_backs = []
     for s in each:
@@ -1085,9 +1134,9 @@
         )
     keyval_back = keyval_sum(keyval_parts, cosine, sine, seqs, tokens)
     head = passed_along(join([scan_backs[s][4] for s in each]), "ctx", -1)
+    dx, dbc, dstep, edge = (list(a) for a in list(zip(*scan_backs))[:4])
     late_terms, part = late_grads(
-        normed_t, mixer_both, cols, after(part, ffn_reduced), keyval_back,
-        [[*scan_backs[s][:4], head] for s in each], seqs,
+        normed_t, mixer_both, cols, after(part, ffn_reduced), keyval_back, head, dx, dbc, dstep, edge
     )
     part = [part[tokens * s : tokens * (s + 1)] for s in each]
     part_other = [swapped(p, "tp", 1) for p in part]
@@ -1127,7 +1176,9 @@
     fill = -flat.shape[0] % 1024
     flat = after(jnp.pad(flat, (0, fill)).reshape(-1, 128), *sends)
     flat = sum_over(flat, ("ctx",))
-    held = after(added(own, got).astype(low), part_other[0], flat)
+    held, early_reduced, *_ = lax.optimization_barrier(
+        (added(own, got).astype(low), early_reduced, part_other[0], flat)
+    )
     own, sends, got = spread(held, "dp", 0, 0)
     flat = sum_over(after(flat, *sends), ("tp", "dp"))
     late_reduced = added(own, [after(got[0], flat), *got[1:]])
@@ -1145,7 +1196,7 @@
     head_total = narrow(summed[4], 1, heads)
     loss = summed[5][0] * loss_scale
     ffn_reduced = ffn_reduced.astype(f32)
-    early_reduced = after(early_reduced, late_reduced).astype(f32)
+    early_reduced = early_reduced.astype(f32)
     out_reduced = early_reduced[:, channels + q_cols :]
     state_reduced = summed_pair(*offer(late_reduced[:, channels : channels + bc_cols]))
     rest = late_reduced[:, channels + bc_cols :]

time: 497 us -> 456 us (0.918)
  waiting for transfers between devices: 156 us -> 130 us
  matrix products: 50.5 us -> 43.3 us
  starting transfers between devices: 55.9 us -> 50.5 us
    reduce_scatter x1, waiting for transfers between devices: 14 us -> 0.01 us  [per_device(): lax.psum_scatter(early_terms, owners, scatter_dimension=0, tiled=True)]
    ppermute x14 -> x8, starting transfers between devices: 26.6 us -> 12.6 us  [passed_along(): return lax.ppermute(array, axis, route)]
    ppermute x14 -> x8, waiting for transfers between devices: 12.7 us -> 0.06 us  [passed_along(): return lax.ppermute(array, axis, route)]
    ppermute x0 -> x6, starting transfers between devices: none -> 9.18 us  [the longest x2 5.35 us: states_beside(): lax.ppermute(sent, 'ctx', [(2 * k + far, 2 * k + near) for k in chips])]
    unnamed x151 -> x161, local copies, waits for them, and re-layouts: 12.3 us -> 14.2 us
  transfers between devices with their start and end apart: 37 -> 37, of which waited for: 13 -> 12; matrix products, arithmetic and copies ran while one was open for 24% -> 24% of each run, Pallas kernels for 20% -> 24%
where the time goes in v4:
time: 456 us; the launch traced here: 448 us
  waiting for transfers between devices  130 us (29%)
  Pallas kernels  108 us (24%)
  other arithmetic  55.2 us (12%)
  starting transfers between devices  50.5 us (11%)
  matrix products  43.3 us (9%)
  local copies, waits for them, and re-layouts  40.8 us (9%)
  between operations  19.4 us (4%)
    pallas_call x12, Pallas kernels, run(): pl.pallas_call(inner, grid=(seqs,), in_specs=specs, out_specs=out_specs,...  89.6 us
    ppermute x19, waiting for transfers between devices, swapped(): return lax.ppermute(array, axis, [(i, i ^ distance) for i in devices])  67.6 us
    all_gather x1, waiting for transfers between devices, per_device(): mixer_both = lax.all_gather(mixer_shard, owners, axis=0, tiled=True)  59.2 us
    ppermute x19, starting transfers between devices, swapped(): return lax.ppermute(array, axis, [(i, i ^ distance) for i in devices])  28.3 us
    pallas_call x2, Pallas kernels, tiled(): pl.pallas_call(body, grid=(width // TILE,), in_specs=specs, out_specs=[sp...  18.8 us
    unnamed x161, local copies, waits for them, and re-layouts  14.2 us
    ppermute x8, starting transfers between devices, passed_along(): return lax.ppermute(array, axis, route)  12.6 us
    reduce_sum x4, other arithmetic, rms_norm(): values * lax.rsqrt(jnp.mean(values * values, -1, keepdims=True) + eps_norm)  9.2 us
  transfers between devices with their start and end apart: 37, of which 12 were waited for; matrix products, arithmetic and copies ran while one was open for 24% of the time, Pallas kernels for 24%

profile of v4, /device:TPU:0, one launch (start us, length us, event | category | flops | bytes accessed | tf_op | source)
XLA Modules:
  0.0 448.0 jit_solution(14281071106996194876)
XLA Ops:
  11.2 1.9 concatenate.47
  15.0 1.6 copy.91
  21.7 59.2 %all-gather.3.cloned.1.call-done.wz_ref.wq_ref.wx_ref.wbc_ref.wrest_ref = bf16[1024,3328]{1,0:T(8,128)(2,1)} async-done(((bf16[64,3328]{1,0:T(8,128)(2,1)}), bf16[1024,3328]{1,0:T(8,128)(2,1)}) %all-gather.3.cloned.1.call-update) | async-done | bytes 6815760 | tf_op jit(solution)/shard_map/all_gather | solution.py:995
  80.9 6.7 %fusion.refs_0_.refs_1_.refs_2_.refs_4_.refs_5_.refs_6_ = f32[768,2304]{1,0:T(8,128)S(1)} fusion(bf16[768,1024]{0,1:T(8,128)(2,1)} %copy.91, bf16[1024,3328]{1,0:T(8,128)(2,1)} %all-gather.3.cloned.1.call-done.wz_ref.wq_ref.wx_ref.wbc_ref.wrest_ref), kind=kOutput, calls=%fused_computation.1 | convolution fusion | flops 3623878656 | bytes 13369344 | tf_op jit(solution)/shard_map/dot_general | solution.py:1023
  87.7 2.8 copy-done
  90.4 2.7 shard_map.382
  93.1 2.2 collective-permute-start.1
  95.3 2.5 collective-permute-start.2
  99.1 1.5 collective-permute-start
  101.9 10.7 %shard_map.383 = (f32[768,768]{1,0:T(8,128)}, f32[768,256]{1,0:T(8,128)}, f32[768,768]{1,0:T(8,128)}, f32[768,128]{1,0:T(8,128)}, f32[768,768]{1,0:T(8,128)}, /*index=5*/bf16[288,768]{1,0:T(8,128)(2,1)}) custom-call(f32[768,2304]{1,0:T(8,128)} %copy-done, f32[768,2304]{1,0:T(8,128)} %copy-done, f32[768,2304]{1,0:T(8,128)} %copy-done, f32[16,1024]{1,0:T(8,128)} %copy-done.34, ...), custom_call_target="tpu_custom_call" | custom-call | flops 603979776 | bytes 21401600 | tf_op jit(solution)/shard_map/pallas_call | solution.py:491
  112.7 4.1 collective-permute-start.4
  122.1 10.3 %shard_map.385 = (bf16[768,256]{1,0:T(8,128)(2,1)}, f32[768,128]{1,0:T(8,128)}) custom-call(s32[1]{0:T(128)} %bitcast.17.refs_0_, bf16[768,256]{1,0:T(8,128)(2,1)} %get-tuple-element.121.refs_1_, bf16[768,128]{1,0:T(8,128)(2,1)} %get-tuple-element.111.refs_2_.refs_7_, bf16[768,128]{1,0:T(8,128)(2,1)} %copy-done.68, bf16[768,128]{1,0:T(8,128)(2,1)} %copy-done.69, ...), custom_call_target="tpu_custom_call" | custom-call | flops 4831838208 | bytes 1179652 | tf_op jit(solution)/shard_map/pallas_call | solution.py:491
  134.3 4.6 %shard_map.384 = (bf16[384,768]{1,0:T(8,128)(2,1)}, f32[384,768]{1,0:T(8,128)}, f32[128,768]{1,0:T(8,128)}) custom-call(f32[768,2304]{1,0:T(8,128)} %copy-done, f32[768,768]{1,0:T(8,128)} %get-tuple-element.113.refs_1_, f32[768,768]{1,0:T(8,128)} %get-tuple-element.114.refs_2_.refs_3_, f32[768,256]{1,0:T(8,128)} %get-tuple-element.115.refs_3_.refs_4_, ...), custom_call_target="tpu_custom_call" | custom-call | flops 150994944 | bytes 14307328 | tf_op jit(solution)/shard_map/pallas_call | solution.py:491
  138.9 3.9 convolution_convert_fusion.5
  146.9 4.6 %shard_map.386 = (bf16[384,768]{1,0:T(8,128)(2,1)}, f32[384,768]{1,0:T(8,128)}, f32[128,768]{1,0:T(8,128)}) custom-call(f32[768,2304]{1,0:T(8,128)} %copy-done, f32[768,768]{1,0:T(8,128)} %get-tuple-element.113.refs_1_, f32[768,768]{1,0:T(8,128)} %get-tuple-element.114.refs_2_.refs_3_, f32[768,256]{1,0:T(8,128)} %get-tuple-element.115.refs_3_.refs_4_, ...), custom_call_target="tpu_custom_call" | custom-call | flops 150994944 | bytes 14307328 | tf_op jit(solution)/shard_map/pallas_call | solution.py:491
  151.6 3.7 convolution_convert_fusion.4
  155.8 4.6 %collective-permute-done.7 = bf16[384,1024]{1,0:T(8,128)(2,1)} collective-permute-done((bf16[384,1024]{1,0:T(8,128)(2,1)}, bf16[384,1024]{1,0:T(8,128)(2,1)}, u32[]{:S(2)}, u32[]{:S(2)}) %collective-permute-start.7) | collective-permute-done | bytes 786464 | tf_op jit(solution)/shard_map/ppermute | solution.py:851
  160.4 1.8 multiply_reduce_fusion.10
  164.5 4.4 fusion.11
  171.6 5.6 %collective-permute-done.9 = bf16[384,1024]{1,0:T(8,128)(2,1)} collective-permute-done((bf16[384,1024]{1,0:T(8,128)(2,1)}, bf16[384,1024]{1,0:T(8,128)(2,1)}, u32[]{:S(2)}, u32[]{:S(2)}) %collective-permute-start.9) | collective-permute-done | bytes 786464 | tf_op jit(solution)/shard_map/ppermute | solution.py:851
  177.2 2.0 multiply_reduce_fusion.5
  179.4 1.8 fusion.9
  184.0 9.9 %collective-permute-done.8 = bf16[384,1024]{1,0:T(8,128)(2,1)S(1)} collective-permute-done((bf16[384,1024]{1,0:T(8,128)(2,1)S(1)}, bf16[384,1024]{1,0:T(8,128)(2,1)S(1)}, u32[]{:S(2)}, u32[]{:S(2)}) %collective-permute-start.8) | collective-permute-done | bytes 786464 | tf_op jit(solution)/shard_map/ppermute | solution.py:851
  194.9 1.5 fusion.80
  196.6 2.7 fusion.43
  199.4 11.4 %collective-permute-done.10 = bf16[384,1024]{1,0:T(8,128)(2,1)S(1)} collective-permute-done((bf16[384,1024]{1,0:T(8,128)(2,1)S(1)}, bf16[384,1024]{1,0:T(8,128)(2,1)S(1)}, u32[]{:S(2)}, u32[]{:S(2)}) %collective-permute-start.10) | collective-permute-done | bytes 786464 | tf_op jit(solution)/shard_map/ppermute | solution.py:851
  211.8 1.8 convolution_convert_fusion.1
  216.4 3.7 convolution_convert_fusion
  220.1 3.3 pad_maximum_fusion
  225.0 5.4 %fusion.46 = bf16[384,1024]{1,0:T(8,128)(2,1)} fusion(bf16[384,2048]{1,0:T(8,128)(2,1)} %copy-done.40, bf16[1024,3072]{1,0:T(8,128)(2,1)} %all-gather.5.cloned.1.call-done), kind=kOutput, calls=%fused_computation.94 | convolution fusion | flops 1611005952 | bytes 6553600 | tf_op jit(solution)/shard_map/tc,dc->td/dot_general | solution.py:1082
  231.2 11.1 %collective-permute-done.12 = bf16[384,1024]{1,0:T(8,128)(2,1)S(1)} collective-permute-done((bf16[384,1024]{1,0:T(8,128)(2,1)}, bf16[384,1024]{1,0:T(8,128)(2,1)S(1)}, u32[]{:S(2)}, u32[]{:S(2)}) %collective-permute-start.12) | collective-permute-done | bytes 786464 | tf_op jit(solution)/shard_map/ppermute | solution.py:851
  242.3 1.8 multiply_reduce_fusion.4
  244.2 2.6 fusion.95
  246.8 2.1 fusion.57.refs_0_.refs_2_
  248.9 5.2 %shard_map.387 = (f32[384,768]{1,0:T(8,128)}, bf16[384,768]{1,0:T(8,128)(2,1)}, f32[8,768]{1,0:T(8,128)}, bf16[288,768]{1,0:T(8,128)(2,1)}) custom-call(f32[384,1024]{1,0:T(8,128)} %fusion.57.refs_0_.refs_2_, f32[768,2304]{1,0:T(8,128)} %copy-done, f32[384,768]{1,0:T(8,128)} %get-tuple-element.130.refs_2_.refs_1_, ...), custom_call_target="tpu_custom_call" | custom-call | flops 150994944 | bytes 13815808 | tf_op jit(solution)/shard_map/pallas_call | solution.py:491
  254.1 5.2 %collective-permute-done.11 = bf16[384,1024]{1,0:T(8,128)(2,1)} collective-permute-done((bf16[384,1024]{1,0:T(8,128)(2,1)}, bf16[384,1024]{1,0:T(8,128)(2,1)}, u32[]{:S(2)}, u32[]{:S(2)}) %collective-permute-start.11) | collective-permute-done | bytes 786464 | tf_op jit(solution)/shard_map/ppermute | solution.py:851
  259.3 4.2 multiply_reduce_fusion.3
  263.5 3.9 fusion.93
  267.3 2.1 fusion.55.refs_0_.refs_2_
  269.5 5.2 %shard_map.388 = (f32[384,768]{1,0:T(8,128)}, bf16[384,768]{1,0:T(8,128)(2,1)}, f32[8,768]{1,0:T(8,128)}, bf16[288,768]{1,0:T(8,128)(2,1)}) custom-call(f32[384,1024]{1,0:T(8,128)} %fusion.55.refs_0_.refs_2_, f32[768,2304]{1,0:T(8,128)} %copy-done, f32[384,768]{1,0:T(8,128)} %get-tuple-element.133.refs_2_.refs_1_, ...), custom_call_target="tpu_custom_call", output_to_operand_aliasing={{3}: (8, {})} | custom-call | flops 150994944 | bytes 13815808 | tf_op jit(solution)/shard_map/pallas_call | solution.py:491
  276.7 2.9 collective-permute-done.13
  284.4 10.4 %shard_map.389 = (bf16[384,256]{1,0:T(8,128)(2,1)}, bf16[768,128]{1,0:T(8,128)(2,1)}, bf16[768,128]{1,0:T(8,128)(2,1)}, bf16[768,128]{1,0:T(8,128)(2,1)}, bf16[768,128]{1,0:T(8,128)(2,1)}) custom-call(s32[1]{0:T(128)} %bitcast.17.refs_0_, bf16[768,256]{1,0:T(8,128)(2,1)} %get-tuple-element.121.refs_1_, f32[384,1024]{1,0:T(8,128)} %fusion.57.refs_0_.refs_2_, ...), custom_call_target="tpu_custom_call" | custom-call | flops 6039797760 | bytes 4325380 | tf_op jit(solution)/shard_map/pallas_call | solution.py:491
  294.8 10.6 %shard_map.390 = (bf16[384,256]{1,0:T(8,128)(2,1)}, bf16[768,128]{1,0:T(8,128)(2,1)}, bf16[768,128]{1,0:T(8,128)(2,1)}, bf16[768,128]{1,0:T(8,128)(2,1)}, bf16[768,128]{1,0:T(8,128)(2,1)}) custom-call(s32[1]{0:T(128)} %bitcast.17.refs_0_, ...), custom_call_target="tpu_custom_call", output_to_operand_aliasing={{1}: (11, {}), {2}: (12, {}), {3}: (13, {}), {4}: (14, {})} | custom-call | flops 6039797760 | bytes 4325380 | tf_op jit(solution)/shard_map/pallas_call | solution.py:491
  305.4 10.2 %shard_map.391 = (bf16[1024,2048]{1,0:T(8,128)(2,1)}, f32[768,1024]{1,0:T(8,128)}) custom-call(bf16[1024,768]{1,0:T(8,128)(2,1)} %bitcast.182, bf16[1024,3328]{1,0:T(8,128)(2,1)} %all-gather.3.cloned.1.call-done.wz_ref.wq_ref.wx_ref.wbc_ref.wrest_ref, bf16[1024,3328]{1,0:T(8,128)(2,1)} %all-gather.3.cloned.1.call-done.wz_ref.wq_ref.wx_ref.wbc_ref.wrest_ref, ...), custom_call_target="tpu_custom_call" | custom-call | flops 4831838208 | bytes 19922944 | tf_op jit(solution)/shard_map/pallas_call | solution.py:717
  320.4 11.3 %shard_map.394 = (bf16[384,768]{1,0:T(8,128)(2,1)}, bf16[384,256]{1,0:T(8,128)(2,1)}, bf16[384,128]{1,0:T(8,128)(2,1)}, f32[16,1024]{1,0:T(8,128)}, f32[16,1024]...) custom-call(f32[384,768]{1,0:T(8,128)} %get-tuple-element.160.refs_0_, ...), custom_call_target="tpu_custom_call" | custom-call | flops 1132462080 | bytes 31379456 | tf_op jit(solution)/shard_map/pallas_call | solution.py:491
  331.8 11.8 %shard_map.393 = (bf16[384,768]{1,0:T(8,128)(2,1)}, bf16[384,256]{1,0:T(8,128)(2,1)}, bf16[384,128]{1,0:T(8,128)(2,1)}, f32[16,1024]{1,0:T(8,128)}, f32[16,1024]...) custom-call(f32[384,768]{1,0:T(8,128)} %get-tuple-element.155.refs_0_, ...), custom_call_target="tpu_custom_call" | custom-call | flops 1132462080 | bytes 31379456 | tf_op jit(solution)/shard_map/pallas_call | solution.py:491
  346.5 2.3 shard_map.392.keyval_ref
  349.5 8.6 %shard_map.395 = (bf16[1024,1280]{1,0:T(8,128)(2,1)}, bf16[768,1024]{1,0:T(8,128)(2,1)}) custom-call(bf16[1024,768]{1,0:T(8,128)(2,1)} %bitcast.183, bf16[1024,3328]{1,0:T(8,128)(2,1)} %all-gather.3.cloned.1.call-done.wz_ref.wq_ref.wx_ref.wbc_ref.wrest_ref, bf16[1024,3328]{1,0:T(8,128)(2,1)} %all-gather.3.cloned.1.call-done.wz_ref.wq_ref.wx_ref.wbc_ref.wrest_ref, ...), custom_call_target="tpu_custom_call" | custom-call | flops 4026531840 | bytes 27394048 | tf_op jit(solution)/shard_map/pallas_call | solution.py:717
  358.1 3.0 constant_dynamic-slice_fusion.1
  361.3 6.9 %collective-permute-start.20 = (bf16[4,2,64,1280]{3,2,0,1:T(8,128)(2,1)S(1)}, bf16[4,2,64,1280]{3,2,0,1:T(8,128)(2,1)}, u32[]{:S(2)}, u32[]{:S(2)}) collective-permute-start(bf16[4,2,64,1280]{3,2,0,1:T(8,128)(2,1)S(1)} %bitcast.189), channel_id=1, source_target_pairs={{0,2},{2,0},{4,6},{6,4},{1,3},{3,1},{5,7},{7,5},{8,10},{10,8},{12,... | collective-permute-start | bytes 3932168 | tf_op jit(solution)/shard_map/ppermute | solution.py:851
  373.6 1.8 fusion.13
  378.0 2.7 pad_maximum_fusion.1
  381.6 1.9 collective-permute-start.22
  385.1 2.3 reshape.355
  387.3 9.3 %collective-permute-done.22 = f32[88,128]{1,0:T(8,128)S(1)} collective-permute-done((f32[88,128]{1,0:T(8,128)S(1)}, f32[88,128]{1,0:T(8,128)S(1)}, u32[]{:S(2)}, u32[]{:S(2)}) %collective-permute-start.22) | collective-permute-done | bytes 45088 | tf_op jit(solution)/shard_map/ppermute | solution.py:851
  396.7 2.3 fusion.61
  399.0 1.8 dynamic-slice_bitcast_fusion.1
  400.8 2.4 collective-permute-start.30
  404.4 5.1 %collective-permute-done.28 = bf16[384,1024]{1,0:T(8,128)(2,1)} collective-permute-done((bf16[384,1024]{1,0:T(8,128)(2,1)}, bf16[384,1024]{1,0:T(8,128)(2,1)}, u32[]{:S(2)}, u32[]{:S(2)}) %collective-permute-start.28) | collective-permute-done | bytes 786464 | tf_op jit(solution)/shard_map/ppermute | solution.py:851
  409.5 2.7 multiply_reduce_fusion.2
  412.8 2.3 fusion.69
  418.7 1.7 collective-permute-start.31
  420.4 2.8 collective-permute-start.27
  423.9 5.3 %collective-permute-done.27 = f32[88,128]{1,0:T(8,128)S(1)} collective-permute-done((f32[88,128]{1,0:T(8,128)S(1)}, f32[88,128]{1,0:T(8,128)S(1)}, u32[]{:S(2)}, u32[]{:S(2)}) %collective-permute-start.27) | collective-permute-done | bytes 45088 | tf_op jit(solution)/shard_map/ppermute | solution.py:851
  (342 shorter events, 80.2 us)
Async XLA Ops:
  7.2 73.7 %all-gather.3.cloned.1.call-start = ((), (), s32[]{:S(2)}) async-start(), calls=%async_computation.2 | async-start | bytes 7241728 | tf_op jit(solution)/shard_map/all_gather | solution.py:995
  13.1 151.3 %all-gather.5.cloned.1.call-start = ((), (), s32[]{:S(2)}) async-start(), calls=%async_computation.3 | async-start | bytes 6684672 | tf_op jit(solution)/shard_map/all_gather | solution.py:1000
  14.0 334.8 %reduce-scatter.3.cloned.1.call-start = ((), (), s32[]{:S(2)}) async-start(), calls=%async_computation.4 | async-start | bytes 6684672 | tf_op jit(solution)/shard_map/reduce_scatter | solution.py:1092
  90.4 10.2 %copy-start.65 = (f32[12]{0:T(128)S(1)}, f32[12]{0:T(128)}, u32[]{:S(2)}) copy-start(f32[12]{0:T(128)} %param.43) | copy-start | bytes 148
  90.4 10.2 %copy-start.66 = (f32[12]{0:T(128)S(1)}, f32[12]{0:T(128)}, u32[]{:S(2)}) copy-start(f32[12]{0:T(128)} %param.41) | copy-start | bytes 148
  93.1 19.5 %collective-permute-start.1 = (bf16[768,128]{1,0:T(8,128)(2,1)}, bf16[768,128]{1,0:T(8,128)(2,1)S(1)}, u32[]{:S(2)}, u32[]{:S(2)}) collective-permute-start(bf16[768,128]{1,0:T(8,128)(2,1)} %get-tuple-element.111.refs_2_.refs_7_), channel_id=1, source_target_pairs={{0,2},{2,4},{4,6},{1,3},{3,5},{5,7},{8,10},{10,12},{12,14},{9,11},... | collective-permute-start | bytes 589832 | tf_op jit(solution)/shard_map/ppermute | solution.py:842
  95.3 17.4 %collective-permute-start.2 = (bf16[768,128]{1,0:T(8,128)(2,1)}, bf16[768,128]{1,0:T(8,128)(2,1)S(1)}, u32[]{:S(2)}, u32[]{:S(2)}) collective-permute-start(bf16[768,128]{1,0:T(8,128)(2,1)} %get-tuple-element.111.refs_2_.refs_7_), channel_id=1, source_target_pairs={{0,4},{2,6},{1,5},{3,7},{8,12},{10,14},{9,13},{11,15},{16,20},{18,... | collective-permute-start | bytes 589832 | tf_op jit(solution)/shard_map/ppermute | solution.py:842
  97.8 14.9 %collective-permute-start.3 = (bf16[768,128]{1,0:T(8,128)(2,1)}, bf16[768,128]{1,0:T(8,128)(2,1)S(1)}, u32[]{:S(2)}, u32[]{:S(2)}) collective-permute-start(bf16[768,128]{1,0:T(8,128)(2,1)} %get-tuple-element.111.refs_2_.refs_7_), channel_id=1, source_target_pairs={{0,6},{1,7},{8,14},{9,15},{16,22},{17,23},{24,30},{25,31}} | collective-permute-start | bytes 589832 | tf_op jit(solution)/shard_map/ppermute | solution.py:842
  99.1 2.2 collective-permute-start
  112.6 9.4 %copy-start.68 = (bf16[768,128]{1,0:T(8,128)(2,1)}, bf16[768,128]{1,0:T(8,128)(2,1)S(1)}, u32[]{:S(2)}) copy-start(bf16[768,128]{1,0:T(8,128)(2,1)S(1)} %collective-permute-done.1.refs_3_.refs_8_) | copy-start | bytes 589828
  112.6 9.4 %copy-start.69 = (bf16[768,128]{1,0:T(8,128)(2,1)}, bf16[768,128]{1,0:T(8,128)(2,1)S(1)}, u32[]{:S(2)}) copy-start(bf16[768,128]{1,0:T(8,128)(2,1)S(1)} %collective-permute-done.2.refs_4_.refs_9_) | copy-start | bytes 589828
  112.7 5.7 %collective-permute-start.4 = (bf16[288,768]{1,0:T(8,128)(2,1)}, bf16[288,768]{1,0:T(8,128)(2,1)S(1)}, u32[]{:S(2)}, u32[]{:S(2)}) collective-permute-start(bf16[288,768]{1,0:T(8,128)(2,1)} %get-tuple-element.118.refs_7_), channel_id=1, source_target_pairs={{0,2},{4,6},{1,3},{5,7},{8,10},{12,14},{9,11},{13,15},{16,18},{20,... | collective-permute-start | bytes 1327112 | tf_op jit(solution)/shard_map/ppermute | solution.py:887
  119.7 13.6 %collective-permute-start.5 = (bf16[288,768]{1,0:T(8,128)(2,1)S(1)}, bf16[288,768]{1,0:T(8,128)(2,1)S(1)}, u32[]{:S(2)}, u32[]{:S(2)}) collective-permute-start(bf16[288,768]{1,0:T(8,128)(2,1)S(1)} %fusion.63), channel_id=1, source_target_pairs={{2,4},{3,5},{10,12},{11,13},{18,20},{19,21},{26,28},{27,29}} | collective-permute-start | bytes 1327112 | tf_op jit(solution)/shard_map/ppermute | solution.py:897
  120.4 13.0 %collective-permute-start.6 = (bf16[288,768]{1,0:T(8,128)(2,1)S(1)}, bf16[288,768]{1,0:T(8,128)(2,1)S(1)}, u32[]{:S(2)}, u32[]{:S(2)}) collective-permute-start(bf16[288,768]{1,0:T(8,128)(2,1)S(1)} %fusion.63), channel_id=1, source_target_pairs={{2,6},{3,7},{10,14},{11,15},{18,22},{19,23},{26,30},{27,31}} | collective-permute-start | bytes 1327112 | tf_op jit(solution)/shard_map/ppermute | solution.py:897
  142.8 17.5 %collective-permute-start.7 = (bf16[384,1024]{1,0:T(8,128)(2,1)}, bf16[384,1024]{1,0:T(8,128)(2,1)}, u32[]{:S(2)}, u32[]{:S(2)}) collective-permute-start(bf16[384,1024]{1,0:T(8,128)(2,1)} %convolution_convert_fusion.5), channel_id=1, source_target_pairs={{0,1},{1,0},{2,3},{3,2},{4,5},{5,4},{6,7},{7,6},{8,9},{9,8},{10,11... | collective-permute-start | bytes 2359304 | tf_op jit(solution)/shard_map/ppermute | solution.py:851
  144.7 32.5 %copy-start.1 = (f32[2,384,1024]{2,1,0:T(8,128)}, f32[2,384,1024]{2,1,0:T(8,128)S(1)}, u32[]{:S(2)}) copy-start(f32[2,384,1024]{2,1,0:T(8,128)S(1)} %convert_element_type.278) | copy-start | bytes 9437188
  155.2 22.0 %collective-permute-start.9 = (bf16[384,1024]{1,0:T(8,128)(2,1)}, bf16[384,1024]{1,0:T(8,128)(2,1)}, u32[]{:S(2)}, u32[]{:S(2)}) collective-permute-start(bf16[384,1024]{1,0:T(8,128)(2,1)} %convolution_convert_fusion.4), channel_id=1, source_target_pairs={{0,1},{1,0},{2,3},{3,2},{4,5},{5,4},{6,7},{7,6},{8,9},{9,8},{10,11... | collective-permute-start | bytes 2359304 | tf_op jit(solution)/shard_map/ppermute | solution.py:851
  170.3 23.6 %copy-start.20 = (bf16[384,1024]{1,0:T(8,128)(2,1)}, bf16[384,1024]{1,0:T(8,128)(2,1)S(1)}, u32[]{:S(2)}) copy-start(bf16[384,1024]{1,0:T(8,128)(2,1)S(1)} %convolution_convert_fusion.3) | copy-start | bytes 2359300
  170.3 23.6 %collective-permute-start.8 = (bf16[384,1024]{1,0:T(8,128)(2,1)S(1)}, bf16[384,1024]{1,0:T(8,128)(2,1)S(1)}, u32[]{:S(2)}, u32[]{:S(2)}) collective-permute-start(bf16[384,1024]{1,0:T(8,128)(2,1)S(1)} %convolution_convert_fusion.3), channel_id=1, source_target_pairs={{0,1},{1,0},{2,3},{3,2},{4,5},{5,4},{6,7},{7,6},{8,9},{9,8},{10,11... | collective-permute-start | bytes 2359304 | tf_op jit(solution)/shard_map/ppermute | solution.py:851
  179.2 31.6 %copy-start.3 = (f32[384,1024]{1,0:T(8,128)}, f32[384,1024]{1,0:T(8,128)S(1)}, u32[]{:S(2)}) copy-start(f32[384,1024]{1,0:T(8,128)S(1)} %get-tuple-element.281) | copy-start | bytes 4718596
  181.7 12.3 %copy-start.6 = (f32[384,1024]{1,0:T(8,128)S(1)}, f32[384,1024]{1,0:T(8,128)}, u32[]{:S(2)}) copy-start(f32[384,1024]{1,0:T(8,128)} %copy-done.5) | copy-start | bytes 4718596
  181.7 12.3 %copy-start.13 = (bf16[2,384,1024]{2,1,0:T(8,128)(2,1)S(1)}, bf16[2,384,1024]{2,1,0:T(8,128)(2,1)}, u32[]{:S(2)}) copy-start(bf16[2,384,1024]{2,1,0:T(8,128)(2,1)} %param.28) | copy-start | bytes 4718596
  181.7 12.3 %copy-start.24 = (bf16[2,384,1024]{2,1,0:T(8,128)(2,1)S(1)}, bf16[2,384,1024]{2,1,0:T(8,128)(2,1)}, u32[]{:S(2)}) copy-start(bf16[2,384,1024]{2,1,0:T(8,128)(2,1)} %param.29) | copy-start | bytes 4718596
  182.7 28.1 %copy-start.16 = (bf16[384,1024]{1,0:T(8,128)(2,1)}, bf16[384,1024]{1,0:T(8,128)(2,1)S(1)}, u32[]{:S(2)}) copy-start(bf16[384,1024]{1,0:T(8,128)(2,1)S(1)} %convolution_convert_fusion.2) | copy-start | bytes 2359300
  182.7 28.1 %collective-permute-start.10 = (bf16[384,1024]{1,0:T(8,128)(2,1)S(1)}, bf16[384,1024]{1,0:T(8,128)(2,1)S(1)}, u32[]{:S(2)}, u32[]{:S(2)}) collective-permute-start(bf16[384,1024]{1,0:T(8,128)(2,1)S(1)} %convolution_convert_fusion.2), channel_id=1, source_target_pairs={{0,1},{1,0},{2,3},{3,2},{4,5},{5,4},{6,7},{7,6},{8,9},{9,8},{10,11... | collective-permute-start | bytes 2359304 | tf_op jit(solution)/shard_map/ppermute | solution.py:851
  223.4 175.6 %reduce-scatter.5.cloned.1.call-start = ((), (), s32[]{:S(2)}) async-start(), calls=%async_computation.5 | async-start | bytes 4456448 | tf_op jit(solution)/shard_map/reduce_scatter | solution.py:1126
  223.7 18.6 %copy-start.21 = (bf16[384,1024]{1,0:T(8,128)(2,1)S(1)}, bf16[384,1024]{1,0:T(8,128)(2,1)}, u32[]{:S(2)}) copy-start(bf16[384,1024]{1,0:T(8,128)(2,1)} %copy-done.20) | copy-start | bytes 2359300
  223.7 18.6 %copy-start.23 = (bf16[384,1024]{1,0:T(8,128)(2,1)S(1)}, bf16[384,1024]{1,0:T(8,128)(2,1)}, u32[]{:S(2)}) copy-start(bf16[384,1024]{1,0:T(8,128)(2,1)} %copy-done.22) | copy-start | bytes 2359300
  223.7 18.6 %copy-start.33 = (bf16[384,1024]{1,0:T(8,128)(2,1)S(1)}, bf16[384,1024]{1,0:T(8,128)(2,1)}, u32[]{:S(2)}) copy-start(bf16[384,1024]{1,0:T(8,128)(2,1)} %fusion.43) | copy-start | bytes 2359300
  223.7 18.6 %collective-permute-start.12 = (bf16[384,1024]{1,0:T(8,128)(2,1)}, bf16[384,1024]{1,0:T(8,128)(2,1)S(1)}, u32[]{:S(2)}, u32[]{:S(2)}) collective-permute-start(bf16[384,1024]{1,0:T(8,128)(2,1)} %fusion.43), channel_id=1, source_target_pairs={{0,1},{1,0},{2,3},{3,2},{4,5},{5,4},{6,7},{7,6},{8,9},{9,8},{10,11... | collective-permute-start | bytes 2359304 | tf_op jit(solution)/shard_map/ppermute | solution.py:851
  230.4 13.8 %copy-start.7 = (f32[384,1024]{1,0:T(8,128)S(1)}, f32[384,1024]{1,0:T(8,128)}, u32[]{:S(2)}) copy-start(f32[384,1024]{1,0:T(8,128)} %copy-done.5) | copy-start | bytes 4718596
  230.4 13.8 %copy-start.14 = (bf16[2,384,1024]{2,1,0:T(8,128)(2,1)S(1)}, bf16[2,384,1024]{2,1,0:T(8,128)(2,1)}, u32[]{:S(2)}) copy-start(bf16[2,384,1024]{2,1,0:T(8,128)(2,1)} %param.28) | copy-start | bytes 4718596
  230.4 13.8 %copy-start.25 = (bf16[2,384,1024]{2,1,0:T(8,128)(2,1)S(1)}, bf16[2,384,1024]{2,1,0:T(8,128)(2,1)}, u32[]{:S(2)}) copy-start(bf16[2,384,1024]{2,1,0:T(8,128)(2,1)} %param.29) | copy-start | bytes 4718596
  230.4 28.9 %collective-permute-start.11 = (bf16[384,1024]{1,0:T(8,128)(2,1)}, bf16[384,1024]{1,0:T(8,128)(2,1)}, u32[]{:S(2)}, u32[]{:S(2)}) collective-permute-start(bf16[384,1024]{1,0:T(8,128)(2,1)} %fusion.46), channel_id=1, source_target_pairs={{0,1},{1,0},{2,3},{3,2},{4,5},{5,4},{6,7},{7,6},{8,9},{9,8},{10,11... | collective-permute-start | bytes 2359304 | tf_op jit(solution)/shard_map/ppermute | solution.py:851
  248.9 10.3 %copy-start.17 = (bf16[384,1024]{1,0:T(8,128)(2,1)S(1)}, bf16[384,1024]{1,0:T(8,128)(2,1)}, u32[]{:S(2)}) copy-start(bf16[384,1024]{1,0:T(8,128)(2,1)} %copy-done.16) | copy-start | bytes 2359300
  274.6 5.0 %collective-permute-start.13 = (bf16[288,768]{1,0:T(8,128)(2,1)}, bf16[288,768]{1,0:T(8,128)(2,1)S(1)}, u32[]{:S(2)}, u32[]{:S(2)}) collective-permute-start(bf16[288,768]{1,0:T(8,128)(2,1)} %get-tuple-element.134), channel_id=1, source_target_pairs={{2,0},{6,4},{3,1},{7,5},{10,8},{14,12},{11,9},{15,13},{18,16},{22,... | collective-permute-start | bytes 1327112 | tf_op jit(solution)/shard_map/ppermute | solution.py:887
  281.0 24.3 %collective-permute-start.14 = (bf16[288,768]{1,0:T(8,128)(2,1)S(1)}, bf16[288,768]{1,0:T(8,128)(2,1)S(1)}, u32[]{:S(2)}, u32[]{:S(2)}) collective-permute-start(bf16[288,768]{1,0:T(8,128)(2,1)S(1)} %fusion.65), channel_id=1, source_target_pairs={{4,0},{5,1},{12,8},{13,9},{20,16},{21,17},{28,24},{29,25}} | collective-permute-start | bytes 1327112 | tf_op jit(solution)/shard_map/ppermute | solution.py:897
  282.3 23.0 %collective-permute-start.15 = (bf16[288,768]{1,0:T(8,128)(2,1)S(1)}, bf16[288,768]{1,0:T(8,128)(2,1)S(1)}, u32[]{:S(2)}, u32[]{:S(2)}) collective-permute-start(bf16[288,768]{1,0:T(8,128)(2,1)S(1)} %fusion.65), channel_id=1, source_target_pairs={{4,2},{5,3},{12,10},{13,11},{20,18},{21,19},{28,26},{29,27}} | collective-permute-start | bytes 1327112 | tf_op jit(solution)/shard_map/ppermute | solution.py:897
  305.3 10.2 %copy-start.36 = (bf16[288,768]{1,0:T(8,128)(2,1)}, bf16[288,768]{1,0:T(8,128)(2,1)S(1)}, u32[]{:S(2)}) copy-start(bf16[288,768]{1,0:T(8,128)(2,1)S(1)} %collective-permute-done.14.refs_16_) | copy-start | bytes 1327108
  305.4 10.2 %copy-start.37 = (bf16[288,768]{1,0:T(8,128)(2,1)}, bf16[288,768]{1,0:T(8,128)(2,1)S(1)}, u32[]{:S(2)}) copy-start(bf16[288,768]{1,0:T(8,128)(2,1)S(1)} %collective-permute-done.15.refs_17_) | copy-start | bytes 1327108
  316.5 29.2 %collective-permute-start.16 = (bf16[768,128]{1,0:T(8,128)(2,1)S(1)}, bf16[768,128]{1,0:T(8,128)(2,1)S(1)}, u32[]{:S(2)}, u32[]{:S(2)}) collective-permute-start(bf16[768,128]{1,0:T(8,128)(2,1)S(1)} %copy-done.71), channel_id=1, source_target_pairs={{2,0},{4,2},{6,4},{3,1},{5,3},{7,5},{10,8},{12,10},{14,12},{11,9},... | collective-permute-start | bytes 589832 | tf_op jit(solution)/shard_map/ppermute | solution.py:842
  317.8 27.9 %collective-permute-start.17 = (bf16[768,128]{1,0:T(8,128)(2,1)S(1)}, bf16[768,128]{1,0:T(8,128)(2,1)S(1)}, u32[]{:S(2)}, u32[]{:S(2)}) collective-permute-start(bf16[768,128]{1,0:T(8,128)(2,1)S(1)} %copy-done.72), channel_id=1, source_target_pairs={{4,0},{6,2},{5,1},{7,3},{12,8},{14,10},{13,9},{15,11},{20,16},{22,... | collective-permute-start | bytes 589832 | tf_op jit(solution)/shard_map/ppermute | solution.py:842
  319.1 26.7 %collective-permute-start.18 = (bf16[768,128]{1,0:T(8,128)(2,1)S(1)}, bf16[768,128]{1,0:T(8,128)(2,1)S(1)}, u32[]{:S(2)}, u32[]{:S(2)}) collective-permute-start(bf16[768,128]{1,0:T(8,128)(2,1)S(1)} %copy-done.73), channel_id=1, source_target_pairs={{6,0},{7,1},{14,8},{15,9},{22,16},{23,17},{30,24},{31,25}} | collective-permute-start | bytes 589832 | tf_op jit(solution)/shard_map/ppermute | solution.py:842
  331.8 11.8 %copy-start.50 = (f32[16,1024]{1,0:T(8,128)S(1)}, f32[16,1024]{1,0:T(8,128)}, u32[]{:S(2)}) copy-start(f32[16,1024]{1,0:T(8,128)} %get-tuple-element.162) | copy-start | bytes 196612
  344.4 4.5 collective-permute-start.19
  361.1 9.4 %copy-start.57 = (f32[8,256]{1,0:T(8,128)S(1)}, f32[8,256]{1,0:T(8,128)}, u32[]{:S(2)}) copy-start(f32[8,256]{1,0:T(8,128)} %get-tuple-element.175) | copy-start | bytes 24580
  361.1 9.4 %copy-start.58 = (f32[8,256]{1,0:T(8,128)S(1)}, f32[8,256]{1,0:T(8,128)}, u32[]{:S(2)}) copy-start(f32[8,256]{1,0:T(8,128)} %get-tuple-element.174) | copy-start | bytes 24580
  361.1 9.5 %copy-start.60 = (f32[8,128]{1,0:T(8,128)S(1)}, f32[8,128]{1,0:T(8,128)}, u32[]{:S(2)}) copy-start(f32[8,128]{1,0:T(8,128)} %get-tuple-element.177) | copy-start | bytes 12292
  361.2 9.5 %copy-start.61 = (f32[8,128]{1,0:T(8,128)S(1)}, f32[8,128]{1,0:T(8,128)}, u32[]{:S(2)}) copy-start(f32[8,128]{1,0:T(8,128)} %get-tuple-element.176) | copy-start | bytes 12292
  361.2 9.8 %copy-start.8 = (bf16[768,1024]{1,0:T(8,128)(2,1)S(1)}, bf16[768,1024]{1,0:T(8,128)(2,1)}, u32[]{:S(2)}) copy-start(bf16[768,1024]{1,0:T(8,128)(2,1)} %get-tuple-element.171) | copy-start | bytes 4718596
  361.3 12.4 %collective-permute-start.20 = (bf16[4,2,64,1280]{3,2,0,1:T(8,128)(2,1)S(1)}, bf16[4,2,64,1280]{3,2,0,1:T(8,128)(2,1)}, u32[]{:S(2)}, u32[]{:S(2)}) collective-permute-start(bf16[4,2,64,1280]{3,2,0,1:T(8,128)(2,1)S(1)} %bitcast.189), channel_id=1, source_target_pairs={{0,2},{2,0},{4,6},{6,4},{1,3},{3,1},{5,7},{7,5},{8,10},{10,8},{12,... | collective-permute-start | bytes 3932168 | tf_op jit(solution)/shard_map/ppermute | solution.py:851
  372.2 26.8 %collective-permute-start.24 = (bf16[384,1024]{1,0:T(8,128)(2,1)}, bf16[384,1024]{1,0:T(8,128)(2,1)}, u32[]{:S(2)}, u32[]{:S(2)}) collective-permute-start(bf16[384,1024]{1,0:T(8,128)(2,1)} %get-tuple-element.285), channel_id=1, source_target_pairs={{0,1},{1,0},{2,3},{3,2},{4,5},{5,4},{6,7},{7,6},{8,9},{9,8},{10,11... | collective-permute-start | bytes 2359304 | tf_op jit(solution)/shard_map/ppermute | solution.py:851
  377.4 19.3 %collective-permute-start.23 = (bf16[4,64,1280]{2,1,0:T(8,128)(2,1)}, bf16[4,64,1280]{2,1,0:T(8,128)(2,1)}, u32[]{:S(2)}, u32[]{:S(2)}) collective-permute-start(bf16[4,64,1280]{2,1,0:T(8,128)(2,1)} %dynamic-slice_bitcast_fusion), channel_id=1, source_target_pairs={{0,4},{2,6},{4,0},{6,2},{1,5},{3,7},{5,1},{7,3},{8,12},{10,14},{12... | collective-permute-start | bytes 1966088 | tf_op jit(solution)/shard_map/ppermute | solution.py:851
  378.0 3.6 collective-permute-start.21
  380.7 28.8 %collective-permute-start.28 = (bf16[384,1024]{1,0:T(8,128)(2,1)}, bf16[384,1024]{1,0:T(8,128)(2,1)}, u32[]{:S(2)}, u32[]{:S(2)}) collective-permute-start(bf16[384,1024]{1,0:T(8,128)(2,1)} %get-tuple-element.284), channel_id=1, source_target_pairs={{0,1},{1,0},{2,3},{3,2},{4,5},{5,4},{6,7},{7,6},{8,9},{9,8},{10,11... | collective-permute-start | bytes 2359304 | tf_op jit(solution)/shard_map/ppermute | solution.py:851
  381.6 15.0 %collective-permute-start.22 = (f32[88,128]{1,0:T(8,128)S(1)}, f32[88,128]{1,0:T(8,128)S(1)}, u32[]{:S(2)}, u32[]{:S(2)}) collective-permute-start(f32[88,128]{1,0:T(8,128)S(1)} %add.250), channel_id=1, source_target_pairs={{0,4},{2,6},{4,0},{6,2},{1,5},{3,7},{5,1},{7,3},{8,12},{10,14},{12... | collective-permute-start | bytes 135176 | tf_op jit(solution)/shard_map/ppermute | solution.py:851
  387.3 22.2 %copy-start.52 = (f32[1024]{0:T(1024)S(1)}, f32[1024]{0:T(1024)}, u32[]{:S(2)}) copy-start(f32[1024]{0:T(1024)} %param.30) | copy-start | bytes 12292
  400.8 33.4 %collective-permute-start.30 = (bf16[64,1280]{1,0:T(8,128)(2,1)S(1)}, bf16[64,1280]{1,0:T(8,128)(2,1)S(1)}, u32[]{:S(2)}, u32[]{:S(2)}) collective-permute-start(bf16[64,1280]{1,0:T(8,128)(2,1)S(1)} %get-tuple-element.287), channel_id=1, source_target_pairs={{0,16},{8,24},{16,0},{24,8},{1,17},{9,25},{17,1},{25,9},{2,18},{10... | collective-permute-start | bytes 491528 | tf_op jit(solution)/shard_map/ppermute | solution.py:851
  403.2 12.6 %collective-permute-start.25 = (f32[88,128]{1,0:T(8,128)S(1)}, f32[88,128]{1,0:T(8,128)S(1)}, u32[]{:S(2)}, u32[]{:S(2)}) collective-permute-start(f32[88,128]{1,0:T(8,128)S(1)} %add.251), channel_id=1, source_target_pairs={{0,1},{1,0},{2,3},{3,2},{4,5},{5,4},{6,7},{7,6},{8,9},{9,8},{10,11... | collective-permute-start | bytes 135176 | tf_op jit(solution)/shard_map/ppermute | solution.py:851
  415.8 4.6 %collective-permute-start.26 = (f32[88,128]{1,0:T(8,128)S(1)}, f32[88,128]{1,0:T(8,128)S(1)}, u32[]{:S(2)}, u32[]{:S(2)}) collective-permute-start(f32[88,128]{1,0:T(8,128)S(1)} %add.253), channel_id=1, source_target_pairs={{0,8},{8,0},{16,24},{24,16},{1,9},{9,1},{17,25},{25,17},{2,10},{10... | collective-permute-start | bytes 135176 | tf_op jit(solution)/shard_map/ppermute | solution.py:851
  418.7 15.5 %collective-permute-start.31 = (bf16[64,1280]{1,0:T(8,128)(2,1)}, bf16[64,1280]{1,0:T(8,128)(2,1)S(1)}, u32[]{:S(2)}, u32[]{:S(2)}) collective-permute-start(bf16[64,1280]{1,0:T(8,128)(2,1)} %get-tuple-element.286), channel_id=1, source_target_pairs={{0,24},{8,16},{16,8},{24,0},{1,25},{9,17},{17,9},{25,1},{2,26},{10... | collective-permute-start | bytes 491528 | tf_op jit(solution)/shard_map/ppermute | solution.py:851
  420.4 13.8 %collective-permute-start.29 = (bf16[64,1280]{1,0:T(8,128)(2,1)}, bf16[64,1280]{1,0:T(8,128)(2,1)S(1)}, u32[]{:S(2)}, u32[]{:S(2)}) collective-permute-start(bf16[64,1280]{1,0:T(8,128)(2,1)} %get-tuple-element.288), channel_id=1, source_target_pairs={{0,8},{8,0},{16,24},{24,16},{1,9},{9,1},{17,25},{25,17},{2,10},{10... | collective-permute-start | bytes 491528 | tf_op jit(solution)/shard_map/ppermute | solution.py:851
  420.4 8.8 %collective-permute-start.27 = (f32[88,128]{1,0:T(8,128)S(1)}, f32[88,128]{1,0:T(8,128)S(1)}, u32[]{:S(2)}, u32[]{:S(2)}) collective-permute-start(f32[88,128]{1,0:T(8,128)S(1)} %add.254), channel_id=1, source_target_pairs={{0,16},{8,24},{16,0},{24,8},{1,17},{9,25},{17,1},{25,9},{2,18},{10... | collective-permute-start | bytes 135176 | tf_op jit(solution)/shard_map/ppermute | solution.py:851
  435.3 4.0 collective-permute-start.32
  (50 other events, 160.0 us)
Sparse Core Ops, SparseCore 0:
  13.2 67.6 all-gather.2
  83.2 60.3 all-gather.4
  223.5 89.3 reduce-scatter.2
  317.1 76.4 reduce-scatter.4
